TPU v7x, 128 devices: a whole 4x4x4 slice. The times are simulated.
128 devices in a mesh: group: 4 (over y), ctx: 32 (over x, z, core).
Axes of the slice: x: 4, y: 4, z: 4, core: 2. Of those that a mesh axis runs over, the one named last changes fastest.
Arguments:
- query: bfloat16 [128, 128, 576], P('group', 'ctx'), may hold values from -160 to 160
- cache: bfloat16 [32, 32768, 576], P('group', 'ctx'), may hold values from -6 to 6
- new_keys: bfloat16 [128, 576], P('group'), may hold values from -7 to 7
- lengths: int32 [32], P('group'), may hold values from 1 to 32768, as said below
- value_up_weight: bfloat16 [128, 512, 128], P('ctx'), may hold values from -1 to 1
- w_out: bfloat16 [16384, 7168], P('ctx'), may hold values from -0.1875 to 0.1875
- residual: bfloat16 [128, 7168], P(('group', 'ctx')), may hold values from -6 to 6
- norm_gain: float32 [7168], replicated, may hold values from 0.1 to 1.9
- w_router: bfloat16 [7168, 16], replicated, may hold values from -0.125 to 0.125
- routes: int32 [128, 8], P(('group', 'ctx')), may hold values from 0 to 15, all different within a row
- w_gate: bfloat16 [7168, 32768], P(None, ('group', 'ctx')), may hold values from -0.0625 to 0.0625
- w_up: bfloat16 [7168, 32768], P(None, ('group', 'ctx')), may hold values from -0.0625 to 0.0625
- w_down: bfloat16 [32768, 7168], P(('group', 'ctx')), may hold values from -0.125 to 0.125
Outputs:
- attn_out: bfloat16 [128, 7168], P(('group', 'ctx'))
- layer_out: bfloat16 [128, 7168], P(('group', 'ctx'))
Inputs may be any that keep to these rules, and one draw needn't show every extreme that they name: `lengths`: some request has all 32768 positions live.
All inputs are finite; a program needn't handle non-finite values.
Results may differ from a plain program's by a relative error of at most 0.018.
Values may be sent and summed in bfloat16 or wider, within the bound.
No kernel may reach another device: no remote copies, remote signals or barrier semaphores. Data moves between devices by JAX's collectives and lax.ppermute only.
A program may use at most 192 MiB of HBM per device.

v0:
```python
import jax
import jax.numpy as jnp
from jax import lax
from jax.sharding import PartitionSpec as P

LATENT_WIDTH = 512
ROTARY_WIDTH = 64
QK_NOPE = 128
VALUE_HEAD_WIDTH = 128
EXPERTS = 16


neg_floor = -1e30
route_scale = 2.5
norm_eps = 1e-06


def expert_partial(slot_rows, w_gate, w_up, w_down):
    gate_sum = jnp.dot(slot_rows, w_gate, preferred_element_type=jnp.float32)
    up_sum = jnp.dot(slot_rows, w_up, preferred_element_type=jnp.float32)
    hidden = (jax.nn.silu(gate_sum) * up_sum).astype(jnp.bfloat16)
    return jnp.dot(hidden, w_down, preferred_element_type=jnp.float32)


def local(
    query,
    cache,
    new_keys,
    lengths,
    value_up_weight,
    w_out,
    residual,
    norm_gain,
    w_router,
    routes,
    w_gate,
    w_up,
    w_down,
):
    score_scale = (QK_NOPE + ROTARY_WIDTH) ** (-0.5)
    ctx_count = lax.axis_size("ctx")
    group_count = lax.axis_size("group")
    ctx_index = lax.axis_index("ctx")
    grouped_rows, local_heads, features = query.shape
    request_batch = lengths.shape[0]
    draft_tokens = grouped_rows // request_batch
    block_len = cache.shape[1]
    positions = ctx_index * block_len + jnp.arange(block_len, dtype=jnp.int32)
    live_mask = (positions[None, :] < lengths[:, None])[:, None, None, :]
    compressed_keys = cache[:, :, :LATENT_WIDTH]
    all_heads = lax.all_gather(query, "ctx", axis=1, tiled=True)
    current_width = all_heads.shape[1]
    shaped = all_heads.reshape(request_batch, draft_tokens, current_width, features)
    scores = score_scale * jnp.einsum(
        "rqhd,rtd->rqht", shaped, cache, preferred_element_type=jnp.float32
    )
    block_max = jnp.max(jnp.where(live_mask, scores, neg_floor), axis=-1)
    probability = jnp.exp(jnp.where(live_mask, scores - block_max[..., None], neg_floor))
    block_sum = jnp.sum(probability, axis=-1)
    block_result = jnp.einsum(
        "rqht,rtk->rqhk",
        probability.astype(jnp.bfloat16),
        compressed_keys,
        preferred_element_type=jnp.float32,
    )
    arrived = (
        lax.all_to_all(
            block_max.reshape(grouped_rows, current_width)[None],
            "ctx",
            split_axis=2,
            concat_axis=0,
            tiled=True,
        ),
        lax.all_to_all(
            block_sum.reshape(grouped_rows, current_width)[None],
            "ctx",
            split_axis=2,
            concat_axis=0,
            tiled=True,
        ),
        lax.all_to_all(
            block_result.reshape(grouped_rows, current_width, LATENT_WIDTH)[None],
            "ctx",
            split_axis=2,
            concat_axis=0,
            tiled=True,
        ),
    )
    cache_max = jnp.max(arrived[0], axis=0)
    factors = jnp.exp(arrived[0] - cache_max[None])
    cache_sum = jnp.sum(factors * arrived[1], axis=0)
    cache_result = jnp.sum(factors[..., None] * arrived[2], axis=0)
    own_query = query.reshape(request_batch, draft_tokens, local_heads, features)
    recent_keys = new_keys.reshape(request_batch, draft_tokens, features)
    near_scores = score_scale * jnp.einsum(
        "rqhd,rjd->rqhj", own_query, recent_keys, preferred_element_type=jnp.float32
    )
    causal = (
        jnp.arange(draft_tokens, dtype=jnp.int32)[None, :]
        <= jnp.arange(draft_tokens, dtype=jnp.int32)[:, None]
    )
    causal = causal[None, :, None, :]
    near_max = jnp.max(jnp.where(causal, near_scores, neg_floor), axis=-1)
    shaped_max = cache_max.reshape(request_batch, draft_tokens, local_heads)
    joint_max = jnp.maximum(shaped_max, near_max)
    cache_rescale = jnp.exp(shaped_max - joint_max)
    nearby_probability = jnp.exp(jnp.where(causal, near_scores - joint_max[..., None], neg_floor))
    denominator = cache_sum.reshape(
        request_batch, draft_tokens, local_heads
    ) * cache_rescale + jnp.sum(nearby_probability, axis=-1)
    softmax_numerator = cache_result.reshape(
        request_batch, draft_tokens, local_heads, LATENT_WIDTH
    ) * cache_rescale[..., None] + jnp.einsum(
        "rqhj,rjk->rqhk",
        nearby_probability,
        recent_keys[:, :, :LATENT_WIDTH].astype(jnp.float32),
        precision=lax.Precision.HIGHEST,
    )
    latent_vector = (
        (softmax_numerator / denominator[..., None])
        .astype(jnp.bfloat16)
        .reshape(grouped_rows, local_heads, LATENT_WIDTH)
    )
    per_head_values = jnp.einsum(
        "gxj,xjs->gxs", latent_vector, value_up_weight, preferred_element_type=jnp.float32
    )
    per_head_values = per_head_values.astype(jnp.bfloat16).reshape(
        grouped_rows, local_heads * VALUE_HEAD_WIDTH
    )
    row_count = residual.shape[0]
    attention = lax.psum_scatter(
        jnp.dot(per_head_values, w_out, preferred_element_type=jnp.float32).astype(jnp.bfloat16),
        "ctx",
        scatter_dimension=0,
        tiled=True,
    ).astype(jnp.float32)
    attn_out = attention.astype(jnp.bfloat16)
    stream = (residual.astype(jnp.float32) + attention).astype(jnp.bfloat16)
    stream_wide = stream.astype(jnp.float32)
    mean_square = jnp.mean(stream_wide * stream_wide, axis=-1, keepdims=True)
    normed = (stream_wide * lax.rsqrt(mean_square + norm_eps) * norm_gain).astype(jnp.bfloat16)
    gate_values = jax.nn.sigmoid(jnp.dot(normed, w_router, preferred_element_type=jnp.float32))
    expert_ids = jnp.arange(EXPERTS, dtype=jnp.int32)
    selected_experts = (routes[:, :, None] == expert_ids[None, None, :]).astype(jnp.float32)
    picked = jnp.sum(selected_experts * gate_values[:, None, :], axis=-1)
    route_weights = route_scale * picked / jnp.sum(picked, axis=-1, keepdims=True)
    device_count = group_count * ctx_count
    slices = device_count // EXPERTS
    owners = jnp.arange(device_count, dtype=jnp.int32) // slices
    row_ids = jnp.arange(row_count, dtype=jnp.int32)
    earlier = row_ids[:, None] > row_ids[None, :]
    same_expert = routes[:, :, None, None] == routes[None, None, :, :]
    slot_index = jnp.sum((same_expert & earlier[:, None, :, None]).astype(jnp.int32), axis=(2, 3))
    targets = (routes[:, :, None] == owners[None, None, :])[..., None] & (
        slot_index[:, :, None, None] == row_ids[None, None, None, :]
    )
    placing = jnp.sum(targets.astype(jnp.float32), axis=1)
    coefficient = jnp.sum(route_weights[:, :, None, None] * targets.astype(jnp.float32), axis=1)
    outgoing = jnp.einsum(
        "idc,ij->dcj", placing.astype(jnp.bfloat16), normed, preferred_element_type=jnp.float32
    ).astype(jnp.bfloat16)
    model_width = residual.shape[1]
    slot_block = lax.all_to_all(outgoing, ("group", "ctx"), split_axis=0, concat_axis=0, tiled=True)
    slot_span = slot_block.shape[1]
    partial_out = expert_partial(
        slot_block.reshape(device_count * slot_span, model_width), w_gate, w_up, w_down
    )
    returned = lax.all_to_all(
        partial_out.reshape(device_count, slot_span, model_width).astype(jnp.bfloat16),
        ("group", "ctx"),
        split_axis=0,
        concat_axis=0,
        tiled=True,
    ).astype(jnp.float32)
    expert_mix = jnp.einsum("idc,dcj->ij", coefficient, returned, precision=lax.Precision.HIGHEST)
    layer_out = (stream_wide + expert_mix).astype(jnp.bfloat16)
    return (attn_out, layer_out)


def solution(mesh):
    return jax.shard_map(
        local,
        mesh=mesh,
        in_specs=(
            P("group", "ctx", None),
            P("group", "ctx", None),
            P("group", None),
            P("group"),
            P("ctx", None, None),
            P("ctx", None),
            P(("group", "ctx"), None),
            P(),
            P(),
            P(("group", "ctx"), None),
            P(None, ("group", "ctx")),
            P(None, ("group", "ctx")),
            P(("group", "ctx"), None),
        ),
        out_specs=(P(("group", "ctx"), None), P(("group", "ctx"), None)),
        check_vma=False,
    )
```

profile of v0, /device:TPU:0, one launch (start us, length us, event | category | flops | bytes accessed | tf_op | source)
XLA Modules:
  0.0 506.4 jit_solution(4167287995145306483)
XLA Ops:
  7.2 0.0 copy-start
  7.2 0.0 all-gather.2.cloned.1.call-start
  7.2 1.6 copy.86
  8.9 0.0 all-gather.2.cloned.1.call-update
  8.9 0.7 broadcast_compare_fusion
  9.6 50.7 %all-gather.2.cloned.1.call-done = bf16[32,128,576]{2,0,1:T(8,128)(2,1)} async-done(((bf16[32,4,576]{2,0,1:T(8,128)(2,1)}), bf16[32,128,576]{2,0,1:T(8,128)(2,1)}) %all-gather.2.cloned.1.call-update) | async-done | bytes 4718608 | tf_op jit(solution)/shard_map/all_gather | solution.py:51
  60.3 8.7 %copy.87 = bf16[32,128,576]{1,2,0:T(8,128)(2,1)} copy(bf16[32,128,576]{2,0,1:T(8,128)(2,1)} %all-gather.2.cloned.1.call-done) | data formatting | bytes 9437184 | tf_op jit(solution)/shard_map/all_gather | solution.py:51
  69.0 10.9 %select_reduce_fusion = (f32[8,4,128]{2,1,0:T(4,128)S(1)}, f32[8,4,128,1024]{3,2,1,0:T(8,128)S(1)}) fusion(pred[8,1024]{1,0:T(8,128)(4,1)S(1)} %broadcast_compare_fusion, bf16[8,4,128,576]{2,3,1,0:T(8,128)(2,1)} %bitcast.110, bf16[8,1024,576]{1,2,0:T(8,128)(2,1)} %param.14), kind=kOutput, calls=%fused_computation.1 | convolution fusion | flops 4844417024 | bytes 30957568 | tf_op jit(solution)/shard_map/rqhd,rtd->rqht/dot_general | solution.py:54
  79.9 4.4 fusion
  84.3 1.3 copy-done.1
  85.6 0.1 copy.95
  85.7 0.5 broadcast.318
  86.3 0.8 reduce.9
  87.0 0.7 reshape.421
  87.7 5.3 %all-to-all-start.2 = ((f32[32,1,128]{2,1,0:T(1,128)}), f32[32,1,128]{2,1,0:T(1,128)S(1)}, u32[]{:S(2)}, u32[]{:S(2)}) async-start(f32[32,1,128]{2,1,0:T(1,128)} %reshape.421), calls=%async_computation.2 | async-start | bytes 32768 | tf_op jit(solution)/shard_map/all_to_all | solution.py:74
  93.0 0.1 copy.88
  93.1 0.8 reduce.11
  93.9 0.7 reshape.419
  94.6 5.7 %all-to-all-done.2 = f32[32,1,128]{2,1,0:T(1,128)S(1)} async-done(((f32[32,1,128]{2,1,0:T(1,128)}), f32[32,1,128]{2,1,0:T(1,128)S(1)}, u32[]{:S(2)}, u32[]{:S(2)}) %all-to-all-start.2) | async-done | bytes 16416 | tf_op jit(solution)/shard_map/all_to_all | solution.py:74
  100.3 4.0 all-to-all-start
  104.3 13.0 %fusion.4 = f32[8,4,128,512]{3,2,1,0:T(8,128)} fusion(f32[8,4,128,1024]{3,2,1,0:T(8,128)} %copy-done.1, bf16[8,1024,576]{1,2,0:T(8,128)(2,1)} %param.14, f32[8,4,128]{2,1,0:T(4,128)S(1)} %get-tuple-element.13, pred[8,1024]{1,0:T(8,128)(4,1)S(1)} %broadcast_compare_fusion), kind=kOutput, calls=%fused_computation.7 | convolution fusion | flops 4311744512 | bytes 33579008 | tf_op jit(solution)/shard_map/rqht,rtk->rqhk/dot_general | solution.py:60
  117.3 11.5 %copy.90 = f32[1,32,128,512]{3,1,0,2:T(8,128)} copy(f32[1,32,128,512]{3,2,1,0:T(8,128)} %bitcast.109) | data formatting | bytes 16777216 | tf_op jit(solution)/shard_map/broadcast_in_dim;reshape | solution.py:82
  128.8 7.5 %all-to-all-start.1 = ((f32[1,32,128,512]{3,1,0,2:T(8,128)}), f32[1,32,128,512]{3,1,0,2:T(8,128)}, u32[]{:S(2)}, u32[]{:S(2)}) async-start(f32[1,32,128,512]{3,1,0,2:T(8,128)} %copy.90), calls=%async_computation.1 | async-start | bytes 16777216 | tf_op jit(solution)/shard_map/all_to_all | solution.py:81
  136.3 0.3 all-reduce.3.cloned.1.call-start
  136.6 1.0 select_reduce_fusion.1
  137.6 0.7 reduce.10
  138.3 0.1 reshape.422
  138.5 0.7 reduce.12
  139.1 0.1 reshape.420
  139.3 0.1 copy.107
  139.4 0.1 multiply_reduce_fusion.1
  139.5 0.1 copy.106
  139.6 0.1 fusion.45
  139.7 110.3 %all-to-all-done.1 = f32[1,32,128,512]{3,1,0,2:T(8,128)} async-done(((f32[1,32,128,512]{3,1,0,2:T(8,128)}), f32[1,32,128,512]{3,1,0,2:T(8,128)}, u32[]{:S(2)}, u32[]{:S(2)}) %all-to-all-start.1) | async-done | bytes 8388640 | tf_op jit(solution)/shard_map/all_to_all | solution.py:81
  250.0 3.8 multiply_reduce_fusion
  253.8 0.2 copy.91
  254.0 0.5 fusion.22
  254.6 0.2 fusion.29
  254.8 0.0 copy-start.8
  254.8 0.0 copy-start.7
  254.8 0.0 copy-start.6
  254.8 5.3 %convolution_convert_fusion.1 = bf16[32,7168]{1,0:T(8,128)(2,1)} fusion(bf16[512,7168]{1,0:T(8,128)(2,1)} %param.18, bf16[4,4,8,128]{3,2,1,0:T(8,128)(2,1)S(1)} %fusion.29), kind=kOutput, calls=%fused_computation.16 | convolution fusion | flops 235110400 | bytes 7831552 | tf_op jit(solution)/shard_map/dot_general | solution.py:132
  260.1 0.0 all-reduce.3.cloned.1.call-update
  260.2 0.6 dynamic-slice
  260.7 112.3 %all-reduce.3.cloned.1.call-done = bf16[32,7168]{1,0:T(8,128)(2,1)} async-done(((bf16[32,7168]{1,0:T(8,128)(2,1)}), bf16[32,7168]{1,0:T(8,128)(2,1)}) %all-reduce.3.cloned.1.call-update) | async-done | bytes 458768
  373.0 2.8 multiply_reduce_fusion.2
  376.5 0.1 convert_reduce_fusion
  376.6 0.2 fusion.33
  376.8 0.7 select_reduce_fusion.2
  377.5 0.6 multiply_divide_fusion
  378.2 0.1 fusion.54
  378.3 0.3 fusion.14
  378.6 0.5 broadcast.322
  379.1 2.7 reduce.13
  381.8 4.6 reshape.423
  386.4 36.4 %all_to_all.64 = bf16[128,2,3584]{2,1,0:T(2,128)(2,1)} all-to-all(bf16[128,2,3584]{2,1,0:T(2,128)(2,1)S(1)} %reshape.423), channel_id=1, replica_groups=mesh['group'=4,'ctx'=32] {'group','ctx'}, dimensions={0} | all-to-all | bytes 3670016 | tf_op jit(solution)/shard_map/all_to_all | solution.py:163
  422.9 11.5 %reshape.424 = bf16[128,1,7168]{2,1,0:T(2,128)(2,1)} reshape(bf16[128,2,3584]{2,1,0:T(2,128)(2,1)} %all_to_all.64) | data formatting | bytes 3670016
  434.3 3.9 fusion.19
  438.3 6.3 %fusion.12 = bf16[128,1,7168]{2,0,1:T(8,128)(2,1)S(1)} fusion(bf16[256,7168]{1,0:T(8,128)(2,1)} %param.25, bf16[7168,256]{1,0:T(8,128)(2,1)} %param.24, bf16[128,1,7168]{2,1,0:T(2,128)(2,1)} %reshape.424, f32[128,256]{1,0:T(8,128)S(1)} %fusion.19), kind=kOutput, calls=%fused_computation.15 | convolution fusion | flops 940638208 | bytes 11141120 | tf_op jit(solution)/shard_map/dot_general | solution.py:22
  444.6 2.7 reduce.14
  447.4 4.6 reshape.425
  451.9 32.3 %all_to_all.65 = bf16[128,2,3584]{2,1,0:T(2,128)(2,1)} all-to-all(bf16[128,2,3584]{2,1,0:T(2,128)(2,1)S(1)} %reshape.425), channel_id=1, replica_groups=mesh['group'=4,'ctx'=32] {'group','ctx'}, dimensions={0} | all-to-all | bytes 3670016 | tf_op jit(solution)/shard_map/all_to_all | solution.py:168
  484.3 11.5 %reshape.426 = bf16[128,1,7168]{2,1,0:T(2,128)(2,1)} reshape(bf16[128,2,3584]{2,1,0:T(2,128)(2,1)} %all_to_all.65) | data formatting | bytes 3670016
  495.7 3.8 fusion.13
  (24 shorter events, 0.2 us)
Async XLA Ops:
  7.2 247.4 %copy-start = (bf16[4,512,128]{2,1,0:T(8,128)(2,1)S(1)}, bf16[4,512,128]{2,1,0:T(8,128)(2,1)}, u32[]{:S(2)}) copy-start(bf16[4,512,128]{2,1,0:T(8,128)(2,1)} %param.17) | copy-start | bytes 1572868
  7.2 53.1 %all-gather.2.cloned.1.call-start = ((), (), s32[]{:S(2)}) async-start(), calls=%async_computation.5 | async-start | bytes 5406720 | tf_op jit(solution)/shard_map/all_gather | solution.py:51
  79.9 5.7 %copy-start.1 = (f32[8,4,128,1024]{3,2,1,0:T(8,128)}, f32[8,4,128,1024]{3,2,1,0:T(8,128)S(1)}, u32[]{:S(2)}) copy-start(f32[8,4,128,1024]{3,2,1,0:T(8,128)S(1)} %get-tuple-element.14) | copy-start | bytes 50331652
  87.7 12.5 %all-to-all-start.2 = ((f32[32,1,128]{2,1,0:T(1,128)}), f32[32,1,128]{2,1,0:T(1,128)S(1)}, u32[]{:S(2)}, u32[]{:S(2)}) async-start(f32[32,1,128]{2,1,0:T(1,128)} %reshape.421), calls=%async_computation.2 | async-start | bytes 32768 | tf_op jit(solution)/shard_map/all_to_all | solution.py:74
  100.3 28.5 %all-to-all-start = ((f32[32,1,128]{2,1,0:T(1,128)}), f32[32,1,128]{2,1,0:T(1,128)S(1)}, u32[]{:S(2)}, u32[]{:S(2)}) async-start(f32[32,1,128]{2,1,0:T(1,128)} %reshape.419), calls=%async_computation | async-start | bytes 32768 | tf_op jit(solution)/shard_map/all_to_all | solution.py:67
  128.8 7.8 %copy-start.3 = (bf16[32,576]{1,0:T(8,128)(2,1)S(1)}, bf16[32,576]{1,0:T(8,128)(2,1)}, u32[]{:S(2)}) copy-start(bf16[32,576]{1,0:T(8,128)(2,1)} %param.15) | copy-start | bytes 110596
  128.8 7.8 %copy-start.2 = (bf16[32,4,576]{2,1,0:T(4,128)(2,1)S(1)}, bf16[32,4,576]{2,1,0:T(4,128)(2,1)}, u32[]{:S(2)}) copy-start(bf16[32,4,576]{2,1,0:T(4,128)(2,1)} %param.13) | copy-start | bytes 442372
  128.8 121.2 %all-to-all-start.1 = ((f32[1,32,128,512]{3,1,0,2:T(8,128)}), f32[1,32,128,512]{3,1,0,2:T(8,128)}, u32[]{:S(2)}, u32[]{:S(2)}) async-start(f32[1,32,128,512]{3,1,0,2:T(8,128)} %copy.90), calls=%async_computation.1 | async-start | bytes 16777216 | tf_op jit(solution)/shard_map/all_to_all | solution.py:81
  136.3 236.7 %all-reduce.3.cloned.1.call-start = ((), (), s32[]{:S(2)}) async-start(), calls=%async_computation.6 | async-start | bytes 917504
  254.8 5.4 %copy-start.8 = (u32[128]{0:T(128)S(1)}, u32[128]{0:T(128)}, u32[]{:S(2)}) copy-start(u32[128]{0:T(128)} %constant.59) | copy-start | bytes 1540
  254.8 118.3 %copy-start.4 = (bf16[1,7168]{1,0:T(2,128)(2,1)S(1)}, bf16[1,7168]{1,0:T(2,128)(2,1)}, u32[]{:S(2)}) copy-start(bf16[1,7168]{1,0:T(2,128)(2,1)} %param.19) | copy-start | bytes 43012
  254.8 121.8 %copy-start.5 = (f32[7168]{0:T(1024)S(1)}, f32[7168]{0:T(1024)}, u32[]{:S(2)}) copy-start(f32[7168]{0:T(1024)} %param.20) | copy-start | bytes 86020
  254.8 121.8 %copy-start.7 = (bf16[7168,16]{0,1:T(8,128)(2,1)S(1)}, bf16[7168,16]{0,1:T(8,128)(2,1)}, u32[]{:S(2)}) copy-start(bf16[7168,16]{0,1:T(8,128)(2,1)} %param.21) | copy-start | bytes 688132
  254.8 122.0 %copy-start.6 = (s32[1,8]{1,0:T(1,128)S(1)}, s32[1,8]{1,0:T(1,128)}, u32[]{:S(2)}) copy-start(s32[1,8]{1,0:T(1,128)} %param.22) | copy-start | bytes 100
Sparse Core Ops, SparseCore 0:
  10.3 49.9 all-gather.1
  260.3 112.7 all-reduce.2
where the time goes:
time: 508 us; the launch traced here: 506 us
  waiting for transfers between devices  279 us (55%)
  blocking collectives  68.8 us (14%)
  local copies, waits for them, and re-layouts  59.1 us (12%)
  matrix products  45.3 us (9%)
  other arithmetic  22.2 us (4%)
  starting transfers between devices  17 us (3%)
  between operations  15.1 us (3%)
    unnamed x3, waiting for transfers between devices  112 us
    all_to_all x1, waiting for transfers between devices, local(): lax.all_to_all(block_result.reshape(grouped_rows, current_width, LATENT_W...  110 us
    all_gather x1, waiting for transfers between devices, local(): all_heads = lax.all_gather(query, 'ctx', axis=1, tiled=True)  50.7 us
    unnamed x29, local copies, waits for them, and re-layouts  37.8 us
    all_to_all x1, blocking collectives, local(): lax.all_to_all(outgoing, ('group', 'ctx'), split_axis=0, concat_axis=0, t...  36.4 us
    all_to_all x1, blocking collectives, local(): lax.all_to_all(partial_out.reshape(device_count, slot_span, model_width)....  32.3 us
    dot_general x1, matrix products, local(): jnp.einsum('rqht,rtk->rqhk', probability.astype(jnp.bfloat16), compressed...  13 us
    another operation x1, local copies, waits for them, and re-layouts, local(): block_result.reshape(grouped_rows, current_width, LATENT_WIDTH)[None]  11.5 us
  transfers between devices with their start and end apart: 5, of which 4 were waited for; matrix products, arithmetic and copies ran while one was open for 6% of the time, Pallas kernels for 0%

commit v1 on v0

v1 whole, which is shorter than its diff:
```python
import functools

import jax
import jax.numpy as jnp
from jax import lax
from jax.experimental import pallas as pl
from jax.experimental.pallas import tpu as pltpu
from jax.sharding import Mesh, PartitionSpec as P

LATENT_WIDTH = 512
ROTARY_WIDTH = 64
QK_NOPE = 128
VALUE_HEAD_WIDTH = 128
EXPERTS = 16
LANES = 128
STAT = 16

neg_floor = -1e30
route_scale = 2.5
norm_eps = 1e-06
score_scale = (QK_NOPE + ROTARY_WIDTH) ** (-0.5)
f32 = jnp.float32
bf16 = jnp.bfloat16


def split3(value):
    high = value.astype(bf16).astype(f32)
    rest = value - high
    middle = rest.astype(bf16).astype(f32)
    return high, middle, (rest - middle).astype(bf16).astype(f32)


def place(stat_lanes, column, request, base):
    lane = lax.broadcasted_iota(jnp.int32, stat_lanes.shape, 1)
    for part, piece in enumerate(split3(column)):
        stat_lanes = jnp.where(lane == base + part * STAT + request, piece, stat_lanes)
    return stat_lanes


def join3(tile):
    return tile + pltpu.roll(tile, LANES - STAT, 1) + pltpu.roll(tile, LANES - 2 * STAT, 1)


def attend_kernel(blocks_ref, lengths_ref, q0, q1, q2, q3, own_ref, sib_ref, o0, o1, o2, o3, stat_ref, *, first, count):
    step = pl.program_id(0)
    length = lengths_ref[first + step]
    outs = (o0, o1, o2, o3)
    query = jnp.concatenate([ref[...].reshape(-1, ref.shape[-1]) for ref in (q0, q1, q2, q3)], axis=0)
    rows = query.shape[0]
    block_len = own_ref.shape[2]
    scores = []
    for which, keys in enumerate((own_ref, sib_ref)):
        score = score_scale * jnp.dot(query, keys[0], preferred_element_type=f32)
        position = blocks_ref[which] * block_len + lax.broadcasted_iota(jnp.int32, (1, block_len), 1)
        scores.append(jnp.where(position < length, score, neg_floor))
    top = jnp.maximum(
        jnp.max(scores[0], axis=-1, keepdims=True), jnp.max(scores[1], axis=-1, keepdims=True)
    )
    shift = jnp.where(top <= neg_floor, 0.0, top)
    total = jnp.zeros((rows, 1), f32)
    result = jnp.zeros((rows, LATENT_WIDTH), f32)
    for score, keys in zip(scores, (own_ref, sib_ref)):
        probability = jnp.exp(score - shift)
        total = total + jnp.sum(probability, axis=-1, keepdims=True)
        result = result + lax.dot_general(
            probability.astype(bf16),
            keys[0, :LATENT_WIDTH],
            (((1,), (1,)), ((), ())),
            preferred_element_type=f32,
        )

    @pl.when(step == 0)
    def _():
        stat_ref[...] = jnp.zeros_like(stat_ref)

    stats = place(place(stat_ref[...], top, step, 0), total, step, 3 * STAT)
    stat_ref[...] = stats
    part = rows // 4
    pieces = part // 16
    for d, out in enumerate(outs):
        for chunk in range(LATENT_WIDTH // LANES):
            tile = result[d * part : (d + 1) * part, chunk * LANES : (chunk + 1) * LANES]
            out[:, step * 4 + chunk] = tile.astype(bf16).reshape(pieces, 16, LANES)

    @pl.when(step == count - 1)
    def _():
        for d, out in enumerate(outs):
            out[:, 4 * count] = stats[d * part : (d + 1) * part].astype(bf16).reshape(pieces, 16, LANES)


def attend(blocks, lengths, queries, cache, sibling, first, count):
    features, block_len = cache.shape[1:]
    tiles = 4 * count + 1
    out = jax.ShapeDtypeStruct((4, tiles, 16, LANES), bf16)
    rows = 4 * queries[0].shape[0] * 16
    return pl.pallas_call(
        functools.partial(attend_kernel, first=first, count=count),
        out_shape=[out] * 4,
        grid_spec=pltpu.PrefetchScalarGridSpec(
            num_scalar_prefetch=2,
            grid=(count,),
            in_specs=[pl.BlockSpec((4, None, 16, features), lambda i, *_: (0, i, 0, 0))] * 4
            + [pl.BlockSpec((1, features, block_len), lambda i, *_: (first + i, 0, 0))] * 2,
            out_specs=[pl.BlockSpec((4, tiles, 16, LANES), lambda i, *_: (0, 0, 0, 0))] * 4,
            scratch_shapes=[pltpu.VMEM((rows, LANES), f32)],
        ),
        compiler_params=pltpu.CompilerParams(
            dimension_semantics=("arbitrary",), vmem_limit_bytes=48 << 20
        ),
        name="attend",
    )(blocks, lengths, *queries, cache, sibling)


def merged_stats(tiles):
    joined = [join3(tile) for tile in tiles]
    sums = [pltpu.roll(one, LANES - 3 * STAT, 1) for one in joined]
    top = functools.reduce(jnp.maximum, joined)
    weights = [jnp.exp(one - top) for one in joined]
    total = sum(weight * one for weight, one in zip(weights, sums))
    return weights, top, total


def merge_kernel(a0, a1, a2, a3, o0, o1, o2, o3, *, count):
    refs = (a0, a1, a2, a3)
    for piece, out in enumerate((o0, o1, o2, o3)):
        weights, top, total = merged_stats([ref[piece, 4 * count].astype(f32) for ref in refs])
        stats = jnp.zeros((16, LANES), f32)
        for request in range(count):
            stats = place(stats, top[:, request : request + 1], request, 0)
            stats = place(stats, total[:, request : request + 1], request, 3 * STAT)
            shares = [weight[:, request : request + 1] for weight in weights]
            for chunk in range(4):
                tile = sum(
                    share * ref[piece, 4 * request + chunk].astype(f32)
                    for share, ref in zip(shares, refs)
                )
                out[4 * request + chunk] = tile.astype(bf16)
        out[4 * count] = stats.astype(bf16)


def merge(pieces, count):
    return pl.pallas_call(
        functools.partial(merge_kernel, count=count),
        out_shape=[jax.ShapeDtypeStruct((4 * count + 1, 16, LANES), bf16)] * 4,
        compiler_params=pltpu.CompilerParams(vmem_limit_bytes=32 << 20),
        name="merge",
    )(*pieces)


def project_kernel(core_ref, *refs, count):
    first, second = refs[0:4], refs[4:8]
    q_ref, keys_ref, up_ref, w_hbm, kept_ref, given_ref, w_ref, rows_ref, sems = refs[8:]
    chunk = kept_ref.shape[2]

    def fetch(k):
        window = pl.ds(k * chunk, chunk)
        return pltpu.make_async_copy(w_hbm.at[:, window], w_ref.at[:, window], sems.at[k])

    for k in range(SPAN):
        fetch(k).start()
    tops, totals, results = [], [], []
    for half in (first, second):
        weights, top, total = merged_stats([ref[4 * count].astype(f32) for ref in half])
        for request in range(count):
            tops.append(top[:, request : request + 1])
            totals.append(total[:, request : request + 1])
            shares = [weight[:, request : request + 1] for weight in weights]
            results.append(
                jnp.concatenate(
                    [
                        sum(
                            share * ref[4 * request + part].astype(f32)
                            for share, ref in zip(shares, half)
                        )
                        for part in range(4)
                    ],
                    axis=1,
                )
            )
    cache_max = jnp.concatenate(tops, axis=0)
    cache_sum = jnp.concatenate(totals, axis=0)
    cache_result = jnp.concatenate(results, axis=0)
    rows = cache_max.shape[0]
    keys = keys_ref[...]
    near = score_scale * lax.dot_general(
        q_ref[...].reshape(rows, keys.shape[1]), keys, (((1,), (1,)), ((), ())), preferred_element_type=f32
    )
    row = lax.broadcasted_iota(jnp.int32, near.shape, 0)
    column = lax.broadcasted_iota(jnp.int32, near.shape, 1)
    seen = (row // 16 == column // 4) & (column % 4 <= (row % 16) // 4)
    near = jnp.where(seen, near, neg_floor)
    joint = jnp.maximum(cache_max, jnp.max(near, axis=-1, keepdims=True))
    rescale = jnp.exp(cache_max - joint)
    probability = jnp.where(seen, jnp.exp(near - joint), 0.0)
    denominator = cache_sum * rescale + jnp.sum(probability, axis=-1, keepdims=True)
    near_result = sum(
        jnp.dot(part.astype(bf16), keys[:, :LATENT_WIDTH], preferred_element_type=f32)
        for part in split3(probability)
    )
    latent = ((cache_result * rescale + near_result) / denominator).astype(bf16)
    grouped = rows // 4
    pick_row = lax.broadcasted_iota(jnp.int32, (grouped, rows), 0)
    pick_column = lax.broadcasted_iota(jnp.int32, (grouped, rows), 1)
    halves = grouped // 2
    core = core_ref[0]
    order = 2 * (pick_row % halves) + jnp.where(pick_row < halves, core, 1 - core)
    values = []
    for head in range(4):
        head_value = jnp.dot(latent, up_ref[head], preferred_element_type=f32).astype(bf16)
        pick = (pick_column == 4 * order + head).astype(f32).astype(bf16)
        values.append(jnp.dot(pick, head_value, preferred_element_type=f32).astype(bf16))
    values = jnp.concatenate(values, axis=1)
    for k in range(SPAN):
        fetch(k).wait()
        block = jnp.dot(values, w_ref[:, k * chunk : (k + 1) * chunk], preferred_element_type=f32)
        for piece in range(chunk // LANES):
            rows_ref[piece, pl.ds(k, grouped, stride=SPAN), :] = block[:, piece * LANES : (piece + 1) * LANES]
    for piece in range(chunk // LANES):
        window = slice(piece * LANES, (piece + 1) * LANES)
        whole = rows_ref[piece].reshape(grouped, SPAN, LANES).astype(bf16)
        kept_ref[:, :, window] = whole[:halves]
        given_ref[:, :, window] = whole[halves:]


SPAN = 8


def project(core, first, second, own_query, new_keys, value_up, w_out, count):
    grouped = new_keys.shape[0]
    width = w_out.shape[1]
    out = jax.ShapeDtypeStruct((grouped // 2, SPAN, width // SPAN), bf16)
    inside = pl.BlockSpec(memory_space=pltpu.VMEM)
    return pl.pallas_call(
        functools.partial(project_kernel, count=count),
        out_shape=[out, out],
        in_specs=[pl.BlockSpec(memory_space=pltpu.SMEM)] + [inside] * 11 + [pl.BlockSpec(memory_space=pltpu.HBM)],
        out_specs=[inside] * 2,
        scratch_shapes=[
            pltpu.VMEM(w_out.shape, bf16),
            pltpu.VMEM((width // SPAN // LANES, grouped * SPAN, LANES), f32),
            pltpu.SemaphoreType.DMA((SPAN,)),
        ],
        compiler_params=pltpu.CompilerParams(vmem_limit_bytes=32 << 20),
        name="project",
    )(core, *first, *second, own_query, new_keys, value_up, pltpu.with_memory_space_constraint(w_out, pltpu.HBM))


def spread_kernel(arrived_ref, residual_ref, gain_ref, chosen_ref, attn_ref, stream_ref, rows_ref):
    attention = jnp.sum(arrived_ref[...].astype(f32), axis=0)
    attn_ref[...] = attention.astype(bf16)
    stream = (residual_ref[...].astype(f32) + attention).astype(bf16)
    stream_ref[...] = stream
    wide = stream.astype(f32)
    square = jnp.sum(jnp.sum(wide * wide, axis=1, keepdims=True), axis=0, keepdims=True)
    mean_square = square / (wide.shape[0] * wide.shape[1])
    normed = (wide * lax.rsqrt(mean_square + norm_eps) * gain_ref[...]).astype(bf16)
    row = jnp.concatenate([normed, chosen_ref[...]], axis=1)
    rows_ref[...] = jnp.broadcast_to(row[None], rows_ref.shape)


def spread(arrived, residual, gain, chosen, chips):
    one = jax.ShapeDtypeStruct(residual.shape, bf16)
    rows = jax.ShapeDtypeStruct((chips, SPAN, residual.shape[1] + LANES), bf16)
    return pl.pallas_call(
        spread_kernel,
        out_shape=[one, one, rows],
        compiler_params=pltpu.CompilerParams(vmem_limit_bytes=32 << 20),
        name="spread",
    )(arrived, residual, gain, chosen)


def experts_kernel(
    expert_ref, own_ref, sib_ref, router_ref, gate_hbm, up_hbm, down_hbm, out_own, out_sib,
    gate_ref, up_ref, down_ref, rows_ref, sems
):
    half = own_ref.shape[0]
    rows = 2 * half
    chunk = out_own.shape[2]
    tiles = chunk // LANES

    def fetch(which, k):
        window = pl.ds(k * chunk, chunk)
        source, target = ((gate_hbm, gate_ref), (up_hbm, up_ref), (down_hbm, down_ref))[which]
        if which == 2:
            return pltpu.make_async_copy(source.at[:, window], target.at[:, window], sems.at[which, k])
        return pltpu.make_async_copy(source.at[window], target.at[window], sems.at[which, k])

    for k in range(SPAN):
        fetch(0, k).start()
        fetch(1, k).start()
    for k in range(SPAN):
        fetch(2, k).start()
    for piece in range(tiles):
        window = slice(piece * LANES, (piece + 1) * LANES)
        rows_ref[piece, : half * SPAN] = own_ref[:, :, window].astype(f32).reshape(half * SPAN, LANES)
        rows_ref[piece, half * SPAN :] = sib_ref[:, :, window].astype(f32).reshape(half * SPAN, LANES)
    gate = up = values = 0.0
    for k in range(SPAN):
        block = jnp.concatenate(
            [rows_ref[piece, pl.ds(k, rows, stride=SPAN), :] for piece in range(tiles)], axis=1
        ).astype(bf16)
        values = values + lax.dot_general(
            block,
            router_ref[:, k * chunk : (k + 1) * chunk],
            (((1,), (1,)), ((), ())),
            preferred_element_type=f32,
        )
        fetch(0, k).wait()
        gate = gate + jnp.dot(block, gate_ref[k * chunk : (k + 1) * chunk], preferred_element_type=f32)
        fetch(1, k).wait()
        up = up + jnp.dot(block, up_ref[k * chunk : (k + 1) * chunk], preferred_element_type=f32)
    hidden = (gate / (1.0 + jnp.exp(-gate)) * up).astype(bf16)
    values = 1.0 / (1.0 + jnp.exp(-values))
    chosen = jnp.concatenate(
        [ref[:, :, chunk:].astype(f32).reshape(half * SPAN, LANES) for ref in (own_ref, sib_ref)], axis=0
    )
    rows_ref[0] = chosen
    chosen = rows_ref[0, pl.ds(0, rows, stride=SPAN), :][:, :EXPERTS]
    picked = values * chosen
    lane = lax.broadcasted_iota(jnp.int32, picked.shape, 1)
    mine = jnp.sum(jnp.where(lane == expert_ref[0], picked, 0.0), axis=-1, keepdims=True)
    share = route_scale * mine / jnp.sum(picked, axis=-1, keepdims=True)
    for k in range(SPAN):
        fetch(2, k).wait()
        result = share * jnp.dot(
            hidden, down_ref[:, k * chunk : (k + 1) * chunk], preferred_element_type=f32
        )
        for piece in range(tiles):
            rows_ref[piece, pl.ds(k, rows, stride=SPAN), :] = result[:, piece * LANES : (piece + 1) * LANES]
    for piece in range(tiles):
        window = slice(piece * LANES, (piece + 1) * LANES)
        out_own[:, :, window] = rows_ref[piece, : half * SPAN].reshape(half, SPAN, LANES).astype(bf16)
        out_sib[:, :, window] = rows_ref[piece, half * SPAN :].reshape(half, SPAN, LANES).astype(bf16)


def experts(expert, own_rows, sibling_rows, w_gate, w_up, w_router, w_down):
    width = w_gate.shape[0]
    half = own_rows.shape[0]
    out = jax.ShapeDtypeStruct((half, SPAN, width // SPAN), bf16)
    inside = pl.BlockSpec(memory_space=pltpu.VMEM)
    outside = pl.BlockSpec(memory_space=pltpu.HBM)
    return pl.pallas_call(
        experts_kernel,
        out_shape=[out, out],
        in_specs=[pl.BlockSpec(memory_space=pltpu.SMEM)] + [inside] * 3 + [outside] * 3,
        out_specs=[inside] * 2,
        scratch_shapes=[
            pltpu.VMEM(w_gate.shape, bf16),
            pltpu.VMEM(w_up.shape, bf16),
            pltpu.VMEM(w_down.shape, bf16),
            pltpu.VMEM((width // SPAN // LANES, 2 * half * SPAN, LANES), f32),
            pltpu.SemaphoreType.DMA((3, SPAN)),
        ],
        compiler_params=pltpu.CompilerParams(vmem_limit_bytes=48 << 20),
        name="experts",
    )(expert, own_rows, sibling_rows, w_router.T, w_gate, w_up, w_down)


def shift_by(value, axis, offset):
    size = lax.axis_size(axis)
    return lax.ppermute(value, axis, [(i, (i + offset) % size) for i in range(size)])


def all_shifts(value, axis):
    return [value] + [shift_by(value, axis, d) for d in range(1, lax.axis_size(axis))]


def return_shifts(pieces, axis):
    return [pieces[0]] + [shift_by(piece, axis, -d) for d, piece in enumerate(pieces) if d > 0]


def local(
    query,
    cache,
    new_keys,
    lengths,
    value_up_weight,
    w_out,
    residual,
    norm_gain,
    w_router,
    routes,
    w_gate,
    w_up,
    w_down,
):
    y, x, z, core = (lax.axis_index(name) for name in ("y", "x", "z", "c"))
    ctx = (x * lax.axis_size("z") + z) * 2 + core
    requests = lengths.shape[0]
    features = query.shape[-1]
    width = w_out.shape[1]
    count = requests // 2
    cache = cache.swapaxes(1, 2)
    sibling_cache = shift_by(cache, "c", 1)
    own_query = query.reshape(requests, -1, features)
    stack_x = jnp.stack(all_shifts(own_query[:count], "x"))
    stack_z = jnp.stack(all_shifts(own_query[count:], "z"))
    queries_a = all_shifts(stack_x, "z")
    queries_b = all_shifts(stack_z, "x")
    blocks = jnp.stack([ctx, ctx ^ 1]).astype(jnp.int32)
    out_a = attend(blocks, lengths, queries_a, cache, sibling_cache, 0, count)
    out_b = attend(blocks, lengths, queries_b, cache, sibling_cache, count, count)
    final_a = return_shifts(merge(return_shifts(out_a, "z"), count), "x")
    final_b = return_shifts(merge(return_shifts(out_b, "x"), count), "z")
    kept, given = project(
        core.astype(jnp.int32).reshape(1), final_a, final_b, own_query, new_keys, value_up_weight, w_out, count
    )
    chip_sum = (kept.astype(f32) + shift_by(given, "c", 1).astype(f32)).astype(bf16)
    arrived = lax.all_to_all(chip_sum, ("x", "z"), split_axis=0, concat_axis=0, tiled=True)
    lanes = jnp.arange(LANES, dtype=jnp.int32)
    chosen = jnp.any(routes[:, :, None] == lanes[None, None, :], axis=1).astype(bf16)
    chosen = jnp.pad(chosen, ((0, SPAN - 1), (0, 0)))
    chips = lax.axis_size("y") * lax.axis_size("x") * lax.axis_size("z")
    attn_out, stream, rows = spread(
        arrived, residual.reshape(SPAN, -1), norm_gain.reshape(SPAN, -1), chosen, chips
    )
    own_rows = lax.all_to_all(rows, ("y", "x", "z"), split_axis=0, concat_axis=0, tiled=True)
    sibling_rows = shift_by(own_rows, "c", 1)
    devices = 2 * chips
    flat = y * (devices // lax.axis_size("y")) + ctx
    expert = (flat // (devices // EXPERTS)).astype(jnp.int32).reshape(1)
    out_own, out_sibling = experts(expert, own_rows, sibling_rows, w_gate, w_up, w_router, w_down)
    chip_out = (out_own.astype(f32) + shift_by(out_sibling, "c", 1).astype(f32)).astype(bf16)
    returned = lax.all_to_all(chip_out, ("y", "x", "z"), split_axis=0, concat_axis=0, tiled=True)
    layer_out = (stream.astype(f32) + jnp.sum(returned.astype(f32), axis=0)).astype(bf16)
    return (attn_out.reshape(1, width), layer_out.reshape(1, width))


def solution(mesh):
    names = ("y", "x", "z", "c")
    fine = Mesh(mesh.devices.reshape(4, 4, 4, 2), names)
    group, ctx = "y", ("x", "z", "c")
    return jax.shard_map(
        local,
        mesh=fine,
        in_specs=(
            P(group, ctx, None),
            P(group, ctx, None),
            P(group, None),
            P(group),
            P(ctx, None, None),
            P(ctx, None),
            P(names, None),
            P(),
            P(),
            P(names, None),
            P(None, names),
            P(None, names),
            P(names, None),
        ),
        out_specs=(P(names, None), P(names, None)),
        check_vma=False,
    )
```

time: 508 us -> 177 us (0.35)
  waiting for transfers between devices: 279 us -> 58.9 us
  local copies, waits for them, and re-layouts: 59.1 us -> 3.24 us
  matrix products: 45.3 us -> 0 us
  blocking collectives: 68.8 us -> 25 us
  Pallas kernels: 0 us -> 36.2 us
  starting transfers between devices: 17 us -> 50 us
  other arithmetic: 22.2 us -> 2.45 us
  between operations: 15.1 us -> 0.89 us
    unnamed x3 -> x0, waiting for transfers between devices: 112 us -> none
    all_to_all x3 -> x2, waiting for transfers between devices: 116 us -> 25.8 us  [the longest x1 17.3 us: local(): lax.all_to_all(chip_out, ('y', 'x', 'z'), split_axis=0, concat_axis=0, ti...]
    all_gather x1 -> x0, waiting for transfers between devices: 50.7 us -> none  [local(): all_heads = lax.all_gather(query, 'ctx', axis=1, tiled=True)]
    dot_general x10 -> x0, matrix products: 45.3 us -> none  [the longest x1 13 us: local(): jnp.einsum('rqht,rtk->rqhk', probability.astype(jnp.bfloat16), compressed...]
    all_to_all x2 -> x1, blocking collectives: 68.8 us -> 25 us  [local(): lax.all_to_all(rows, ('y', 'x', 'z'), split_axis=0, concat_axis=0, tiled=...]
    ppermute x0 -> x28, starting transfers between devices: none -> 41.7 us  [shift_by(): lax.ppermute(value, axis, [(i, (i + offset) % size) for i in range(size)])]
    pallas_call x0 -> x7, Pallas kernels: none -> 36.2 us  [the longest x2 21.4 us: attend(): pl.pallas_call(functools.partial(attend_kernel, first=first, count=count)...]
    unnamed x29 -> x18, local copies, waits for them, and re-layouts: 37.8 us -> 1.96 us
  transfers between devices with their start and end apart: 5 -> 30, of which waited for: 4 -> 16; matrix products, arithmetic and copies ran while one was open for 6% -> 1% of each run, Pallas kernels for 0% -> 13%
where the time goes in v1:
time: 177 us
  waiting for transfers between devices  58.9 us (33%)
  starting transfers between devices  50 us (28%)
  Pallas kernels  36.2 us (20%)
  blocking collectives  25 us (14%)
  local copies, waits for them, and re-layouts  3.24 us (2%)
  other arithmetic  2.45 us (1%)
    ppermute x28, starting transfers between devices, shift_by(): lax.ppermute(value, axis, [(i, (i + offset) % size) for i in range(size)])  41.7 us
    ppermute x28, waiting for transfers between devices, shift_by(): lax.ppermute(value, axis, [(i, (i + offset) % size) for i in range(size)])  33.1 us
    all_to_all x1, blocking collectives, local(): lax.all_to_all(rows, ('y', 'x', 'z'), split_axis=0, concat_axis=0, tiled=...  25 us
    pallas_call x2, Pallas kernels, attend(): pl.pallas_call(functools.partial(attend_kernel, first=first, count=count)...  21.4 us
    all_to_all x1, waiting for transfers between devices, local(): lax.all_to_all(chip_out, ('y', 'x', 'z'), split_axis=0, concat_axis=0, ti...  17.3 us
    all_to_all x1, waiting for transfers between devices, local(): lax.all_to_all(chip_sum, ('x', 'z'), split_axis=0, concat_axis=0, tiled=T...  8.51 us
    pallas_call x1, Pallas kernels, experts(): pl.pallas_call(experts_kernel, out_shape=[out, out], in_specs=[pl.BlockSp...  8.14 us
    pallas_call x1, Pallas kernels, project(): pl.pallas_call(functools.partial(project_kernel, count=count), out_shape=...  4.74 us
  transfers between devices with their start and end apart: 30, of which 16 were waited for; matrix products, arithmetic and copies ran while one was open for 1% of the time, Pallas kernels for 13%

profile of v1, /device:TPU:0, one launch (start us, length us, event | category | flops | bytes accessed | tf_op | source)
XLA Modules:
  0.0 176.7 jit_solution(12951966487894953054)
XLA Ops:
  0.6 0.1 collective-permute-start.6
  0.7 1.0 fusion.2
  1.8 2.1 %collective-permute-start.13 = (bf16[4,16,576]{2,1,0:T(8,128)(2,1)S(1)}, bf16[4,16,576]{2,1,0:T(8,128)(2,1)S(1)}, u32[]{:S(2)}, u32[]{:S(2)}) collective-permute-start(bf16[4,16,576]{2,1,0:T(8,128)(2,1)S(1)} %slice.15), channel_id=1, source_target_pairs={{0,2},{2,4},{4,6},{6,0},{1,3},{3,5},{5,7},{7,1},{8,10},{10,12},{12... | collective-permute-start | bytes 221192 | tf_op jit(solution)/shard_map/ppermute | solution.py:361
  3.8 3.6 %collective-permute-start.14 = (bf16[4,16,576]{2,1,0:T(8,128)(2,1)S(1)}, bf16[4,16,576]{2,1,0:T(8,128)(2,1)S(1)}, u32[]{:S(2)}, u32[]{:S(2)}) collective-permute-start(bf16[4,16,576]{2,1,0:T(8,128)(2,1)S(1)} %slice.15), channel_id=1, source_target_pairs={{0,4},{2,6},{4,0},{6,2},{1,5},{3,7},{5,1},{7,3},{8,12},{10,14},{12... | collective-permute-start | bytes 221192 | tf_op jit(solution)/shard_map/ppermute | solution.py:361
  7.4 1.0 collective-permute-start.15
  8.5 0.6 collective-permute-done.13
  9.0 2.9 %collective-permute-done.14 = bf16[4,16,576]{2,1,0:T(8,128)(2,1)S(1)} collective-permute-done((bf16[4,16,576]{2,1,0:T(8,128)(2,1)S(1)}, bf16[4,16,576]{2,1,0:T(8,128)(2,1)S(1)}, u32[]{:S(2)}, u32[]{:S(2)}) %collective-permute-start.14) | collective-permute-done | bytes 73760 | tf_op jit(solution)/shard_map/ppermute | solution.py:361
  12.0 0.1 pad_maximum_fusion.1.q0
  12.1 1.6 collective-permute-start.16
  13.6 2.7 %collective-permute-start.17 = (bf16[4,4,16,576]{3,2,1,0:T(8,128)(2,1)S(1)}, bf16[4,4,16,576]{3,2,1,0:T(8,128)(2,1)S(1)}, u32[]{:S(2)}, u32[]{:S(2)}) collective-permute-start(bf16[4,4,16,576]{3,2,1,0:T(8,128)(2,1)S(1)} %pad_maximum_fusion.1.q0), channel_id=1, source_target_pairs={{0,16},{8,24},{16,0},{24,8},{1,17},{9,25},{17,1},{25,9},{2,18},{10... | collective-permute-start | bytes 884744 | tf_op jit(solution)/shard_map/ppermute | solution.py:361
  16.4 0.1 collective-permute-start
  16.5 2.9 %collective-permute-start.1 = (bf16[4,16,576]{2,1,0:T(8,128)(2,1)S(1)}, bf16[4,16,576]{2,1,0:T(8,128)(2,1)S(1)}, u32[]{:S(2)}, u32[]{:S(2)}) collective-permute-start(bf16[4,16,576]{2,1,0:T(8,128)(2,1)S(1)} %slice.13), channel_id=1, source_target_pairs={{0,16},{8,24},{16,0},{24,8},{1,17},{9,25},{17,1},{25,9},{2,18},{10... | collective-permute-start | bytes 221192 | tf_op jit(solution)/shard_map/ppermute | solution.py:361
  19.4 11.5 %collective-permute-done = bf16[4,16,576]{2,1,0:T(8,128)(2,1)S(1)} collective-permute-done((bf16[4,16,576]{2,1,0:T(8,128)(2,1)S(1)}, bf16[4,16,576]{2,1,0:T(8,128)(2,1)S(1)}, u32[]{:S(2)}, u32[]{:S(2)}) %collective-permute-start) | collective-permute-done | bytes 73760 | tf_op jit(solution)/shard_map/ppermute | solution.py:361
  30.9 3.0 %collective-permute-start.2 = (bf16[4,16,576]{2,1,0:T(8,128)(2,1)S(1)}, bf16[4,16,576]{2,1,0:T(8,128)(2,1)S(1)}, u32[]{:S(2)}, u32[]{:S(2)}) collective-permute-start(bf16[4,16,576]{2,1,0:T(8,128)(2,1)S(1)} %slice.13), channel_id=1, source_target_pairs={{0,24},{8,0},{16,8},{24,16},{1,25},{9,1},{17,9},{25,17},{2,26},{10... | collective-permute-start | bytes 221192 | tf_op jit(solution)/shard_map/ppermute | solution.py:361
  33.9 0.3 collective-permute-done.1
  34.2 0.5 collective-permute-start.18
  34.7 2.1 %collective-permute-done.2 = bf16[4,16,576]{2,1,0:T(8,128)(2,1)S(1)} collective-permute-done((bf16[4,16,576]{2,1,0:T(8,128)(2,1)S(1)}, bf16[4,16,576]{2,1,0:T(8,128)(2,1)S(1)}, u32[]{:S(2)}, u32[]{:S(2)}) %collective-permute-start.2) | collective-permute-done | bytes 73760 | tf_op jit(solution)/shard_map/ppermute | solution.py:361
  36.8 0.1 pad_maximum_fusion.q0
  36.9 1.3 collective-permute-start.3
  38.2 2.0 %collective-permute-start.4 = (bf16[4,4,16,576]{3,2,1,0:T(8,128)(2,1)S(1)}, bf16[4,4,16,576]{3,2,1,0:T(8,128)(2,1)S(1)}, u32[]{:S(2)}, u32[]{:S(2)}) collective-permute-start(bf16[4,4,16,576]{3,2,1,0:T(8,128)(2,1)S(1)} %pad_maximum_fusion.q0), channel_id=1, source_target_pairs={{0,4},{2,6},{4,0},{6,2},{1,5},{3,7},{5,1},{7,3},{8,12},{10,14},{12... | collective-permute-start | bytes 884744 | tf_op jit(solution)/shard_map/ppermute | solution.py:361
  40.2 1.3 collective-permute-start.5
  41.5 0.1 pad_add_fusion.blocks_ref
  41.6 0.8 collective-permute-done.18.q3
  42.4 0.7 copy-done.3
  43.0 10.7 %attend.3 = (bf16[4,17,16,128]{3,2,1,0:T(8,128)(2,1)S(1)}, bf16[4,17,16,128]{3,2,1,0:T(8,128)(2,1)S(1)}, bf16[4,17,16,128]{3,2,1,0:T(8,128)(2,1)S(1)}, bf16[4,17,16,128]{3,2,1,0:T(8,128)(2,1)S(1)}) custom-call(s32[2]{0:T(128)S(1)} %pad_add_fusion.blocks_ref, s32[8]{0:T(128)S(1)} %copy-done.3, bf16[4,4,16,576]{3,2,1,0:T(8,128)(2,1)S(1)} %pad_maximum_fusion.1.q0, ...), custom_call_target="tpu_custom_call" | custom-call | tf_op jit(solution)/shard_map/attend/pallas_call | solution.py:96
  53.8 3.0 %collective-permute-start.19 = (bf16[4,17,16,128]{3,2,1,0:T(8,128)(2,1)S(1)}, bf16[4,17,16,128]{3,2,1,0:T(8,128)(2,1)S(1)}, u32[]{:S(2)}, u32[]{:S(2)}) collective-permute-start(bf16[4,17,16,128]{3,2,1,0:T(8,128)(2,1)S(1)} %get-tuple-element.34), channel_id=1, source_target_pairs={{0,24},{8,0},{16,8},{24,16},{1,25},{9,1},{17,9},{25,17},{2,26},{10... | collective-permute-start | bytes 835592 | tf_op jit(solution)/shard_map/ppermute | solution.py:361
  56.8 1.0 collective-permute-start.21
  57.8 10.7 %attend.2 = (bf16[4,17,16,128]{3,2,1,0:T(8,128)(2,1)S(1)}, bf16[4,17,16,128]{3,2,1,0:T(8,128)(2,1)S(1)}, bf16[4,17,16,128]{3,2,1,0:T(8,128)(2,1)S(1)}, bf16[4,17,16,128]{3,2,1,0:T(8,128)(2,1)S(1)}) custom-call(s32[2]{0:T(128)S(1)} %pad_add_fusion.blocks_ref, s32[8]{0:T(128)S(1)} %copy-done.3, bf16[4,4,16,576]{3,2,1,0:T(8,128)(2,1)S(1)} %pad_maximum_fusion.q0, ...), custom_call_target="tpu_custom_call" | custom-call | tf_op jit(solution)/shard_map/attend/pallas_call | solution.py:96
  68.5 1.1 collective-permute-start.7
  69.6 1.7 collective-permute-start.8
  71.3 0.3 collective-permute-start.9
  71.6 0.8 merge.3
  72.4 3.0 %collective-permute-start.22 = (bf16[17,16,128]{2,1,0:T(8,128)(2,1)S(1)}, bf16[17,16,128]{2,1,0:T(8,128)(2,1)S(1)}, u32[]{:S(2)}, u32[]{:S(2)}) collective-permute-start(bf16[17,16,128]{2,1,0:T(8,128)(2,1)S(1)} %get-tuple-element.38), channel_id=1, source_target_pairs={{0,6},{2,0},{4,2},{6,4},{1,7},{3,1},{5,3},{7,5},{8,14},{10,8},{12,... | collective-permute-start | bytes 208904 | tf_op jit(solution)/shard_map/ppermute | solution.py:361
  75.5 0.6 collective-permute-start.23
  76.0 1.8 collective-permute-done.7.a1
  77.8 4.2 %collective-permute-start.24 = (bf16[17,16,128]{2,1,0:T(8,128)(2,1)S(1)}, bf16[17,16,128]{2,1,0:T(8,128)(2,1)S(1)}, u32[]{:S(2)}, u32[]{:S(2)}) collective-permute-start(bf16[17,16,128]{2,1,0:T(8,128)(2,1)S(1)} %get-tuple-element.40), channel_id=1, source_target_pairs={{0,2},{2,4},{4,6},{6,0},{1,3},{3,5},{5,7},{7,1},{8,10},{10,12},{12... | collective-permute-start | bytes 208904 | tf_op jit(solution)/shard_map/ppermute | solution.py:361
  82.0 1.4 collective-permute-done.9.a3
  83.4 0.8 merge.2
  84.2 2.4 %collective-permute-start.10 = (bf16[17,16,128]{2,1,0:T(8,128)(2,1)S(1)}, bf16[17,16,128]{2,1,0:T(8,128)(2,1)S(1)}, u32[]{:S(2)}, u32[]{:S(2)}) collective-permute-start(bf16[17,16,128]{2,1,0:T(8,128)(2,1)S(1)} %get-tuple-element.30), channel_id=1, source_target_pairs={{0,24},{8,0},{16,8},{24,16},{1,25},{9,1},{17,9},{25,17},{2,26},{10... | collective-permute-start | bytes 208904 | tf_op jit(solution)/shard_map/ppermute | solution.py:361
  86.6 2.0 %collective-permute-start.11 = (bf16[17,16,128]{2,1,0:T(8,128)(2,1)S(1)}, bf16[17,16,128]{2,1,0:T(8,128)(2,1)S(1)}, u32[]{:S(2)}, u32[]{:S(2)}) collective-permute-start(bf16[17,16,128]{2,1,0:T(8,128)(2,1)S(1)} %get-tuple-element.31), channel_id=1, source_target_pairs={{0,16},{8,24},{16,0},{24,8},{1,17},{9,25},{17,1},{25,9},{2,18},{10... | collective-permute-start | bytes 208904 | tf_op jit(solution)/shard_map/ppermute | solution.py:361
  88.6 0.1 reshape.80.refs_8_
  88.7 0.1 collective-permute-done.10.refs_1_
  88.9 3.6 %collective-permute-done.11.refs_2_ = bf16[17,16,128]{2,1,0:T(8,128)(2,1)S(1)} collective-permute-done((bf16[17,16,128]{2,1,0:T(8,128)(2,1)S(1)}, bf16[17,16,128]{2,1,0:T(8,128)(2,1)S(1)}, u32[]{:S(2)}, u32[]{:S(2)}) %collective-permute-start.11) | collective-permute-done | bytes 69664 | tf_op jit(solution)/shard_map/ppermute | solution.py:361
  92.4 1.7 collective-permute-done.12.refs_3_
  94.2 4.7 %project.1 = (bf16[16,8,896]{2,1,0:T(8,128)(2,1)S(1)}, bf16[16,8,896]{2,1,0:T(8,128)(2,1)S(1)}) custom-call(s32[1]{0:T(128)} %bitcast.core_ref, bf16[17,16,128]{2,1,0:T(8,128)(2,1)S(1)} %get-tuple-element.29.refs_0_, bf16[17,16,128]{2,1,0:T(8,128)(2,1)S(1)} %collective-permute-done.10.refs_1_, bf16[17,16,128]{2,1,0:T(8,128)(2,1)S(1)} %collective-permute-done.11.refs_2_, ...), custom_call_target="tpu_custom_call" | custom-call | tf_op jit(solution)/shard_map/project/pallas_call | solution.py:233
  98.9 0.1 collective-permute-start.25
  99.1 0.1 reduce.1
  99.2 1.3 collective-permute-done.25
  100.5 0.7 add_convert_fusion.1
  101.3 3.6 %all-to-all-start = ((bf16[16,8,896]{2,1,0:T(8,128)(2,1)}), bf16[16,8,896]{2,1,0:T(8,128)(2,1)S(1)}, u32[]{:S(2)}, u32[]{:S(2)}) async-start(bf16[16,8,896]{2,1,0:T(8,128)(2,1)} %add_convert_fusion.1), calls=%async_computation | async-start | bytes 458752 | tf_op jit(solution)/shard_map/all_to_all | solution.py:409
  104.9 0.1 fusion.1
  105.0 8.5 %all-to-all-done.arrived_ref = bf16[16,8,896]{2,1,0:T(8,128)(2,1)S(1)} async-done(((bf16[16,8,896]{2,1,0:T(8,128)(2,1)}), bf16[16,8,896]{2,1,0:T(8,128)(2,1)S(1)}, u32[]{:S(2)}, u32[]{:S(2)}) %all-to-all-start) | async-done | bytes 229408 | tf_op jit(solution)/shard_map/all_to_all | solution.py:409
  113.5 0.2 spread.1
  113.7 25.0 %all_to_all.15.own_ref = bf16[64,8,1024]{2,1,0:T(8,128)(2,1)S(1)} all-to-all(bf16[64,8,1024]{2,1,0:T(8,128)(2,1)S(1)} %get-tuple-element.45), channel_id=1, replica_groups=mesh['y'=4,'x'=4,'z'=4,'c'=2] {'y','x','z'}, dimensions={0} | all-to-all | bytes 2097152 | tf_op jit(solution)/shard_map/all_to_all | solution.py:417
  138.7 2.7 %collective-permute-done.26.sib_ref = bf16[64,8,1024]{2,1,0:T(8,128)(2,1)S(1)} collective-permute-done((bf16[64,8,1024]{2,1,0:T(8,128)(2,1)S(1)}, bf16[64,8,1024]{2,1,0:T(8,128)(2,1)S(1)}, u32[]{:S(2)}, u32[]{:S(2)}) %collective-permute-start.26) | collective-permute-done | bytes 1048608 | tf_op jit(solution)/shard_map/ppermute | solution.py:361
  141.4 8.1 %experts.1 = (bf16[64,8,896]{2,1,0:T(8,128)(2,1)S(1)}, bf16[64,8,896]{2,1,0:T(8,128)(2,1)S(1)}) custom-call(s32[1]{0:T(128)} %bitcast.12.expert_ref, bf16[64,8,1024]{2,1,0:T(8,128)(2,1)S(1)} %all_to_all.15.own_ref, bf16[64,8,1024]{2,1,0:T(8,128)(2,1)S(1)} %collective-permute-done.26.sib_ref, bf16[16,7168]{1,0:T(8,128)(2,1)S(1)} %bitcast.21, ...), custom_call_target="tpu_custom_call" | custom-call | tf_op jit(solution)/shard_map/experts/pallas_call | solution.py:342
  149.6 0.2 collective-permute-start.27
  149.8 2.3 %collective-permute-done.27 = bf16[64,8,896]{2,1,0:T(8,128)(2,1)S(1)} collective-permute-done((bf16[64,8,896]{2,1,0:T(8,128)(2,1)S(1)}, bf16[64,8,896]{2,1,0:T(8,128)(2,1)S(1)}, u32[]{:S(2)}, u32[]{:S(2)}) %collective-permute-start.27) | collective-permute-done | bytes 917536 | tf_op jit(solution)/shard_map/ppermute | solution.py:361
  152.1 1.2 add_convert_fusion
  153.3 4.7 %all-to-all-start.2 = ((bf16[64,8,896]{2,1,0:T(8,128)(2,1)}), bf16[64,8,896]{2,1,0:T(8,128)(2,1)S(1)}, u32[]{:S(2)}, u32[]{:S(2)}) async-start(bf16[64,8,896]{2,1,0:T(8,128)(2,1)} %add_convert_fusion), calls=%async_computation.2 | async-start | bytes 1835008 | tf_op jit(solution)/shard_map/all_to_all | solution.py:424
  158.0 0.6 copy.15
  158.6 17.3 %all-to-all-done.2 = bf16[64,8,896]{2,1,0:T(8,128)(2,1)S(1)} async-done(((bf16[64,8,896]{2,1,0:T(8,128)(2,1)}), bf16[64,8,896]{2,1,0:T(8,128)(2,1)S(1)}, u32[]{:S(2)}, u32[]{:S(2)}) %all-to-all-start.2) | async-done | bytes 917536 | tf_op jit(solution)/shard_map/all_to_all | solution.py:424
  175.9 0.2 convert_reduce_fusion
  176.0 0.6 copy.16
  (40 shorter events, 0.3 us)
Async XLA Ops:
  0.6 41.7 %collective-permute-start.6 = (bf16[8,576,1024]{2,1,0:T(8,128)(2,1)}, bf16[8,576,1024]{2,1,0:T(8,128)(2,1)}, u32[]{:S(2)}, u32[]{:S(2)}) collective-permute-start(bf16[8,576,1024]{2,1,0:T(8,128)(2,1)} %bitcast.23), channel_id=1, source_target_pairs={{0,1},{1,0},{2,3},{3,2},{4,5},{5,4},{6,7},{7,6},{8,9},{9,8},{10,11... | collective-permute-start | bytes 28311560 | tf_op jit(solution)/shard_map/ppermute | solution.py:361
  1.8 7.3 %collective-permute-start.13 = (bf16[4,16,576]{2,1,0:T(8,128)(2,1)S(1)}, bf16[4,16,576]{2,1,0:T(8,128)(2,1)S(1)}, u32[]{:S(2)}, u32[]{:S(2)}) collective-permute-start(bf16[4,16,576]{2,1,0:T(8,128)(2,1)S(1)} %slice.15), channel_id=1, source_target_pairs={{0,2},{2,4},{4,6},{6,0},{1,3},{3,5},{5,7},{7,1},{8,10},{10,12},{12... | collective-permute-start | bytes 221192 | tf_op jit(solution)/shard_map/ppermute | solution.py:361
  3.8 8.2 %collective-permute-start.14 = (bf16[4,16,576]{2,1,0:T(8,128)(2,1)S(1)}, bf16[4,16,576]{2,1,0:T(8,128)(2,1)S(1)}, u32[]{:S(2)}, u32[]{:S(2)}) collective-permute-start(bf16[4,16,576]{2,1,0:T(8,128)(2,1)S(1)} %slice.15), channel_id=1, source_target_pairs={{0,4},{2,6},{4,0},{6,2},{1,5},{3,7},{5,1},{7,3},{8,12},{10,14},{12... | collective-permute-start | bytes 221192 | tf_op jit(solution)/shard_map/ppermute | solution.py:361
  7.4 4.6 %collective-permute-start.15 = (bf16[4,16,576]{2,1,0:T(8,128)(2,1)S(1)}, bf16[4,16,576]{2,1,0:T(8,128)(2,1)S(1)}, u32[]{:S(2)}, u32[]{:S(2)}) collective-permute-start(bf16[4,16,576]{2,1,0:T(8,128)(2,1)S(1)} %slice.15), channel_id=1, source_target_pairs={{0,6},{2,0},{4,2},{6,4},{1,7},{3,1},{5,3},{7,5},{8,14},{10,8},{12,... | collective-permute-start | bytes 221192 | tf_op jit(solution)/shard_map/ppermute | solution.py:361
  12.1 26.1 %collective-permute-start.16 = (bf16[4,4,16,576]{3,2,1,0:T(8,128)(2,1)S(1)}, bf16[4,4,16,576]{3,2,1,0:T(8,128)(2,1)S(1)}, u32[]{:S(2)}, u32[]{:S(2)}) collective-permute-start(bf16[4,4,16,576]{3,2,1,0:T(8,128)(2,1)S(1)} %pad_maximum_fusion.1.q0), channel_id=1, source_target_pairs={{0,8},{8,16},{16,24},{24,0},{1,9},{9,17},{17,25},{25,1},{2,10},{10... | collective-permute-start | bytes 884744 | tf_op jit(solution)/shard_map/ppermute | solution.py:361
  13.6 26.5 %collective-permute-start.17 = (bf16[4,4,16,576]{3,2,1,0:T(8,128)(2,1)S(1)}, bf16[4,4,16,576]{3,2,1,0:T(8,128)(2,1)S(1)}, u32[]{:S(2)}, u32[]{:S(2)}) collective-permute-start(bf16[4,4,16,576]{3,2,1,0:T(8,128)(2,1)S(1)} %pad_maximum_fusion.1.q0), channel_id=1, source_target_pairs={{0,16},{8,24},{16,0},{24,8},{1,17},{9,25},{17,1},{25,9},{2,18},{10... | collective-permute-start | bytes 884744 | tf_op jit(solution)/shard_map/ppermute | solution.py:361
  16.4 14.5 %collective-permute-start = (bf16[4,16,576]{2,1,0:T(8,128)(2,1)S(1)}, bf16[4,16,576]{2,1,0:T(8,128)(2,1)S(1)}, u32[]{:S(2)}, u32[]{:S(2)}) collective-permute-start(bf16[4,16,576]{2,1,0:T(8,128)(2,1)S(1)} %slice.13), channel_id=1, source_target_pairs={{0,8},{8,16},{16,24},{24,0},{1,9},{9,17},{17,25},{25,1},{2,10},{10... | collective-permute-start | bytes 221192 | tf_op jit(solution)/shard_map/ppermute | solution.py:361
  16.5 17.8 %collective-permute-start.1 = (bf16[4,16,576]{2,1,0:T(8,128)(2,1)S(1)}, bf16[4,16,576]{2,1,0:T(8,128)(2,1)S(1)}, u32[]{:S(2)}, u32[]{:S(2)}) collective-permute-start(bf16[4,16,576]{2,1,0:T(8,128)(2,1)S(1)} %slice.13), channel_id=1, source_target_pairs={{0,16},{8,24},{16,0},{24,8},{1,17},{9,25},{17,1},{25,9},{2,18},{10... | collective-permute-start | bytes 221192 | tf_op jit(solution)/shard_map/ppermute | solution.py:361
  30.9 5.9 %collective-permute-start.2 = (bf16[4,16,576]{2,1,0:T(8,128)(2,1)S(1)}, bf16[4,16,576]{2,1,0:T(8,128)(2,1)S(1)}, u32[]{:S(2)}, u32[]{:S(2)}) collective-permute-start(bf16[4,16,576]{2,1,0:T(8,128)(2,1)S(1)} %slice.13), channel_id=1, source_target_pairs={{0,24},{8,0},{16,8},{24,16},{1,25},{9,1},{17,9},{25,17},{2,26},{10... | collective-permute-start | bytes 221192 | tf_op jit(solution)/shard_map/ppermute | solution.py:361
  34.2 8.1 %collective-permute-start.18 = (bf16[4,4,16,576]{3,2,1,0:T(8,128)(2,1)S(1)}, bf16[4,4,16,576]{3,2,1,0:T(8,128)(2,1)S(1)}, u32[]{:S(2)}, u32[]{:S(2)}) collective-permute-start(bf16[4,4,16,576]{3,2,1,0:T(8,128)(2,1)S(1)} %pad_maximum_fusion.1.q0), channel_id=1, source_target_pairs={{0,24},{8,0},{16,8},{24,16},{1,25},{9,1},{17,9},{25,17},{2,26},{10... | collective-permute-start | bytes 884744 | tf_op jit(solution)/shard_map/ppermute | solution.py:361
  36.9 19.9 %collective-permute-start.3 = (bf16[4,4,16,576]{3,2,1,0:T(8,128)(2,1)S(1)}, bf16[4,4,16,576]{3,2,1,0:T(8,128)(2,1)S(1)}, u32[]{:S(2)}, u32[]{:S(2)}) collective-permute-start(bf16[4,4,16,576]{3,2,1,0:T(8,128)(2,1)S(1)} %pad_maximum_fusion.q0), channel_id=1, source_target_pairs={{0,2},{2,4},{4,6},{6,0},{1,3},{3,5},{5,7},{7,1},{8,10},{10,12},{12... | collective-permute-start | bytes 884744 | tf_op jit(solution)/shard_map/ppermute | solution.py:361
  38.2 19.6 %collective-permute-start.4 = (bf16[4,4,16,576]{3,2,1,0:T(8,128)(2,1)S(1)}, bf16[4,4,16,576]{3,2,1,0:T(8,128)(2,1)S(1)}, u32[]{:S(2)}, u32[]{:S(2)}) collective-permute-start(bf16[4,4,16,576]{3,2,1,0:T(8,128)(2,1)S(1)} %pad_maximum_fusion.q0), channel_id=1, source_target_pairs={{0,4},{2,6},{4,0},{6,2},{1,5},{3,7},{5,1},{7,3},{8,12},{10,14},{12... | collective-permute-start | bytes 884744 | tf_op jit(solution)/shard_map/ppermute | solution.py:361
  40.2 17.6 %collective-permute-start.5 = (bf16[4,4,16,576]{3,2,1,0:T(8,128)(2,1)S(1)}, bf16[4,4,16,576]{3,2,1,0:T(8,128)(2,1)S(1)}, u32[]{:S(2)}, u32[]{:S(2)}) collective-permute-start(bf16[4,4,16,576]{3,2,1,0:T(8,128)(2,1)S(1)} %pad_maximum_fusion.q0), channel_id=1, source_target_pairs={{0,6},{2,0},{4,2},{6,4},{1,7},{3,1},{5,3},{7,5},{8,14},{10,8},{12,... | collective-permute-start | bytes 884744 | tf_op jit(solution)/shard_map/ppermute | solution.py:361
  42.4 0.7 copy-start.3
  53.8 17.5 %collective-permute-start.19 = (bf16[4,17,16,128]{3,2,1,0:T(8,128)(2,1)S(1)}, bf16[4,17,16,128]{3,2,1,0:T(8,128)(2,1)S(1)}, u32[]{:S(2)}, u32[]{:S(2)}) collective-permute-start(bf16[4,17,16,128]{3,2,1,0:T(8,128)(2,1)S(1)} %get-tuple-element.34), channel_id=1, source_target_pairs={{0,24},{8,0},{16,8},{24,16},{1,25},{9,1},{17,9},{25,17},{2,26},{10... | collective-permute-start | bytes 835592 | tf_op jit(solution)/shard_map/ppermute | solution.py:361
  56.7 14.9 %collective-permute-start.20 = (bf16[4,17,16,128]{3,2,1,0:T(8,128)(2,1)S(1)}, bf16[4,17,16,128]{3,2,1,0:T(8,128)(2,1)S(1)}, u32[]{:S(2)}, u32[]{:S(2)}) collective-permute-start(bf16[4,17,16,128]{3,2,1,0:T(8,128)(2,1)S(1)} %get-tuple-element.35), channel_id=1, source_target_pairs={{0,16},{8,24},{16,0},{24,8},{1,17},{9,25},{17,1},{25,9},{2,18},{10... | collective-permute-start | bytes 835592 | tf_op jit(solution)/shard_map/ppermute | solution.py:361
  56.7 31.9 %copy-start.4 = (bf16[32,4,576]{2,1,0:T(4,128)(2,1)S(1)}, bf16[32,4,576]{2,1,0:T(4,128)(2,1)}, u32[]{:S(2)}) copy-start(bf16[32,4,576]{2,1,0:T(4,128)(2,1)} %param.13) | copy-start | bytes 442372
  56.7 37.4 %copy-start = (bf16[4,512,128]{2,1,0:T(8,128)(2,1)S(1)}, bf16[4,512,128]{2,1,0:T(8,128)(2,1)}, u32[]{:S(2)}) copy-start(bf16[4,512,128]{2,1,0:T(8,128)(2,1)} %refs_10_.1) | copy-start | bytes 1572868
  56.7 37.4 %copy-start.2 = (bf16[32,576]{1,0:T(8,128)(2,1)S(1)}, bf16[32,576]{1,0:T(8,128)(2,1)}, u32[]{:S(2)}) copy-start(bf16[32,576]{1,0:T(8,128)(2,1)} %refs_9_.1) | copy-start | bytes 110596
  56.8 14.8 %collective-permute-start.21 = (bf16[4,17,16,128]{3,2,1,0:T(8,128)(2,1)S(1)}, bf16[4,17,16,128]{3,2,1,0:T(8,128)(2,1)S(1)}, u32[]{:S(2)}, u32[]{:S(2)}) collective-permute-start(bf16[4,17,16,128]{3,2,1,0:T(8,128)(2,1)S(1)} %get-tuple-element.36), channel_id=1, source_target_pairs={{0,8},{8,16},{16,24},{24,0},{1,9},{9,17},{17,25},{25,1},{2,10},{10... | collective-permute-start | bytes 835592 | tf_op jit(solution)/shard_map/ppermute | solution.py:361
  68.5 9.3 %collective-permute-start.7 = (bf16[4,17,16,128]{3,2,1,0:T(8,128)(2,1)S(1)}, bf16[4,17,16,128]{3,2,1,0:T(8,128)(2,1)S(1)}, u32[]{:S(2)}, u32[]{:S(2)}) collective-permute-start(bf16[4,17,16,128]{3,2,1,0:T(8,128)(2,1)S(1)} %get-tuple-element.26), channel_id=1, source_target_pairs={{0,6},{2,0},{4,2},{6,4},{1,7},{3,1},{5,3},{7,5},{8,14},{10,8},{12,... | collective-permute-start | bytes 835592 | tf_op jit(solution)/shard_map/ppermute | solution.py:361
  69.6 12.4 %collective-permute-start.8 = (bf16[4,17,16,128]{3,2,1,0:T(8,128)(2,1)S(1)}, bf16[4,17,16,128]{3,2,1,0:T(8,128)(2,1)S(1)}, u32[]{:S(2)}, u32[]{:S(2)}) collective-permute-start(bf16[4,17,16,128]{3,2,1,0:T(8,128)(2,1)S(1)} %get-tuple-element.27), channel_id=1, source_target_pairs={{0,4},{2,6},{4,0},{6,2},{1,5},{3,7},{5,1},{7,3},{8,12},{10,14},{12... | collective-permute-start | bytes 835592 | tf_op jit(solution)/shard_map/ppermute | solution.py:361
  71.3 12.1 %collective-permute-start.9 = (bf16[4,17,16,128]{3,2,1,0:T(8,128)(2,1)S(1)}, bf16[4,17,16,128]{3,2,1,0:T(8,128)(2,1)S(1)}, u32[]{:S(2)}, u32[]{:S(2)}) collective-permute-start(bf16[4,17,16,128]{3,2,1,0:T(8,128)(2,1)S(1)} %get-tuple-element.28), channel_id=1, source_target_pairs={{0,2},{2,4},{4,6},{6,0},{1,3},{3,5},{5,7},{7,1},{8,10},{10,12},{12... | collective-permute-start | bytes 835592 | tf_op jit(solution)/shard_map/ppermute | solution.py:361
  72.4 16.2 %collective-permute-start.22 = (bf16[17,16,128]{2,1,0:T(8,128)(2,1)S(1)}, bf16[17,16,128]{2,1,0:T(8,128)(2,1)S(1)}, u32[]{:S(2)}, u32[]{:S(2)}) collective-permute-start(bf16[17,16,128]{2,1,0:T(8,128)(2,1)S(1)} %get-tuple-element.38), channel_id=1, source_target_pairs={{0,6},{2,0},{4,2},{6,4},{1,7},{3,1},{5,3},{7,5},{8,14},{10,8},{12,... | collective-permute-start | bytes 208904 | tf_op jit(solution)/shard_map/ppermute | solution.py:361
  75.5 13.3 %collective-permute-start.23 = (bf16[17,16,128]{2,1,0:T(8,128)(2,1)S(1)}, bf16[17,16,128]{2,1,0:T(8,128)(2,1)S(1)}, u32[]{:S(2)}, u32[]{:S(2)}) collective-permute-start(bf16[17,16,128]{2,1,0:T(8,128)(2,1)S(1)} %get-tuple-element.39), channel_id=1, source_target_pairs={{0,4},{2,6},{4,0},{6,2},{1,5},{3,7},{5,1},{7,3},{8,12},{10,14},{12... | collective-permute-start | bytes 208904 | tf_op jit(solution)/shard_map/ppermute | solution.py:361
  77.8 10.9 %collective-permute-start.24 = (bf16[17,16,128]{2,1,0:T(8,128)(2,1)S(1)}, bf16[17,16,128]{2,1,0:T(8,128)(2,1)S(1)}, u32[]{:S(2)}, u32[]{:S(2)}) collective-permute-start(bf16[17,16,128]{2,1,0:T(8,128)(2,1)S(1)} %get-tuple-element.40), channel_id=1, source_target_pairs={{0,2},{2,4},{4,6},{6,0},{1,3},{3,5},{5,7},{7,1},{8,10},{10,12},{12... | collective-permute-start | bytes 208904 | tf_op jit(solution)/shard_map/ppermute | solution.py:361
  84.2 4.6 %collective-permute-start.10 = (bf16[17,16,128]{2,1,0:T(8,128)(2,1)S(1)}, bf16[17,16,128]{2,1,0:T(8,128)(2,1)S(1)}, u32[]{:S(2)}, u32[]{:S(2)}) collective-permute-start(bf16[17,16,128]{2,1,0:T(8,128)(2,1)S(1)} %get-tuple-element.30), channel_id=1, source_target_pairs={{0,24},{8,0},{16,8},{24,16},{1,25},{9,1},{17,9},{25,17},{2,26},{10... | collective-permute-start | bytes 208904 | tf_op jit(solution)/shard_map/ppermute | solution.py:361
  86.6 5.8 %collective-permute-start.11 = (bf16[17,16,128]{2,1,0:T(8,128)(2,1)S(1)}, bf16[17,16,128]{2,1,0:T(8,128)(2,1)S(1)}, u32[]{:S(2)}, u32[]{:S(2)}) collective-permute-start(bf16[17,16,128]{2,1,0:T(8,128)(2,1)S(1)} %get-tuple-element.31), channel_id=1, source_target_pairs={{0,16},{8,24},{16,0},{24,8},{1,17},{9,25},{17,1},{25,9},{2,18},{10... | collective-permute-start | bytes 208904 | tf_op jit(solution)/shard_map/ppermute | solution.py:361
  88.6 5.5 %collective-permute-start.12 = (bf16[17,16,128]{2,1,0:T(8,128)(2,1)S(1)}, bf16[17,16,128]{2,1,0:T(8,128)(2,1)S(1)}, u32[]{:S(2)}, u32[]{:S(2)}) collective-permute-start(bf16[17,16,128]{2,1,0:T(8,128)(2,1)S(1)} %get-tuple-element.32), channel_id=1, source_target_pairs={{0,8},{8,16},{16,24},{24,0},{1,9},{9,17},{17,25},{25,1},{2,10},{10... | collective-permute-start | bytes 208904 | tf_op jit(solution)/shard_map/ppermute | solution.py:361
  94.2 4.9 %copy-start.6 = (bf16[1,7168]{1,0:T(2,128)(2,1)S(1)}, bf16[1,7168]{1,0:T(2,128)(2,1)}, u32[]{:S(2)}) copy-start(bf16[1,7168]{1,0:T(2,128)(2,1)} %param.19) | copy-start | bytes 43012
  94.2 5.0 %copy-start.5 = (f32[7168]{0:T(1024)S(1)}, f32[7168]{0:T(1024)}, u32[]{:S(2)}) copy-start(f32[7168]{0:T(1024)} %param.20) | copy-start | bytes 86020
  94.2 10.7 %copy-start.7 = (s32[1,8]{1,0:T(1,128)S(1)}, s32[1,8]{1,0:T(1,128)}, u32[]{:S(2)}) copy-start(s32[1,8]{1,0:T(1,128)} %param.22) | copy-start | bytes 100
  98.9 42.5 %copy-start.1 = (bf16[7168,16]{0,1:T(8,128)(2,1)S(1)}, bf16[7168,16]{0,1:T(8,128)(2,1)}, u32[]{:S(2)}) copy-start(bf16[7168,16]{0,1:T(8,128)(2,1)} %param.21) | copy-start | bytes 688132
  98.9 1.6 collective-permute-start.25
  101.3 12.2 %all-to-all-start = ((bf16[16,8,896]{2,1,0:T(8,128)(2,1)}), bf16[16,8,896]{2,1,0:T(8,128)(2,1)S(1)}, u32[]{:S(2)}, u32[]{:S(2)}) async-start(bf16[16,8,896]{2,1,0:T(8,128)(2,1)} %add_convert_fusion.1), calls=%async_computation | async-start | bytes 458752 | tf_op jit(solution)/shard_map/all_to_all | solution.py:409
  138.7 2.7 %collective-permute-start.26 = (bf16[64,8,1024]{2,1,0:T(8,128)(2,1)S(1)}, bf16[64,8,1024]{2,1,0:T(8,128)(2,1)S(1)}, u32[]{:S(2)}, u32[]{:S(2)}) collective-permute-start(bf16[64,8,1024]{2,1,0:T(8,128)(2,1)S(1)} %all_to_all.15.own_ref), channel_id=1, source_target_pairs={{0,1},{1,0},{2,3},{3,2},{4,5},{5,4},{6,7},{7,6},{8,9},{9,8},{10,11... | collective-permute-start | bytes 3145736 | tf_op jit(solution)/shard_map/ppermute | solution.py:361
  149.6 2.6 %collective-permute-start.27 = (bf16[64,8,896]{2,1,0:T(8,128)(2,1)S(1)}, bf16[64,8,896]{2,1,0:T(8,128)(2,1)S(1)}, u32[]{:S(2)}, u32[]{:S(2)}) collective-permute-start(bf16[64,8,896]{2,1,0:T(8,128)(2,1)S(1)} %get-tuple-element.47), channel_id=1, source_target_pairs={{0,1},{1,0},{2,3},{3,2},{4,5},{5,4},{6,7},{7,6},{8,9},{9,8},{10,11... | collective-permute-start | bytes 2752520 | tf_op jit(solution)/shard_map/ppermute | solution.py:361
  153.3 22.6 %all-to-all-start.2 = ((bf16[64,8,896]{2,1,0:T(8,128)(2,1)}), bf16[64,8,896]{2,1,0:T(8,128)(2,1)S(1)}, u32[]{:S(2)}, u32[]{:S(2)}) async-start(bf16[64,8,896]{2,1,0:T(8,128)(2,1)} %add_convert_fusion), calls=%async_computation.2 | async-start | bytes 1835008 | tf_op jit(solution)/shard_map/all_to_all | solution.py:424

commit v2 on v1

--- a/solution.py
+++ b/solution.py
@@ -245,7 +245,7 @@
     )(core, *first, *second, own_query, new_keys, value_up, pltpu.with_memory_space_constraint(w_out, pltpu.HBM))
 
 
-def spread_kernel(arrived_ref, residual_ref, gain_ref, chosen_ref, attn_ref, stream_ref, rows_ref):
+def spread_kernel(arrived_ref, residual_ref, gain_ref, attn_ref, stream_ref, normed_ref, rows_ref):
     attention = jnp.sum(arrived_ref[...].astype(f32), axis=0)
     attn_ref[...] = attention.astype(bf16)
     stream = (residual_ref[...].astype(f32) + attention).astype(bf16)
@@ -254,24 +254,24 @@
     square = jnp.sum(jnp.sum(wide * wide, axis=1, keepdims=True), axis=0, keepdims=True)
     mean_square = square / (wide.shape[0] * wide.shape[1])
     normed = (wide * lax.rsqrt(mean_square + norm_eps) * gain_ref[...]).astype(bf16)
-    row = jnp.concatenate([normed, chosen_ref[...]], axis=1)
-    rows_ref[...] = jnp.broadcast_to(row[None], rows_ref.shape)
-
-
-def spread(arrived, residual, gain, chosen, chips):
+    normed_ref[...] = normed
+    rows_ref[...] = jnp.broadcast_to(normed[None], rows_ref.shape)
+
+
+def spread(arrived, residual, gain, chips):
     one = jax.ShapeDtypeStruct(residual.shape, bf16)
-    rows = jax.ShapeDtypeStruct((chips, SPAN, residual.shape[1] + LANES), bf16)
+    rows = jax.ShapeDtypeStruct((chips,) + residual.shape, bf16)
     return pl.pallas_call(
         spread_kernel,
-        out_shape=[one, one, rows],
+        out_shape=[one, one, one, rows],
         compiler_params=pltpu.CompilerParams(vmem_limit_bytes=32 << 20),
         name="spread",
-    )(arrived, residual, gain, chosen)
+    )(arrived, residual, gain)
 
 
 def experts_kernel(
-    expert_ref, own_ref, sib_ref, router_ref, gate_hbm, up_hbm, down_hbm, out_own, out_sib,
-    gate_ref, up_ref, down_ref, rows_ref, sems
+    routes_ref, own_ref, sib_ref, normed_ref, router_ref, gate_hbm, up_hbm, down_hbm,
+    out_own, out_sib, coefficient_ref, gate_ref, up_ref, down_ref, rows_ref, sems
 ):
     half = own_ref.shape[0]
     rows = 2 * half
@@ -294,37 +294,29 @@
         window = slice(piece * LANES, (piece + 1) * LANES)
         rows_ref[piece, : half * SPAN] = own_ref[:, :, window].astype(f32).reshape(half * SPAN, LANES)
         rows_ref[piece, half * SPAN :] = sib_ref[:, :, window].astype(f32).reshape(half * SPAN, LANES)
-    gate = up = values = 0.0
+    products = router_ref[...].astype(f32) * normed_ref[...].astype(f32)[None]
+    values = jnp.sum(jnp.sum(products, axis=2, keepdims=True), axis=1, keepdims=True)
+    values = 1.0 / (1.0 + jnp.exp(-values))
+    index = lax.broadcasted_iota(jnp.int32, values.shape, 0)
+    chosen = jnp.zeros(values.shape, f32)
+    for k in range(routes_ref.shape[1]):
+        chosen = jnp.where(index == routes_ref[0, k], 1.0, chosen)
+    picked = values * chosen
+    share = route_scale * picked / jnp.sum(picked, axis=0, keepdims=True)
+    coefficient_ref[...] = jnp.broadcast_to(share, coefficient_ref.shape)
+    gate = up = 0.0
     for k in range(SPAN):
         block = jnp.concatenate(
             [rows_ref[piece, pl.ds(k, rows, stride=SPAN), :] for piece in range(tiles)], axis=1
         ).astype(bf16)
-        values = values + lax.dot_general(
-            block,
-            router_ref[:, k * chunk : (k + 1) * chunk],
-            (((1,), (1,)), ((), ())),
-            preferred_element_type=f32,
-        )
         fetch(0, k).wait()
         gate = gate + jnp.dot(block, gate_ref[k * chunk : (k + 1) * chunk], preferred_element_type=f32)
         fetch(1, k).wait()
         up = up + jnp.dot(block, up_ref[k * chunk : (k + 1) * chunk], preferred_element_type=f32)
     hidden = (gate / (1.0 + jnp.exp(-gate)) * up).astype(bf16)
-    values = 1.0 / (1.0 + jnp.exp(-values))
-    chosen = jnp.concatenate(
-        [ref[:, :, chunk:].astype(f32).reshape(half * SPAN, LANES) for ref in (own_ref, sib_ref)], axis=0
-    )
-    rows_ref[0] = chosen
-    chosen = rows_ref[0, pl.ds(0, rows, stride=SPAN), :][:, :EXPERTS]
-    picked = values * chosen
-    lane = lax.broadcasted_iota(jnp.int32, picked.shape, 1)
-    mine = jnp.sum(jnp.where(lane == expert_ref[0], picked, 0.0), axis=-1, keepdims=True)
-    share = route_scale * mine / jnp.sum(picked, axis=-1, keepdims=True)
     for k in range(SPAN):
         fetch(2, k).wait()
-        result = share * jnp.dot(
-            hidden, down_ref[:, k * chunk : (k + 1) * chunk], preferred_element_type=f32
-        )
+        result = jnp.dot(hidden, down_ref[:, k * chunk : (k + 1) * chunk], preferred_element_type=f32)
         for piece in range(tiles):
             rows_ref[piece, pl.ds(k, rows, stride=SPAN), :] = result[:, piece * LANES : (piece + 1) * LANES]
     for piece in range(tiles):
@@ -333,27 +325,47 @@
         out_sib[:, :, window] = rows_ref[piece, half * SPAN :].reshape(half, SPAN, LANES).astype(bf16)
 
 
-def experts(expert, own_rows, sibling_rows, w_gate, w_up, w_router, w_down):
-    width = w_gate.shape[0]
-    half = own_rows.shape[0]
-    out = jax.ShapeDtypeStruct((half, SPAN, width // SPAN), bf16)
+def experts(routes, own_rows, sibling_rows, normed, w_router, w_gate, w_up, w_down):
+    out = jax.ShapeDtypeStruct(own_rows.shape, bf16)
     inside = pl.BlockSpec(memory_space=pltpu.VMEM)
     outside = pl.BlockSpec(memory_space=pltpu.HBM)
+    half, span, chunk = own_rows.shape
+    weights = [pltpu.with_memory_space_constraint(w, pltpu.HBM) for w in (w_gate, w_up, w_down)]
     return pl.pallas_call(
         experts_kernel,
-        out_shape=[out, out],
-        in_specs=[pl.BlockSpec(memory_space=pltpu.SMEM)] + [inside] * 3 + [outside] * 3,
-        out_specs=[inside] * 2,
+        out_shape=[out, out, jax.ShapeDtypeStruct((EXPERTS, span, LANES), f32)],
+        in_specs=[pl.BlockSpec(memory_space=pltpu.SMEM)] + [inside] * 4 + [outside] * 3,
+        out_specs=[inside] * 3,
         scratch_shapes=[
             pltpu.VMEM(w_gate.shape, bf16),
             pltpu.VMEM(w_up.shape, bf16),
             pltpu.VMEM(w_down.shape, bf16),
-            pltpu.VMEM((width // SPAN // LANES, 2 * half * SPAN, LANES), f32),
-            pltpu.SemaphoreType.DMA((3, SPAN)),
+            pltpu.VMEM((chunk // LANES, 2 * half * span, LANES), f32),
+            pltpu.SemaphoreType.DMA((3, span)),
         ],
         compiler_params=pltpu.CompilerParams(vmem_limit_bytes=48 << 20),
         name="experts",
-    )(expert, own_rows, sibling_rows, w_router.T, w_gate, w_up, w_down)
+    )(routes, own_rows, sibling_rows, normed, w_router.T.reshape(EXPERTS, span, chunk), *weights)
+
+
+def gather_kernel(returned_ref, stream_ref, coefficient_ref, out_ref):
+    slices = returned_ref.shape[0] // EXPERTS
+    for piece in range(stream_ref.shape[1] // LANES):
+        window = slice(piece * LANES, (piece + 1) * LANES)
+        total = jnp.zeros((SPAN, LANES), f32)
+        for expert in range(EXPERTS):
+            part = returned_ref[expert * slices : (expert + 1) * slices, :, window].astype(f32)
+            total = total + coefficient_ref[expert] * jnp.sum(part, axis=0)
+        out_ref[:, window] = (stream_ref[:, window].astype(f32) + total).astype(bf16)
+
+
+def gather(returned, stream, coefficient):
+    return pl.pallas_call(
+        gather_kernel,
+        out_shape=jax.ShapeDtypeStruct(stream.shape, bf16),
+        compiler_params=pltpu.CompilerParams(vmem_limit_bytes=32 << 20),
+        name="gather",
+    )(returned, stream, coefficient)
 
 
 def shift_by(value, axis, offset):
@@ -384,7 +396,7 @@
     w_up,
     w_down,
 ):
-    y, x, z, core = (lax.axis_index(name) for name in ("y", "x", "z", "c"))
+    x, z, core = (lax.axis_index(name) for name in ("x", "z", "c"))
     ctx = (x * lax.axis_size("z") + z) * 2 + core
     requests = lengths.shape[0]
     features = query.shape[-1]
@@ -395,6 +407,7 @@
     own_query = query.reshape(requests, -1, features)
     stack_x = jnp.stack(all_shifts(own_query[:count], "x"))
     stack_z = jnp.stack(all_shifts(own_query[count:], "z"))
+    stack_x, stack_z = lax.optimization_barrier((stack_x, stack_z))
     queries_a = all_shifts(stack_x, "z")
     queries_b = all_shifts(stack_z, "x")
     blocks = jnp.stack([ctx, ctx ^ 1]).astype(jnp.int32)
@@ -407,22 +420,18 @@
     )
     chip_sum = (kept.astype(f32) + shift_by(given, "c", 1).astype(f32)).astype(bf16)
     arrived = lax.all_to_all(chip_sum, ("x", "z"), split_axis=0, concat_axis=0, tiled=True)
-    lanes = jnp.arange(LANES, dtype=jnp.int32)
-    chosen = jnp.any(routes[:, :, None] == lanes[None, None, :], axis=1).astype(bf16)
-    chosen = jnp.pad(chosen, ((0, SPAN - 1), (0, 0)))
     chips = lax.axis_size("y") * lax.axis_size("x") * lax.axis_size("z")
-    attn_out, stream, rows = spread(
-        arrived, residual.reshape(SPAN, -1), norm_gain.reshape(SPAN, -1), chosen, chips
+    attn_out, stream, normed, rows = spread(
+        arrived, residual.reshape(SPAN, -1), norm_gain.reshape(SPAN, -1), chips
     )
     own_rows = lax.all_to_all(rows, ("y", "x", "z"), split_axis=0, concat_axis=0, tiled=True)
     sibling_rows = shift_by(own_rows, "c", 1)
-    devices = 2 * chips
-    flat = y * (devices // lax.axis_size("y")) + ctx
-    expert = (flat // (devices // EXPERTS)).astype(jnp.int32).reshape(1)
-    out_own, out_sibling = experts(expert, own_rows, sibling_rows, w_gate, w_up, w_router, w_down)
+    out_own, out_sibling, coefficient = experts(
+        routes, own_rows, sibling_rows, normed, w_router, w_gate, w_up, w_down
+    )
     chip_out = (out_own.astype(f32) + shift_by(out_sibling, "c", 1).astype(f32)).astype(bf16)
     returned = lax.all_to_all(chip_out, ("y", "x", "z"), split_axis=0, concat_axis=0, tiled=True)
-    layer_out = (stream.astype(f32) + jnp.sum(returned.astype(f32), axis=0)).astype(bf16)
+    layer_out = gather(returned, stream, coefficient)
     return (attn_out.reshape(1, width), layer_out.reshape(1, width))
 
 

time: 177 us -> 170 us (0.960)
  waiting for transfers between devices: 58.9 us -> 54.4 us
    ppermute x28, waiting for transfers between devices: 33.1 us -> 28.6 us  [shift_by(): lax.ppermute(value, axis, [(i, (i + offset) % size) for i in range(size)])]
    pallas_call x2 -> x3, Pallas kernels: 8.36 us -> 8.44 us  [the longest x1 8.09 us: experts(): pl.pallas_call(experts_kernel, out_shape=[out, out, jax.ShapeDtypeStruct(...]
  transfers between devices with their start and end apart: 30 -> 30, of which waited for: 16 -> 15; matrix products, arithmetic and copies ran while one was open for 1% -> 1% of each run, Pallas kernels for 13% -> 14%
where the time goes in v2:
time: 170 us
  waiting for transfers between devices  54.4 us (32%)
  starting transfers between devices  49.3 us (29%)
  Pallas kernels  36.3 us (21%)
  blocking collectives  23.8 us (14%)
  local copies, waits for them, and re-layouts  3.26 us (2%)
  other arithmetic  2.19 us (1%)
    ppermute x28, starting transfers between devices, shift_by(): lax.ppermute(value, axis, [(i, (i + offset) % size) for i in range(size)])  41.1 us
    ppermute x28, waiting for transfers between devices, shift_by(): lax.ppermute(value, axis, [(i, (i + offset) % size) for i in range(size)])  28.6 us
    all_to_all x1, blocking collectives, local(): lax.all_to_all(rows, ('y', 'x', 'z'), split_axis=0, concat_axis=0, tiled=...  23.8 us
    pallas_call x2, Pallas kernels, attend(): pl.pallas_call(functools.partial(attend_kernel, first=first, count=count)...  21.4 us
    all_to_all x1, waiting for transfers between devices, local(): lax.all_to_all(chip_out, ('y', 'x', 'z'), split_axis=0, concat_axis=0, ti...  17.3 us
    all_to_all x1, waiting for transfers between devices, local(): lax.all_to_all(chip_sum, ('x', 'z'), split_axis=0, concat_axis=0, tiled=T...  8.53 us
    pallas_call x1, Pallas kernels, experts(): pl.pallas_call(experts_kernel, out_shape=[out, out, jax.ShapeDtypeStruct(...  8.09 us
    pallas_call x1, Pallas kernels, project(): pl.pallas_call(functools.partial(project_kernel, count=count), out_shape=...  4.74 us
  transfers between devices with their start and end apart: 30, of which 15 were waited for; matrix products, arithmetic and copies ran while one was open for 1% of the time, Pallas kernels for 14%

profile of v2, /device:TPU:0, one launch (start us, length us, event | category | flops | bytes accessed | tf_op | source)
XLA Modules:
  0.0 170.0 jit_solution(17044930533945978517)
XLA Ops:
  0.6 0.1 collective-permute-start.9
  0.7 1.0 fusion
  1.8 2.1 %collective-permute-start.3 = (bf16[4,16,576]{2,1,0:T(8,128)(2,1)S(1)}, bf16[4,16,576]{2,1,0:T(8,128)(2,1)S(1)}, u32[]{:S(2)}, u32[]{:S(2)}) collective-permute-start(bf16[4,16,576]{2,1,0:T(8,128)(2,1)S(1)} %slice.15), channel_id=1, source_target_pairs={{0,2},{2,4},{4,6},{6,0},{1,3},{3,5},{5,7},{7,1},{8,10},{10,12},{12... | collective-permute-start | bytes 221192 | tf_op jit(solution)/shard_map/ppermute | solution.py:373
  3.8 3.6 %collective-permute-start.4 = (bf16[4,16,576]{2,1,0:T(8,128)(2,1)S(1)}, bf16[4,16,576]{2,1,0:T(8,128)(2,1)S(1)}, u32[]{:S(2)}, u32[]{:S(2)}) collective-permute-start(bf16[4,16,576]{2,1,0:T(8,128)(2,1)S(1)} %slice.15), channel_id=1, source_target_pairs={{0,4},{2,6},{4,0},{6,2},{1,5},{3,7},{5,1},{7,3},{8,12},{10,14},{12... | collective-permute-start | bytes 221192 | tf_op jit(solution)/shard_map/ppermute | solution.py:373
  7.4 1.0 collective-permute-start.5
  8.5 1.6 collective-permute-start
  10.1 2.8 %collective-permute-start.1 = (bf16[4,16,576]{2,1,0:T(8,128)(2,1)S(1)}, bf16[4,16,576]{2,1,0:T(8,128)(2,1)S(1)}, u32[]{:S(2)}, u32[]{:S(2)}) collective-permute-start(bf16[4,16,576]{2,1,0:T(8,128)(2,1)S(1)} %slice.13), channel_id=1, source_target_pairs={{0,16},{8,24},{16,0},{24,8},{1,17},{9,25},{17,1},{25,9},{2,18},{10... | collective-permute-start | bytes 221192 | tf_op jit(solution)/shard_map/ppermute | solution.py:373
  12.9 1.8 %collective-permute-start.2 = (bf16[4,16,576]{2,1,0:T(8,128)(2,1)S(1)}, bf16[4,16,576]{2,1,0:T(8,128)(2,1)S(1)}, u32[]{:S(2)}, u32[]{:S(2)}) collective-permute-start(bf16[4,16,576]{2,1,0:T(8,128)(2,1)S(1)} %slice.13), channel_id=1, source_target_pairs={{0,24},{8,0},{16,8},{24,16},{1,25},{9,1},{17,9},{25,17},{2,26},{10... | collective-permute-start | bytes 221192 | tf_op jit(solution)/shard_map/ppermute | solution.py:373
  14.7 0.1 pad_maximum_fusion.1.q0
  14.8 0.2 collective-permute-done
  15.0 1.5 collective-permute-done.1
  16.5 0.9 collective-permute-done.2
  17.4 0.1 pad_maximum_fusion.q0
  17.4 1.4 collective-permute-start.16
  18.8 3.2 %collective-permute-start.17 = (bf16[4,4,16,576]{3,2,1,0:T(8,128)(2,1)S(1)}, bf16[4,4,16,576]{3,2,1,0:T(8,128)(2,1)S(1)}, u32[]{:S(2)}, u32[]{:S(2)}) collective-permute-start(bf16[4,4,16,576]{3,2,1,0:T(8,128)(2,1)S(1)} %pad_maximum_fusion.1.q0), channel_id=1, source_target_pairs={{0,16},{8,24},{16,0},{24,8},{1,17},{9,25},{17,1},{25,9},{2,18},{10... | collective-permute-start | bytes 884744 | tf_op jit(solution)/shard_map/ppermute | solution.py:373
  22.0 0.7 collective-permute-start.18
  22.7 0.4 collective-permute-start.6
  23.1 5.4 %collective-permute-done.16.q1 = bf16[4,4,16,576]{3,2,1,0:T(8,128)(2,1)S(1)} collective-permute-done((bf16[4,4,16,576]{3,2,1,0:T(8,128)(2,1)S(1)}, bf16[4,4,16,576]{3,2,1,0:T(8,128)(2,1)S(1)}, u32[]{:S(2)}, u32[]{:S(2)}) %collective-permute-start.16) | collective-permute-done | bytes 294944 | tf_op jit(solution)/shard_map/ppermute | solution.py:373
  28.4 1.3 collective-permute-start.7
  29.8 5.5 %collective-permute-done.17.q2 = bf16[4,4,16,576]{3,2,1,0:T(8,128)(2,1)S(1)} collective-permute-done((bf16[4,4,16,576]{3,2,1,0:T(8,128)(2,1)S(1)}, bf16[4,4,16,576]{3,2,1,0:T(8,128)(2,1)S(1)}, u32[]{:S(2)}, u32[]{:S(2)}) %collective-permute-start.17) | collective-permute-done | bytes 294944 | tf_op jit(solution)/shard_map/ppermute | solution.py:373
  35.3 1.5 collective-permute-start.8
  36.8 0.1 pad_add_fusion.blocks_ref
  36.9 0.7 copy-done.2
  37.5 10.7 %attend.3 = (bf16[4,17,16,128]{3,2,1,0:T(8,128)(2,1)S(1)}, bf16[4,17,16,128]{3,2,1,0:T(8,128)(2,1)S(1)}, bf16[4,17,16,128]{3,2,1,0:T(8,128)(2,1)S(1)}, bf16[4,17,16,128]{3,2,1,0:T(8,128)(2,1)S(1)}) custom-call(s32[2]{0:T(128)S(1)} %pad_add_fusion.blocks_ref, s32[8]{0:T(128)S(1)} %copy-done.2, bf16[4,4,16,576]{3,2,1,0:T(8,128)(2,1)S(1)} %pad_maximum_fusion.1.q0, ...), custom_call_target="tpu_custom_call" | custom-call | tf_op jit(solution)/shard_map/attend/pallas_call | solution.py:96
  48.3 0.7 collective-permute-start.19
  48.9 1.1 collective-permute-start.20
  50.1 0.5 collective-permute-start.21
  50.6 10.7 %attend.2 = (bf16[4,17,16,128]{3,2,1,0:T(8,128)(2,1)S(1)}, bf16[4,17,16,128]{3,2,1,0:T(8,128)(2,1)S(1)}, bf16[4,17,16,128]{3,2,1,0:T(8,128)(2,1)S(1)}, bf16[4,17,16,128]{3,2,1,0:T(8,128)(2,1)S(1)}) custom-call(s32[2]{0:T(128)S(1)} %pad_add_fusion.blocks_ref, s32[8]{0:T(128)S(1)} %copy-done.2, bf16[4,4,16,576]{3,2,1,0:T(8,128)(2,1)S(1)} %pad_maximum_fusion.q0, ...), custom_call_target="tpu_custom_call" | custom-call | tf_op jit(solution)/shard_map/attend/pallas_call | solution.py:96
  61.3 2.4 %collective-permute-start.10 = (bf16[4,17,16,128]{3,2,1,0:T(8,128)(2,1)S(1)}, bf16[4,17,16,128]{3,2,1,0:T(8,128)(2,1)S(1)}, u32[]{:S(2)}, u32[]{:S(2)}) collective-permute-start(bf16[4,17,16,128]{3,2,1,0:T(8,128)(2,1)S(1)} %get-tuple-element.31), channel_id=1, source_target_pairs={{0,6},{2,0},{4,2},{6,4},{1,7},{3,1},{5,3},{7,5},{8,14},{10,8},{12,... | collective-permute-start | bytes 835592 | tf_op jit(solution)/shard_map/ppermute | solution.py:373
  63.7 0.1 collective-permute-start.11
  63.8 0.8 collective-permute-start.12
  64.7 0.8 merge.3
  65.5 2.4 %collective-permute-start.22 = (bf16[17,16,128]{2,1,0:T(8,128)(2,1)S(1)}, bf16[17,16,128]{2,1,0:T(8,128)(2,1)S(1)}, u32[]{:S(2)}, u32[]{:S(2)}) collective-permute-start(bf16[17,16,128]{2,1,0:T(8,128)(2,1)S(1)} %get-tuple-element.44), channel_id=1, source_target_pairs={{0,6},{2,0},{4,2},{6,4},{1,7},{3,1},{5,3},{7,5},{8,14},{10,8},{12,... | collective-permute-start | bytes 208904 | tf_op jit(solution)/shard_map/ppermute | solution.py:373
  68.0 2.2 %collective-permute-start.23 = (bf16[17,16,128]{2,1,0:T(8,128)(2,1)S(1)}, bf16[17,16,128]{2,1,0:T(8,128)(2,1)S(1)}, u32[]{:S(2)}, u32[]{:S(2)}) collective-permute-start(bf16[17,16,128]{2,1,0:T(8,128)(2,1)S(1)} %get-tuple-element.45), channel_id=1, source_target_pairs={{0,4},{2,6},{4,0},{6,2},{1,5},{3,7},{5,1},{7,3},{8,12},{10,14},{12... | collective-permute-start | bytes 208904 | tf_op jit(solution)/shard_map/ppermute | solution.py:373
  70.2 2.7 %collective-permute-done.10.a1 = bf16[4,17,16,128]{3,2,1,0:T(8,128)(2,1)S(1)} collective-permute-done((bf16[4,17,16,128]{3,2,1,0:T(8,128)(2,1)S(1)}, bf16[4,17,16,128]{3,2,1,0:T(8,128)(2,1)S(1)}, u32[]{:S(2)}, u32[]{:S(2)}) %collective-permute-start.10) | collective-permute-done | bytes 278560 | tf_op jit(solution)/shard_map/ppermute | solution.py:373
  72.8 4.4 %collective-permute-start.24 = (bf16[17,16,128]{2,1,0:T(8,128)(2,1)S(1)}, bf16[17,16,128]{2,1,0:T(8,128)(2,1)S(1)}, u32[]{:S(2)}, u32[]{:S(2)}) collective-permute-start(bf16[17,16,128]{2,1,0:T(8,128)(2,1)S(1)} %get-tuple-element.46), channel_id=1, source_target_pairs={{0,2},{2,4},{4,6},{6,0},{1,3},{3,5},{5,7},{7,1},{8,10},{10,12},{12... | collective-permute-start | bytes 208904 | tf_op jit(solution)/shard_map/ppermute | solution.py:373
  77.2 1.1 collective-permute-done.12.a3
  78.3 0.8 merge.2
  79.1 2.5 %collective-permute-start.13 = (bf16[17,16,128]{2,1,0:T(8,128)(2,1)S(1)}, bf16[17,16,128]{2,1,0:T(8,128)(2,1)S(1)}, u32[]{:S(2)}, u32[]{:S(2)}) collective-permute-start(bf16[17,16,128]{2,1,0:T(8,128)(2,1)S(1)} %get-tuple-element.35), channel_id=1, source_target_pairs={{0,24},{8,0},{16,8},{24,16},{1,25},{9,1},{17,9},{25,17},{2,26},{10... | collective-permute-start | bytes 208904 | tf_op jit(solution)/shard_map/ppermute | solution.py:373
  81.6 1.9 %collective-permute-start.14 = (bf16[17,16,128]{2,1,0:T(8,128)(2,1)S(1)}, bf16[17,16,128]{2,1,0:T(8,128)(2,1)S(1)}, u32[]{:S(2)}, u32[]{:S(2)}) collective-permute-start(bf16[17,16,128]{2,1,0:T(8,128)(2,1)S(1)} %get-tuple-element.36), channel_id=1, source_target_pairs={{0,16},{8,24},{16,0},{24,8},{1,17},{9,25},{17,1},{25,9},{2,18},{10... | collective-permute-start | bytes 208904 | tf_op jit(solution)/shard_map/ppermute | solution.py:373
  83.5 0.4 collective-permute-start.15
  83.9 0.1 reshape.30.refs_8_
  84.0 0.5 collective-permute-done.13.refs_1_
  84.4 3.1 %collective-permute-done.14.refs_2_ = bf16[17,16,128]{2,1,0:T(8,128)(2,1)S(1)} collective-permute-done((bf16[17,16,128]{2,1,0:T(8,128)(2,1)S(1)}, bf16[17,16,128]{2,1,0:T(8,128)(2,1)S(1)}, u32[]{:S(2)}, u32[]{:S(2)}) %collective-permute-start.14) | collective-permute-done | bytes 69664 | tf_op jit(solution)/shard_map/ppermute | solution.py:373
  87.5 1.5 collective-permute-done.15.refs_3_
  89.1 4.7 %project.1 = (bf16[16,8,896]{2,1,0:T(8,128)(2,1)S(1)}, bf16[16,8,896]{2,1,0:T(8,128)(2,1)S(1)}) custom-call(s32[1]{0:T(128)} %bitcast.core_ref, bf16[17,16,128]{2,1,0:T(8,128)(2,1)S(1)} %get-tuple-element.34.refs_0_, bf16[17,16,128]{2,1,0:T(8,128)(2,1)S(1)} %collective-permute-done.13.refs_1_, bf16[17,16,128]{2,1,0:T(8,128)(2,1)S(1)} %collective-permute-done.14.refs_2_, ...), custom_call_target="tpu_custom_call" | custom-call | tf_op jit(solution)/shard_map/project/pallas_call | solution.py:233
  93.8 0.1 collective-permute-start.25
  93.9 1.5 collective-permute-done.25
  95.4 0.7 add_convert_fusion.1
  96.1 3.5 %all-to-all-start = ((bf16[16,8,896]{2,1,0:T(8,128)(2,1)}), bf16[16,8,896]{2,1,0:T(8,128)(2,1)S(1)}, u32[]{:S(2)}, u32[]{:S(2)}) async-start(bf16[16,8,896]{2,1,0:T(8,128)(2,1)} %add_convert_fusion.1), calls=%async_computation | async-start | bytes 458752 | tf_op jit(solution)/shard_map/all_to_all | solution.py:422
  99.7 0.1 reduce
  99.8 8.5 %all-to-all-done.arrived_ref = bf16[16,8,896]{2,1,0:T(8,128)(2,1)S(1)} async-done(((bf16[16,8,896]{2,1,0:T(8,128)(2,1)}), bf16[16,8,896]{2,1,0:T(8,128)(2,1)S(1)}, u32[]{:S(2)}, u32[]{:S(2)}) %all-to-all-start) | async-done | bytes 229408 | tf_op jit(solution)/shard_map/all_to_all | solution.py:422
  108.4 0.2 spread.1
  108.6 23.8 %all_to_all.15.own_ref = bf16[64,8,896]{2,1,0:T(8,128)(2,1)S(1)} all-to-all(bf16[64,8,896]{2,1,0:T(8,128)(2,1)S(1)} %get-tuple-element.50), channel_id=1, replica_groups=mesh['y'=4,'x'=4,'z'=4,'c'=2] {'y','x','z'}, dimensions={0} | all-to-all | bytes 1835008 | tf_op jit(solution)/shard_map/all_to_all | solution.py:427
  132.4 2.4 %collective-permute-done.26.sib_ref = bf16[64,8,896]{2,1,0:T(8,128)(2,1)S(1)} collective-permute-done((bf16[64,8,896]{2,1,0:T(8,128)(2,1)S(1)}, bf16[64,8,896]{2,1,0:T(8,128)(2,1)S(1)}, u32[]{:S(2)}, u32[]{:S(2)}) %collective-permute-start.26) | collective-permute-done | bytes 917536 | tf_op jit(solution)/shard_map/ppermute | solution.py:373
  134.8 8.1 %experts.1 = (bf16[64,8,896]{2,1,0:T(8,128)(2,1)S(1)}, bf16[64,8,896]{2,1,0:T(8,128)(2,1)S(1)}, f32[16,8,128]{2,1,0:T(8,128)S(1)}) custom-call(s32[1,8]{1,0:T(1,128)S(1)} %copy-done.3, bf16[64,8,896]{2,1,0:T(8,128)(2,1)S(1)} %all_to_all.15.own_ref, bf16[64,8,896]{2,1,0:T(8,128)(2,1)S(1)} %collective-permute-done.26.sib_ref, ...), custom_call_target="tpu_custom_call" | custom-call | tf_op jit(solution)/shard_map/experts/pallas_call | solution.py:334
  142.9 0.2 collective-permute-start.27
  143.2 2.3 %collective-permute-done.27 = bf16[64,8,896]{2,1,0:T(8,128)(2,1)S(1)} collective-permute-done((bf16[64,8,896]{2,1,0:T(8,128)(2,1)S(1)}, bf16[64,8,896]{2,1,0:T(8,128)(2,1)S(1)}, u32[]{:S(2)}, u32[]{:S(2)}) %collective-permute-start.27) | collective-permute-done | bytes 917536 | tf_op jit(solution)/shard_map/ppermute | solution.py:373
  145.5 1.2 add_convert_fusion
  146.7 4.7 %all-to-all-start.2 = ((bf16[64,8,896]{2,1,0:T(8,128)(2,1)}), bf16[64,8,896]{2,1,0:T(8,128)(2,1)S(1)}, u32[]{:S(2)}, u32[]{:S(2)}) async-start(bf16[64,8,896]{2,1,0:T(8,128)(2,1)} %add_convert_fusion), calls=%async_computation.2 | async-start | bytes 1835008 | tf_op jit(solution)/shard_map/all_to_all | solution.py:433
  151.4 0.6 copy.15
  152.0 17.3 %all-to-all-done.2.returned_ref = bf16[64,8,896]{2,1,0:T(8,128)(2,1)S(1)} async-done(((bf16[64,8,896]{2,1,0:T(8,128)(2,1)}), bf16[64,8,896]{2,1,0:T(8,128)(2,1)S(1)}, u32[]{:S(2)}, u32[]{:S(2)}) %all-to-all-start.2) | async-done | bytes 917536 | tf_op jit(solution)/shard_map/all_to_all | solution.py:433
  169.2 0.1 gather.1
  169.4 0.6 copy.17
  (38 shorter events, 0.4 us)
Async XLA Ops:
  0.6 36.2 %collective-permute-start.9 = (bf16[8,576,1024]{2,1,0:T(8,128)(2,1)}, bf16[8,576,1024]{2,1,0:T(8,128)(2,1)}, u32[]{:S(2)}, u32[]{:S(2)}) collective-permute-start(bf16[8,576,1024]{2,1,0:T(8,128)(2,1)} %bitcast.22), channel_id=1, source_target_pairs={{0,1},{1,0},{2,3},{3,2},{4,5},{5,4},{6,7},{7,6},{8,9},{9,8},{10,11... | collective-permute-start | bytes 28311560 | tf_op jit(solution)/shard_map/ppermute | solution.py:373
  1.8 8.4 %collective-permute-start.3 = (bf16[4,16,576]{2,1,0:T(8,128)(2,1)S(1)}, bf16[4,16,576]{2,1,0:T(8,128)(2,1)S(1)}, u32[]{:S(2)}, u32[]{:S(2)}) collective-permute-start(bf16[4,16,576]{2,1,0:T(8,128)(2,1)S(1)} %slice.15), channel_id=1, source_target_pairs={{0,2},{2,4},{4,6},{6,0},{1,3},{3,5},{5,7},{7,1},{8,10},{10,12},{12... | collective-permute-start | bytes 221192 | tf_op jit(solution)/shard_map/ppermute | solution.py:373
  3.8 9.1 %collective-permute-start.4 = (bf16[4,16,576]{2,1,0:T(8,128)(2,1)S(1)}, bf16[4,16,576]{2,1,0:T(8,128)(2,1)S(1)}, u32[]{:S(2)}, u32[]{:S(2)}) collective-permute-start(bf16[4,16,576]{2,1,0:T(8,128)(2,1)S(1)} %slice.15), channel_id=1, source_target_pairs={{0,4},{2,6},{4,0},{6,2},{1,5},{3,7},{5,1},{7,3},{8,12},{10,14},{12... | collective-permute-start | bytes 221192 | tf_op jit(solution)/shard_map/ppermute | solution.py:373
  7.4 7.3 %collective-permute-start.5 = (bf16[4,16,576]{2,1,0:T(8,128)(2,1)S(1)}, bf16[4,16,576]{2,1,0:T(8,128)(2,1)S(1)}, u32[]{:S(2)}, u32[]{:S(2)}) collective-permute-start(bf16[4,16,576]{2,1,0:T(8,128)(2,1)S(1)} %slice.15), channel_id=1, source_target_pairs={{0,6},{2,0},{4,2},{6,4},{1,7},{3,1},{5,3},{7,5},{8,14},{10,8},{12,... | collective-permute-start | bytes 221192 | tf_op jit(solution)/shard_map/ppermute | solution.py:373
  8.5 6.5 %collective-permute-start = (bf16[4,16,576]{2,1,0:T(8,128)(2,1)S(1)}, bf16[4,16,576]{2,1,0:T(8,128)(2,1)S(1)}, u32[]{:S(2)}, u32[]{:S(2)}) collective-permute-start(bf16[4,16,576]{2,1,0:T(8,128)(2,1)S(1)} %slice.13), channel_id=1, source_target_pairs={{0,8},{8,16},{16,24},{24,0},{1,9},{9,17},{17,25},{25,1},{2,10},{10... | collective-permute-start | bytes 221192 | tf_op jit(solution)/shard_map/ppermute | solution.py:373
  10.1 6.4 %collective-permute-start.1 = (bf16[4,16,576]{2,1,0:T(8,128)(2,1)S(1)}, bf16[4,16,576]{2,1,0:T(8,128)(2,1)S(1)}, u32[]{:S(2)}, u32[]{:S(2)}) collective-permute-start(bf16[4,16,576]{2,1,0:T(8,128)(2,1)S(1)} %slice.13), channel_id=1, source_target_pairs={{0,16},{8,24},{16,0},{24,8},{1,17},{9,25},{17,1},{25,9},{2,18},{10... | collective-permute-start | bytes 221192 | tf_op jit(solution)/shard_map/ppermute | solution.py:373
  12.9 4.4 %collective-permute-start.2 = (bf16[4,16,576]{2,1,0:T(8,128)(2,1)S(1)}, bf16[4,16,576]{2,1,0:T(8,128)(2,1)S(1)}, u32[]{:S(2)}, u32[]{:S(2)}) collective-permute-start(bf16[4,16,576]{2,1,0:T(8,128)(2,1)S(1)} %slice.13), channel_id=1, source_target_pairs={{0,24},{8,0},{16,8},{24,16},{1,25},{9,1},{17,9},{25,17},{2,26},{10... | collective-permute-start | bytes 221192 | tf_op jit(solution)/shard_map/ppermute | solution.py:373
  17.4 11.0 %collective-permute-start.16 = (bf16[4,4,16,576]{3,2,1,0:T(8,128)(2,1)S(1)}, bf16[4,4,16,576]{3,2,1,0:T(8,128)(2,1)S(1)}, u32[]{:S(2)}, u32[]{:S(2)}) collective-permute-start(bf16[4,4,16,576]{3,2,1,0:T(8,128)(2,1)S(1)} %pad_maximum_fusion.1.q0), channel_id=1, source_target_pairs={{0,8},{8,16},{16,24},{24,0},{1,9},{9,17},{17,25},{25,1},{2,10},{10... | collective-permute-start | bytes 884744 | tf_op jit(solution)/shard_map/ppermute | solution.py:373
  18.8 16.5 %collective-permute-start.17 = (bf16[4,4,16,576]{3,2,1,0:T(8,128)(2,1)S(1)}, bf16[4,4,16,576]{3,2,1,0:T(8,128)(2,1)S(1)}, u32[]{:S(2)}, u32[]{:S(2)}) collective-permute-start(bf16[4,4,16,576]{3,2,1,0:T(8,128)(2,1)S(1)} %pad_maximum_fusion.1.q0), channel_id=1, source_target_pairs={{0,16},{8,24},{16,0},{24,8},{1,17},{9,25},{17,1},{25,9},{2,18},{10... | collective-permute-start | bytes 884744 | tf_op jit(solution)/shard_map/ppermute | solution.py:373
  22.0 14.9 %collective-permute-start.18 = (bf16[4,4,16,576]{3,2,1,0:T(8,128)(2,1)S(1)}, bf16[4,4,16,576]{3,2,1,0:T(8,128)(2,1)S(1)}, u32[]{:S(2)}, u32[]{:S(2)}) collective-permute-start(bf16[4,4,16,576]{3,2,1,0:T(8,128)(2,1)S(1)} %pad_maximum_fusion.1.q0), channel_id=1, source_target_pairs={{0,24},{8,0},{16,8},{24,16},{1,25},{9,1},{17,9},{25,17},{2,26},{10... | collective-permute-start | bytes 884744 | tf_op jit(solution)/shard_map/ppermute | solution.py:373
  22.7 27.4 %collective-permute-start.6 = (bf16[4,4,16,576]{3,2,1,0:T(8,128)(2,1)S(1)}, bf16[4,4,16,576]{3,2,1,0:T(8,128)(2,1)S(1)}, u32[]{:S(2)}, u32[]{:S(2)}) collective-permute-start(bf16[4,4,16,576]{3,2,1,0:T(8,128)(2,1)S(1)} %pad_maximum_fusion.q0), channel_id=1, source_target_pairs={{0,2},{2,4},{4,6},{6,0},{1,3},{3,5},{5,7},{7,1},{8,10},{10,12},{12... | collective-permute-start | bytes 884744 | tf_op jit(solution)/shard_map/ppermute | solution.py:373
  28.4 22.1 %collective-permute-start.7 = (bf16[4,4,16,576]{3,2,1,0:T(8,128)(2,1)S(1)}, bf16[4,4,16,576]{3,2,1,0:T(8,128)(2,1)S(1)}, u32[]{:S(2)}, u32[]{:S(2)}) collective-permute-start(bf16[4,4,16,576]{3,2,1,0:T(8,128)(2,1)S(1)} %pad_maximum_fusion.q0), channel_id=1, source_target_pairs={{0,4},{2,6},{4,0},{6,2},{1,5},{3,7},{5,1},{7,3},{8,12},{10,14},{12... | collective-permute-start | bytes 884744 | tf_op jit(solution)/shard_map/ppermute | solution.py:373
  35.3 15.3 %collective-permute-start.8 = (bf16[4,4,16,576]{3,2,1,0:T(8,128)(2,1)S(1)}, bf16[4,4,16,576]{3,2,1,0:T(8,128)(2,1)S(1)}, u32[]{:S(2)}, u32[]{:S(2)}) collective-permute-start(bf16[4,4,16,576]{3,2,1,0:T(8,128)(2,1)S(1)} %pad_maximum_fusion.q0), channel_id=1, source_target_pairs={{0,6},{2,0},{4,2},{6,4},{1,7},{3,1},{5,3},{7,5},{8,14},{10,8},{12,... | collective-permute-start | bytes 884744 | tf_op jit(solution)/shard_map/ppermute | solution.py:373
  36.9 0.7 copy-start.2
  48.3 15.6 %collective-permute-start.19 = (bf16[4,17,16,128]{3,2,1,0:T(8,128)(2,1)S(1)}, bf16[4,17,16,128]{3,2,1,0:T(8,128)(2,1)S(1)}, u32[]{:S(2)}, u32[]{:S(2)}) collective-permute-start(bf16[4,17,16,128]{3,2,1,0:T(8,128)(2,1)S(1)} %get-tuple-element.40), channel_id=1, source_target_pairs={{0,24},{8,0},{16,8},{24,16},{1,25},{9,1},{17,9},{25,17},{2,26},{10... | collective-permute-start | bytes 835592 | tf_op jit(solution)/shard_map/ppermute | solution.py:373
  48.9 15.7 %collective-permute-start.20 = (bf16[4,17,16,128]{3,2,1,0:T(8,128)(2,1)S(1)}, bf16[4,17,16,128]{3,2,1,0:T(8,128)(2,1)S(1)}, u32[]{:S(2)}, u32[]{:S(2)}) collective-permute-start(bf16[4,17,16,128]{3,2,1,0:T(8,128)(2,1)S(1)} %get-tuple-element.41), channel_id=1, source_target_pairs={{0,16},{8,24},{16,0},{24,8},{1,17},{9,25},{17,1},{25,9},{2,18},{10... | collective-permute-start | bytes 835592 | tf_op jit(solution)/shard_map/ppermute | solution.py:373
  50.1 33.8 %copy-start.4 = (bf16[32,4,576]{2,1,0:T(4,128)(2,1)S(1)}, bf16[32,4,576]{2,1,0:T(4,128)(2,1)}, u32[]{:S(2)}) copy-start(bf16[32,4,576]{2,1,0:T(4,128)(2,1)} %param.13) | copy-start | bytes 442372
  50.1 39.0 %copy-start = (bf16[4,512,128]{2,1,0:T(8,128)(2,1)S(1)}, bf16[4,512,128]{2,1,0:T(8,128)(2,1)}, u32[]{:S(2)}) copy-start(bf16[4,512,128]{2,1,0:T(8,128)(2,1)} %refs_10_.1) | copy-start | bytes 1572868
  50.1 39.0 %copy-start.1 = (bf16[32,576]{1,0:T(8,128)(2,1)S(1)}, bf16[32,576]{1,0:T(8,128)(2,1)}, u32[]{:S(2)}) copy-start(bf16[32,576]{1,0:T(8,128)(2,1)} %refs_9_.1) | copy-start | bytes 110596
  50.1 14.6 %collective-permute-start.21 = (bf16[4,17,16,128]{3,2,1,0:T(8,128)(2,1)S(1)}, bf16[4,17,16,128]{3,2,1,0:T(8,128)(2,1)S(1)}, u32[]{:S(2)}, u32[]{:S(2)}) collective-permute-start(bf16[4,17,16,128]{3,2,1,0:T(8,128)(2,1)S(1)} %get-tuple-element.42), channel_id=1, source_target_pairs={{0,8},{8,16},{16,24},{24,0},{1,9},{9,17},{17,25},{25,1},{2,10},{10... | collective-permute-start | bytes 835592 | tf_op jit(solution)/shard_map/ppermute | solution.py:373
  61.3 11.5 %collective-permute-start.10 = (bf16[4,17,16,128]{3,2,1,0:T(8,128)(2,1)S(1)}, bf16[4,17,16,128]{3,2,1,0:T(8,128)(2,1)S(1)}, u32[]{:S(2)}, u32[]{:S(2)}) collective-permute-start(bf16[4,17,16,128]{3,2,1,0:T(8,128)(2,1)S(1)} %get-tuple-element.31), channel_id=1, source_target_pairs={{0,6},{2,0},{4,2},{6,4},{1,7},{3,1},{5,3},{7,5},{8,14},{10,8},{12,... | collective-permute-start | bytes 835592 | tf_op jit(solution)/shard_map/ppermute | solution.py:373
  63.7 13.5 %collective-permute-start.11 = (bf16[4,17,16,128]{3,2,1,0:T(8,128)(2,1)S(1)}, bf16[4,17,16,128]{3,2,1,0:T(8,128)(2,1)S(1)}, u32[]{:S(2)}, u32[]{:S(2)}) collective-permute-start(bf16[4,17,16,128]{3,2,1,0:T(8,128)(2,1)S(1)} %get-tuple-element.32), channel_id=1, source_target_pairs={{0,4},{2,6},{4,0},{6,2},{1,5},{3,7},{5,1},{7,3},{8,12},{10,14},{12... | collective-permute-start | bytes 835592 | tf_op jit(solution)/shard_map/ppermute | solution.py:373
  63.8 14.5 %collective-permute-start.12 = (bf16[4,17,16,128]{3,2,1,0:T(8,128)(2,1)S(1)}, bf16[4,17,16,128]{3,2,1,0:T(8,128)(2,1)S(1)}, u32[]{:S(2)}, u32[]{:S(2)}) collective-permute-start(bf16[4,17,16,128]{3,2,1,0:T(8,128)(2,1)S(1)} %get-tuple-element.33), channel_id=1, source_target_pairs={{0,2},{2,4},{4,6},{6,0},{1,3},{3,5},{5,7},{7,1},{8,10},{10,12},{12... | collective-permute-start | bytes 835592 | tf_op jit(solution)/shard_map/ppermute | solution.py:373
  65.5 18.0 %collective-permute-start.22 = (bf16[17,16,128]{2,1,0:T(8,128)(2,1)S(1)}, bf16[17,16,128]{2,1,0:T(8,128)(2,1)S(1)}, u32[]{:S(2)}, u32[]{:S(2)}) collective-permute-start(bf16[17,16,128]{2,1,0:T(8,128)(2,1)S(1)} %get-tuple-element.44), channel_id=1, source_target_pairs={{0,6},{2,0},{4,2},{6,4},{1,7},{3,1},{5,3},{7,5},{8,14},{10,8},{12,... | collective-permute-start | bytes 208904 | tf_op jit(solution)/shard_map/ppermute | solution.py:373
  68.0 16.0 %collective-permute-start.23 = (bf16[17,16,128]{2,1,0:T(8,128)(2,1)S(1)}, bf16[17,16,128]{2,1,0:T(8,128)(2,1)S(1)}, u32[]{:S(2)}, u32[]{:S(2)}) collective-permute-start(bf16[17,16,128]{2,1,0:T(8,128)(2,1)S(1)} %get-tuple-element.45), channel_id=1, source_target_pairs={{0,4},{2,6},{4,0},{6,2},{1,5},{3,7},{5,1},{7,3},{8,12},{10,14},{12... | collective-permute-start | bytes 208904 | tf_op jit(solution)/shard_map/ppermute | solution.py:373
  72.8 11.1 %collective-permute-start.24 = (bf16[17,16,128]{2,1,0:T(8,128)(2,1)S(1)}, bf16[17,16,128]{2,1,0:T(8,128)(2,1)S(1)}, u32[]{:S(2)}, u32[]{:S(2)}) collective-permute-start(bf16[17,16,128]{2,1,0:T(8,128)(2,1)S(1)} %get-tuple-element.46), channel_id=1, source_target_pairs={{0,2},{2,4},{4,6},{6,0},{1,3},{3,5},{5,7},{7,1},{8,10},{10,12},{12... | collective-permute-start | bytes 208904 | tf_op jit(solution)/shard_map/ppermute | solution.py:373
  79.1 5.3 %collective-permute-start.13 = (bf16[17,16,128]{2,1,0:T(8,128)(2,1)S(1)}, bf16[17,16,128]{2,1,0:T(8,128)(2,1)S(1)}, u32[]{:S(2)}, u32[]{:S(2)}) collective-permute-start(bf16[17,16,128]{2,1,0:T(8,128)(2,1)S(1)} %get-tuple-element.35), channel_id=1, source_target_pairs={{0,24},{8,0},{16,8},{24,16},{1,25},{9,1},{17,9},{25,17},{2,26},{10... | collective-permute-start | bytes 208904 | tf_op jit(solution)/shard_map/ppermute | solution.py:373
  81.6 5.9 %collective-permute-start.14 = (bf16[17,16,128]{2,1,0:T(8,128)(2,1)S(1)}, bf16[17,16,128]{2,1,0:T(8,128)(2,1)S(1)}, u32[]{:S(2)}, u32[]{:S(2)}) collective-permute-start(bf16[17,16,128]{2,1,0:T(8,128)(2,1)S(1)} %get-tuple-element.36), channel_id=1, source_target_pairs={{0,16},{8,24},{16,0},{24,8},{1,17},{9,25},{17,1},{25,9},{2,18},{10... | collective-permute-start | bytes 208904 | tf_op jit(solution)/shard_map/ppermute | solution.py:373
  83.5 5.5 %collective-permute-start.15 = (bf16[17,16,128]{2,1,0:T(8,128)(2,1)S(1)}, bf16[17,16,128]{2,1,0:T(8,128)(2,1)S(1)}, u32[]{:S(2)}, u32[]{:S(2)}) collective-permute-start(bf16[17,16,128]{2,1,0:T(8,128)(2,1)S(1)} %get-tuple-element.37), channel_id=1, source_target_pairs={{0,8},{8,16},{16,24},{24,0},{1,9},{9,17},{17,25},{25,1},{2,10},{10... | collective-permute-start | bytes 208904 | tf_op jit(solution)/shard_map/ppermute | solution.py:373
  89.0 10.6 %copy-start.7 = (bf16[1,7168]{1,0:T(2,128)(2,1)S(1)}, bf16[1,7168]{1,0:T(2,128)(2,1)}, u32[]{:S(2)}) copy-start(bf16[1,7168]{1,0:T(2,128)(2,1)} %param.19) | copy-start | bytes 43012
  89.0 10.8 %copy-start.6 = (f32[7168]{0:T(1024)S(1)}, f32[7168]{0:T(1024)}, u32[]{:S(2)}) copy-start(f32[7168]{0:T(1024)} %param.20) | copy-start | bytes 86020
  89.0 43.3 %copy-start.5 = (bf16[7168,16]{0,1:T(8,128)(2,1)S(1)}, bf16[7168,16]{0,1:T(8,128)(2,1)}, u32[]{:S(2)}) copy-start(bf16[7168,16]{0,1:T(8,128)(2,1)} %param.21) | copy-start | bytes 688132
  93.8 41.0 %copy-start.3 = (s32[1,8]{1,0:T(1,128)S(1)}, s32[1,8]{1,0:T(1,128)}, u32[]{:S(2)}) copy-start(s32[1,8]{1,0:T(1,128)} %routes_ref.1) | copy-start | bytes 100
  93.8 1.6 collective-permute-start.25
  96.1 12.2 %all-to-all-start = ((bf16[16,8,896]{2,1,0:T(8,128)(2,1)}), bf16[16,8,896]{2,1,0:T(8,128)(2,1)S(1)}, u32[]{:S(2)}, u32[]{:S(2)}) async-start(bf16[16,8,896]{2,1,0:T(8,128)(2,1)} %add_convert_fusion.1), calls=%async_computation | async-start | bytes 458752 | tf_op jit(solution)/shard_map/all_to_all | solution.py:422
  132.4 2.5 %collective-permute-start.26 = (bf16[64,8,896]{2,1,0:T(8,128)(2,1)S(1)}, bf16[64,8,896]{2,1,0:T(8,128)(2,1)S(1)}, u32[]{:S(2)}, u32[]{:S(2)}) collective-permute-start(bf16[64,8,896]{2,1,0:T(8,128)(2,1)S(1)} %all_to_all.15.own_ref), channel_id=1, source_target_pairs={{0,1},{1,0},{2,3},{3,2},{4,5},{5,4},{6,7},{7,6},{8,9},{9,8},{10,11... | collective-permute-start | bytes 2752520 | tf_op jit(solution)/shard_map/ppermute | solution.py:373
  142.9 2.6 %collective-permute-start.27 = (bf16[64,8,896]{2,1,0:T(8,128)(2,1)S(1)}, bf16[64,8,896]{2,1,0:T(8,128)(2,1)S(1)}, u32[]{:S(2)}, u32[]{:S(2)}) collective-permute-start(bf16[64,8,896]{2,1,0:T(8,128)(2,1)S(1)} %get-tuple-element.53), channel_id=1, source_target_pairs={{0,1},{1,0},{2,3},{3,2},{4,5},{5,4},{6,7},{7,6},{8,9},{9,8},{10,11... | collective-permute-start | bytes 2752520 | tf_op jit(solution)/shard_map/ppermute | solution.py:373
  146.7 22.6 %all-to-all-start.2 = ((bf16[64,8,896]{2,1,0:T(8,128)(2,1)}), bf16[64,8,896]{2,1,0:T(8,128)(2,1)S(1)}, u32[]{:S(2)}, u32[]{:S(2)}) async-start(bf16[64,8,896]{2,1,0:T(8,128)(2,1)} %add_convert_fusion), calls=%async_computation.2 | async-start | bytes 1835008 | tf_op jit(solution)/shard_map/all_to_all | solution.py:433

commit v3 on v2

--- a/solution.py
+++ b/solution.py
@@ -41,9 +41,9 @@
     return tile + pltpu.roll(tile, LANES - STAT, 1) + pltpu.roll(tile, LANES - 2 * STAT, 1)
 
 
-def attend_kernel(blocks_ref, lengths_ref, q0, q1, q2, q3, own_ref, sib_ref, o0, o1, o2, o3, stat_ref, *, first, count):
+def attend_kernel(scalars_ref, q0, q1, q2, q3, own_ref, sib_ref, o0, o1, o2, o3, stat_ref, *, first, count):
     step = pl.program_id(0)
-    length = lengths_ref[first + step]
+    length = scalars_ref[2 + first + step]
     outs = (o0, o1, o2, o3)
     query = jnp.concatenate([ref[...].reshape(-1, ref.shape[-1]) for ref in (q0, q1, q2, q3)], axis=0)
     rows = query.shape[0]
@@ -51,7 +51,7 @@
     scores = []
     for which, keys in enumerate((own_ref, sib_ref)):
         score = score_scale * jnp.dot(query, keys[0], preferred_element_type=f32)
-        position = blocks_ref[which] * block_len + lax.broadcasted_iota(jnp.int32, (1, block_len), 1)
+        position = scalars_ref[which] * block_len + lax.broadcasted_iota(jnp.int32, (1, block_len), 1)
         scores.append(jnp.where(position < length, score, neg_floor))
     top = jnp.maximum(
         jnp.max(scores[0], axis=-1, keepdims=True), jnp.max(scores[1], axis=-1, keepdims=True)
@@ -88,7 +88,7 @@
             out[:, 4 * count] = stats[d * part : (d + 1) * part].astype(bf16).reshape(pieces, 16, LANES)
 
 
-def attend(blocks, lengths, queries, cache, sibling, first, count):
+def attend(scalars, queries, cache, sibling, first, count):
     features, block_len = cache.shape[1:]
     tiles = 4 * count + 1
     out = jax.ShapeDtypeStruct((4, tiles, 16, LANES), bf16)
@@ -97,7 +97,7 @@
         functools.partial(attend_kernel, first=first, count=count),
         out_shape=[out] * 4,
         grid_spec=pltpu.PrefetchScalarGridSpec(
-            num_scalar_prefetch=2,
+            num_scalar_prefetch=1,
             grid=(count,),
             in_specs=[pl.BlockSpec((4, None, 16, features), lambda i, *_: (0, i, 0, 0))] * 4
             + [pl.BlockSpec((1, features, block_len), lambda i, *_: (first + i, 0, 0))] * 2,
@@ -108,7 +108,7 @@
             dimension_semantics=("arbitrary",), vmem_limit_bytes=48 << 20
         ),
         name="attend",
-    )(blocks, lengths, *queries, cache, sibling)
+    )(scalars, *queries, cache, sibling)
 
 
 def merged_stats(tiles):
@@ -269,31 +269,7 @@
     )(arrived, residual, gain)
 
 
-def experts_kernel(
-    routes_ref, own_ref, sib_ref, normed_ref, router_ref, gate_hbm, up_hbm, down_hbm,
-    out_own, out_sib, coefficient_ref, gate_ref, up_ref, down_ref, rows_ref, sems
-):
-    half = own_ref.shape[0]
-    rows = 2 * half
-    chunk = out_own.shape[2]
-    tiles = chunk // LANES
-
-    def fetch(which, k):
-        window = pl.ds(k * chunk, chunk)
-        source, target = ((gate_hbm, gate_ref), (up_hbm, up_ref), (down_hbm, down_ref))[which]
-        if which == 2:
-            return pltpu.make_async_copy(source.at[:, window], target.at[:, window], sems.at[which, k])
-        return pltpu.make_async_copy(source.at[window], target.at[window], sems.at[which, k])
-
-    for k in range(SPAN):
-        fetch(0, k).start()
-        fetch(1, k).start()
-    for k in range(SPAN):
-        fetch(2, k).start()
-    for piece in range(tiles):
-        window = slice(piece * LANES, (piece + 1) * LANES)
-        rows_ref[piece, : half * SPAN] = own_ref[:, :, window].astype(f32).reshape(half * SPAN, LANES)
-        rows_ref[piece, half * SPAN :] = sib_ref[:, :, window].astype(f32).reshape(half * SPAN, LANES)
+def route_kernel(routes_ref, normed_ref, router_ref, coefficient_ref):
     products = router_ref[...].astype(f32) * normed_ref[...].astype(f32)[None]
     values = jnp.sum(jnp.sum(products, axis=2, keepdims=True), axis=1, keepdims=True)
     values = 1.0 / (1.0 + jnp.exp(-values))
@@ -304,18 +280,73 @@
     picked = values * chosen
     share = route_scale * picked / jnp.sum(picked, axis=0, keepdims=True)
     coefficient_ref[...] = jnp.broadcast_to(share, coefficient_ref.shape)
+
+
+def route(routes, normed, w_router):
+    span, chunk = normed.shape
+    inside = pl.BlockSpec(memory_space=pltpu.VMEM)
+    return pl.pallas_call(
+        route_kernel,
+        out_shape=jax.ShapeDtypeStruct((EXPERTS, span, LANES), f32),
+        in_specs=[pl.BlockSpec(memory_space=pltpu.SMEM), inside, inside],
+        compiler_params=pltpu.CompilerParams(vmem_limit_bytes=16 << 20),
+        name="route",
+    )(routes, normed, w_router.T.reshape(EXPERTS, span, chunk))
+
+
+def hold_kernel(*refs):
+    count = len(refs) // 2
+    sems = refs[-1]
+    copies = []
+    for i, (source, target) in enumerate(zip(refs[:count], refs[count : 2 * count])):
+        part = source.shape[0] // SPAN
+        for k in range(SPAN):
+            window = pl.ds(k * part, part)
+            copies.append(pltpu.make_async_copy(source.at[window], target.at[window], sems.at[i, k]))
+    for copy in copies:
+        copy.start()
+    for copy in copies:
+        copy.wait()
+
+
+def hold(*weights):
+    return pl.pallas_call(
+        hold_kernel,
+        out_shape=[pltpu.VMEM(w.shape, w.dtype) for w in weights],
+        in_specs=[pl.BlockSpec(memory_space=pltpu.HBM)] * len(weights),
+        out_specs=[pl.BlockSpec(memory_space=pltpu.VMEM)] * len(weights),
+        scratch_shapes=[pltpu.SemaphoreType.DMA((len(weights), SPAN))],
+        compiler_params=pltpu.CompilerParams(vmem_limit_bytes=24 << 20),
+        name="hold",
+    )(*[pltpu.with_memory_space_constraint(w, pltpu.HBM) for w in weights])
+
+
+def experts_kernel(own_ref, sib_ref, gate_ref, up_ref, down_hbm, out_own, out_sib, down_ref, rows_ref, sems):
+    half = own_ref.shape[0]
+    rows = 2 * half
+    chunk = out_own.shape[2]
+    tiles = chunk // LANES
+
+    def fetch(k):
+        window = pl.ds(k * chunk, chunk)
+        return pltpu.make_async_copy(down_hbm.at[:, window], down_ref.at[:, window], sems.at[k])
+
+    for k in range(SPAN):
+        fetch(k).start()
+    for piece in range(tiles):
+        window = slice(piece * LANES, (piece + 1) * LANES)
+        rows_ref[piece, : half * SPAN] = own_ref[:, :, window].astype(f32).reshape(half * SPAN, LANES)
+        rows_ref[piece, half * SPAN :] = sib_ref[:, :, window].astype(f32).reshape(half * SPAN, LANES)
     gate = up = 0.0
     for k in range(SPAN):
         block = jnp.concatenate(
             [rows_ref[piece, pl.ds(k, rows, stride=SPAN), :] for piece in range(tiles)], axis=1
         ).astype(bf16)
-        fetch(0, k).wait()
         gate = gate + jnp.dot(block, gate_ref[k * chunk : (k + 1) * chunk], preferred_element_type=f32)
-        fetch(1, k).wait()
         up = up + jnp.dot(block, up_ref[k * chunk : (k + 1) * chunk], preferred_element_type=f32)
     hidden = (gate / (1.0 + jnp.exp(-gate)) * up).astype(bf16)
     for k in range(SPAN):
-        fetch(2, k).wait()
+        fetch(k).wait()
         result = jnp.dot(hidden, down_ref[:, k * chunk : (k + 1) * chunk], preferred_element_type=f32)
         for piece in range(tiles):
             rows_ref[piece, pl.ds(k, rows, stride=SPAN), :] = result[:, piece * LANES : (piece + 1) * LANES]
@@ -325,27 +356,23 @@
         out_sib[:, :, window] = rows_ref[piece, half * SPAN :].reshape(half, SPAN, LANES).astype(bf16)
 
 
-def experts(routes, own_rows, sibling_rows, normed, w_router, w_gate, w_up, w_down):
+def experts(own_rows, sibling_rows, w_gate, w_up, w_down):
     out = jax.ShapeDtypeStruct(own_rows.shape, bf16)
     inside = pl.BlockSpec(memory_space=pltpu.VMEM)
-    outside = pl.BlockSpec(memory_space=pltpu.HBM)
     half, span, chunk = own_rows.shape
-    weights = [pltpu.with_memory_space_constraint(w, pltpu.HBM) for w in (w_gate, w_up, w_down)]
     return pl.pallas_call(
         experts_kernel,
-        out_shape=[out, out, jax.ShapeDtypeStruct((EXPERTS, span, LANES), f32)],
-        in_specs=[pl.BlockSpec(memory_space=pltpu.SMEM)] + [inside] * 4 + [outside] * 3,
-        out_specs=[inside] * 3,
+        out_shape=[out, out],
+        in_specs=[inside] * 4 + [pl.BlockSpec(memory_space=pltpu.HBM)],
+        out_specs=[inside] * 2,
         scratch_shapes=[
-            pltpu.VMEM(w_gate.shape, bf16),
-            pltpu.VMEM(w_up.shape, bf16),
             pltpu.VMEM(w_down.shape, bf16),
             pltpu.VMEM((chunk // LANES, 2 * half * span, LANES), f32),
-            pltpu.SemaphoreType.DMA((3, span)),
+            pltpu.SemaphoreType.DMA((span,)),
         ],
-        compiler_params=pltpu.CompilerParams(vmem_limit_bytes=48 << 20),
+        compiler_params=pltpu.CompilerParams(vmem_limit_bytes=20 << 20),
         name="experts",
-    )(routes, own_rows, sibling_rows, normed, w_router.T.reshape(EXPERTS, span, chunk), *weights)
+    )(own_rows, sibling_rows, w_gate, w_up, pltpu.with_memory_space_constraint(w_down, pltpu.HBM))
 
 
 def gather_kernel(returned_ref, stream_ref, coefficient_ref, out_ref):
@@ -410,9 +437,9 @@
     stack_x, stack_z = lax.optimization_barrier((stack_x, stack_z))
     queries_a = all_shifts(stack_x, "z")
     queries_b = all_shifts(stack_z, "x")
-    blocks = jnp.stack([ctx, ctx ^ 1]).astype(jnp.int32)
-    out_a = attend(blocks, lengths, queries_a, cache, sibling_cache, 0, count)
-    out_b = attend(blocks, lengths, queries_b, cache, sibling_cache, count, count)
+    scalars = jnp.concatenate([jnp.stack([ctx, ctx ^ 1]).astype(jnp.int32), lengths])
+    out_a = attend(scalars, queries_a, cache, sibling_cache, 0, count)
+    out_b = attend(scalars, queries_b, cache, sibling_cache, count, count)
     final_a = return_shifts(merge(return_shifts(out_a, "z"), count), "x")
     final_b = return_shifts(merge(return_shifts(out_b, "x"), count), "z")
     kept, given = project(
@@ -424,11 +451,13 @@
     attn_out, stream, normed, rows = spread(
         arrived, residual.reshape(SPAN, -1), norm_gain.reshape(SPAN, -1), chips
     )
+    normed, *weights = lax.optimization_barrier((normed, w_gate, w_up))
+    weights = hold(*weights)
+    coefficient = route(routes, normed, w_router)
     own_rows = lax.all_to_all(rows, ("y", "x", "z"), split_axis=0, concat_axis=0, tiled=True)
+    own_rows, coefficient = lax.optimization_barrier((own_rows, coefficient))
     sibling_rows = shift_by(own_rows, "c", 1)
-    out_own, out_sibling, coefficient = experts(
-        routes, own_rows, sibling_rows, normed, w_router, w_gate, w_up, w_down
-    )
+    out_own, out_sibling = experts(own_rows, sibling_rows, *weights, w_down)
     chip_out = (out_own.astype(f32) + shift_by(out_sibling, "c", 1).astype(f32)).astype(bf16)
     returned = lax.all_to_all(chip_out, ("y", "x", "z"), split_axis=0, concat_axis=0, tiled=True)
     layer_out = gather(returned, stream, coefficient)

time: 170 us -> 169 us (level)
  blocking collectives: 23.8 us -> 0 us
  waiting for transfers between devices: 54.4 us -> 70.6 us
  starting transfers between devices: 49.3 us -> 53.5 us
    all_to_all x1 -> x0, blocking collectives: 23.8 us -> none  [local(): lax.all_to_all(rows, ('y', 'x', 'z'), split_axis=0, concat_axis=0, tiled=...]
    all_to_all x0 -> x1, waiting for transfers between devices: none -> 15.9 us  [local(): lax.all_to_all(rows, ('y', 'x', 'z'), split_axis=0, concat_axis=0, tiled=...]
    all_to_all x0 -> x1, starting transfers between devices: none -> 7.17 us  [local(): lax.all_to_all(rows, ('y', 'x', 'z'), split_axis=0, concat_axis=0, tiled=...]
    ppermute x28, starting transfers between devices: 41.1 us -> 38 us  [shift_by(): lax.ppermute(value, axis, [(i, (i + offset) % size) for i in range(size)])]
    pallas_call x1 -> x3, Pallas kernels: 8.09 us -> 8.75 us  [the longest x1 4.85 us: experts(): pl.pallas_call(experts_kernel, out_shape=[out, out], in_specs=[inside] *...]
  transfers between devices with their start and end apart: 30 -> 31, of which waited for: 15 -> 15; matrix products, arithmetic and copies ran while one was open for 1% -> 2% of each run, Pallas kernels for 14% -> 16%
where the time goes in v3:
time: 169 us; the launch traced here: 168 us
  waiting for transfers between devices  70.6 us (42%)
  starting transfers between devices  53.5 us (32%)
  Pallas kernels  37.9 us (22%)
  other arithmetic  2.88 us (2%)
  local copies, waits for them, and re-layouts  2.6 us (2%)
    ppermute x28, starting transfers between devices, shift_by(): lax.ppermute(value, axis, [(i, (i + offset) % size) for i in range(size)])  38 us
    ppermute x28, waiting for transfers between devices, shift_by(): lax.ppermute(value, axis, [(i, (i + offset) % size) for i in range(size)])  28.7 us
    pallas_call x2, Pallas kernels, attend(): pl.pallas_call(functools.partial(attend_kernel, first=first, count=count)...  21.4 us
    all_to_all x1, waiting for transfers between devices, local(): lax.all_to_all(chip_out, ('y', 'x', 'z'), split_axis=0, concat_axis=0, ti...  17.5 us
    all_to_all x1, waiting for transfers between devices, local(): lax.all_to_all(rows, ('y', 'x', 'z'), split_axis=0, concat_axis=0, tiled=...  15.9 us
    all_to_all x1, waiting for transfers between devices, local(): lax.all_to_all(chip_sum, ('x', 'z'), split_axis=0, concat_axis=0, tiled=T...  8.45 us
    all_to_all x1, starting transfers between devices, local(): lax.all_to_all(rows, ('y', 'x', 'z'), split_axis=0, concat_axis=0, tiled=...  7.17 us
    pallas_call x1, Pallas kernels, experts(): pl.pallas_call(experts_kernel, out_shape=[out, out], in_specs=[inside] *...  4.85 us
  transfers between devices with their start and end apart: 31, of which 15 were waited for; matrix products, arithmetic and copies ran while one was open for 2% of the time, Pallas kernels for 16%

profile of v3, /device:TPU:0, one launch (start us, length us, event | category | flops | bytes accessed | tf_op | source)
XLA Modules:
  0.0 168.3 jit_solution(14819540591865887057)
XLA Ops:
  0.6 0.1 collective-permute-start.9
  0.7 1.0 fusion
  1.8 2.1 %collective-permute-start.3 = (bf16[4,16,576]{2,1,0:T(8,128)(2,1)S(1)}, bf16[4,16,576]{2,1,0:T(8,128)(2,1)S(1)}, u32[]{:S(2)}, u32[]{:S(2)}) collective-permute-start(bf16[4,16,576]{2,1,0:T(8,128)(2,1)S(1)} %slice.15), channel_id=1, source_target_pairs={{0,2},{2,4},{4,6},{6,0},{1,3},{3,5},{5,7},{7,1},{8,10},{10,12},{12... | collective-permute-start | bytes 221192 | tf_op jit(solution)/shard_map/ppermute | solution.py:400
  3.8 3.6 %collective-permute-start.4 = (bf16[4,16,576]{2,1,0:T(8,128)(2,1)S(1)}, bf16[4,16,576]{2,1,0:T(8,128)(2,1)S(1)}, u32[]{:S(2)}, u32[]{:S(2)}) collective-permute-start(bf16[4,16,576]{2,1,0:T(8,128)(2,1)S(1)} %slice.15), channel_id=1, source_target_pairs={{0,4},{2,6},{4,0},{6,2},{1,5},{3,7},{5,1},{7,3},{8,12},{10,14},{12... | collective-permute-start | bytes 221192 | tf_op jit(solution)/shard_map/ppermute | solution.py:400
  7.4 1.0 collective-permute-start.5
  8.5 1.6 collective-permute-start
  10.1 2.8 %collective-permute-start.1 = (bf16[4,16,576]{2,1,0:T(8,128)(2,1)S(1)}, bf16[4,16,576]{2,1,0:T(8,128)(2,1)S(1)}, u32[]{:S(2)}, u32[]{:S(2)}) collective-permute-start(bf16[4,16,576]{2,1,0:T(8,128)(2,1)S(1)} %slice.13), channel_id=1, source_target_pairs={{0,16},{8,24},{16,0},{24,8},{1,17},{9,25},{17,1},{25,9},{2,18},{10... | collective-permute-start | bytes 221192 | tf_op jit(solution)/shard_map/ppermute | solution.py:400
  12.9 1.8 %collective-permute-start.2 = (bf16[4,16,576]{2,1,0:T(8,128)(2,1)S(1)}, bf16[4,16,576]{2,1,0:T(8,128)(2,1)S(1)}, u32[]{:S(2)}, u32[]{:S(2)}) collective-permute-start(bf16[4,16,576]{2,1,0:T(8,128)(2,1)S(1)} %slice.13), channel_id=1, source_target_pairs={{0,24},{8,0},{16,8},{24,16},{1,25},{9,1},{17,9},{25,17},{2,26},{10... | collective-permute-start | bytes 221192 | tf_op jit(solution)/shard_map/ppermute | solution.py:400
  14.8 0.2 collective-permute-done
  15.0 1.5 collective-permute-done.1
  16.5 0.9 collective-permute-done.2
  17.4 0.1 pad_maximum_fusion.q0
  17.4 1.4 collective-permute-start.16
  18.8 3.2 %collective-permute-start.17 = (bf16[4,4,16,576]{3,2,1,0:T(8,128)(2,1)S(1)}, bf16[4,4,16,576]{3,2,1,0:T(8,128)(2,1)S(1)}, u32[]{:S(2)}, u32[]{:S(2)}) collective-permute-start(bf16[4,4,16,576]{3,2,1,0:T(8,128)(2,1)S(1)} %pad_maximum_fusion.1.q0), channel_id=1, source_target_pairs={{0,16},{8,24},{16,0},{24,8},{1,17},{9,25},{17,1},{25,9},{2,18},{10... | collective-permute-start | bytes 884744 | tf_op jit(solution)/shard_map/ppermute | solution.py:400
  22.0 0.7 collective-permute-start.18
  22.7 0.4 collective-permute-start.6
  23.1 5.4 %collective-permute-done.16.q1 = bf16[4,4,16,576]{3,2,1,0:T(8,128)(2,1)S(1)} collective-permute-done((bf16[4,4,16,576]{3,2,1,0:T(8,128)(2,1)S(1)}, bf16[4,4,16,576]{3,2,1,0:T(8,128)(2,1)S(1)}, u32[]{:S(2)}, u32[]{:S(2)}) %collective-permute-start.16) | collective-permute-done | bytes 294944 | tf_op jit(solution)/shard_map/ppermute | solution.py:400
  28.4 1.3 collective-permute-start.7
  29.8 5.5 %collective-permute-done.17.q2 = bf16[4,4,16,576]{3,2,1,0:T(8,128)(2,1)S(1)} collective-permute-done((bf16[4,4,16,576]{3,2,1,0:T(8,128)(2,1)S(1)}, bf16[4,4,16,576]{3,2,1,0:T(8,128)(2,1)S(1)}, u32[]{:S(2)}, u32[]{:S(2)}) %collective-permute-start.17) | collective-permute-done | bytes 294944 | tf_op jit(solution)/shard_map/ppermute | solution.py:400
  35.3 1.5 collective-permute-start.8
  36.8 0.7 pad_add_fusion.scalars_ref
  37.5 10.7 %attend.3 = (bf16[4,17,16,128]{3,2,1,0:T(8,128)(2,1)S(1)}, bf16[4,17,16,128]{3,2,1,0:T(8,128)(2,1)S(1)}, bf16[4,17,16,128]{3,2,1,0:T(8,128)(2,1)S(1)}, bf16[4,17,16,128]{3,2,1,0:T(8,128)(2,1)S(1)}) custom-call(s32[10]{0:T(128)S(1)} %pad_add_fusion.scalars_ref, bf16[4,4,16,576]{3,2,1,0:T(8,128)(2,1)S(1)} %pad_maximum_fusion.1.q0, ...), custom_call_target="tpu_custom_call" | custom-call | tf_op jit(solution)/shard_map/attend/pallas_call | solution.py:96
  48.3 0.1 collective-permute-start.19
  48.3 1.1 collective-permute-start.20
  49.4 1.0 collective-permute-start.21
  50.5 10.7 %attend.2 = (bf16[4,17,16,128]{3,2,1,0:T(8,128)(2,1)S(1)}, bf16[4,17,16,128]{3,2,1,0:T(8,128)(2,1)S(1)}, bf16[4,17,16,128]{3,2,1,0:T(8,128)(2,1)S(1)}, bf16[4,17,16,128]{3,2,1,0:T(8,128)(2,1)S(1)}) custom-call(s32[10]{0:T(128)S(1)} %pad_add_fusion.scalars_ref, bf16[4,4,16,576]{3,2,1,0:T(8,128)(2,1)S(1)} %pad_maximum_fusion.q0, ...), custom_call_target="tpu_custom_call" | custom-call | tf_op jit(solution)/shard_map/attend/pallas_call | solution.py:96
  61.2 2.5 %collective-permute-start.10 = (bf16[4,17,16,128]{3,2,1,0:T(8,128)(2,1)S(1)}, bf16[4,17,16,128]{3,2,1,0:T(8,128)(2,1)S(1)}, u32[]{:S(2)}, u32[]{:S(2)}) collective-permute-start(bf16[4,17,16,128]{3,2,1,0:T(8,128)(2,1)S(1)} %get-tuple-element.37), channel_id=1, source_target_pairs={{0,6},{2,0},{4,2},{6,4},{1,7},{3,1},{5,3},{7,5},{8,14},{10,8},{12,... | collective-permute-start | bytes 835592 | tf_op jit(solution)/shard_map/ppermute | solution.py:400
  63.7 0.1 collective-permute-start.11
  63.8 0.8 collective-permute-start.12
  64.6 0.8 merge.3
  65.5 2.5 %collective-permute-start.22 = (bf16[17,16,128]{2,1,0:T(8,128)(2,1)S(1)}, bf16[17,16,128]{2,1,0:T(8,128)(2,1)S(1)}, u32[]{:S(2)}, u32[]{:S(2)}) collective-permute-start(bf16[17,16,128]{2,1,0:T(8,128)(2,1)S(1)} %get-tuple-element.50), channel_id=1, source_target_pairs={{0,6},{2,0},{4,2},{6,4},{1,7},{3,1},{5,3},{7,5},{8,14},{10,8},{12,... | collective-permute-start | bytes 208904 | tf_op jit(solution)/shard_map/ppermute | solution.py:400
  68.0 2.2 %collective-permute-start.23 = (bf16[17,16,128]{2,1,0:T(8,128)(2,1)S(1)}, bf16[17,16,128]{2,1,0:T(8,128)(2,1)S(1)}, u32[]{:S(2)}, u32[]{:S(2)}) collective-permute-start(bf16[17,16,128]{2,1,0:T(8,128)(2,1)S(1)} %get-tuple-element.51), channel_id=1, source_target_pairs={{0,4},{2,6},{4,0},{6,2},{1,5},{3,7},{5,1},{7,3},{8,12},{10,14},{12... | collective-permute-start | bytes 208904 | tf_op jit(solution)/shard_map/ppermute | solution.py:400
  70.2 4.8 %collective-permute-done.10.a1 = bf16[4,17,16,128]{3,2,1,0:T(8,128)(2,1)S(1)} collective-permute-done((bf16[4,17,16,128]{3,2,1,0:T(8,128)(2,1)S(1)}, bf16[4,17,16,128]{3,2,1,0:T(8,128)(2,1)S(1)}, u32[]{:S(2)}, u32[]{:S(2)}) %collective-permute-start.10) | collective-permute-done | bytes 278560 | tf_op jit(solution)/shard_map/ppermute | solution.py:400
  75.0 1.6 collective-permute-start.24
  76.6 1.7 %collective-permute-done.12.a3 = bf16[4,17,16,128]{3,2,1,0:T(8,128)(2,1)S(1)} collective-permute-done((bf16[4,17,16,128]{3,2,1,0:T(8,128)(2,1)S(1)}, bf16[4,17,16,128]{3,2,1,0:T(8,128)(2,1)S(1)}, u32[]{:S(2)}, u32[]{:S(2)}) %collective-permute-start.12) | collective-permute-done | bytes 278560 | tf_op jit(solution)/shard_map/ppermute | solution.py:400
  78.3 0.8 merge.2
  79.1 2.4 %collective-permute-start.13 = (bf16[17,16,128]{2,1,0:T(8,128)(2,1)S(1)}, bf16[17,16,128]{2,1,0:T(8,128)(2,1)S(1)}, u32[]{:S(2)}, u32[]{:S(2)}) collective-permute-start(bf16[17,16,128]{2,1,0:T(8,128)(2,1)S(1)} %get-tuple-element.41), channel_id=1, source_target_pairs={{0,24},{8,0},{16,8},{24,16},{1,25},{9,1},{17,9},{25,17},{2,26},{10... | collective-permute-start | bytes 208904 | tf_op jit(solution)/shard_map/ppermute | solution.py:400
  81.5 1.4 collective-permute-start.14
  82.9 0.4 collective-permute-start.15
  83.2 0.1 reshape.30.refs_8_
  83.3 0.5 collective-permute-done.13.refs_1_
  83.8 3.6 %collective-permute-done.14.refs_2_ = bf16[17,16,128]{2,1,0:T(8,128)(2,1)S(1)} collective-permute-done((bf16[17,16,128]{2,1,0:T(8,128)(2,1)S(1)}, bf16[17,16,128]{2,1,0:T(8,128)(2,1)S(1)}, u32[]{:S(2)}, u32[]{:S(2)}) %collective-permute-start.14) | collective-permute-done | bytes 69664 | tf_op jit(solution)/shard_map/ppermute | solution.py:400
  87.4 1.0 collective-permute-done.15.refs_3_
  88.4 4.7 %project.1 = (bf16[16,8,896]{2,1,0:T(8,128)(2,1)S(1)}, bf16[16,8,896]{2,1,0:T(8,128)(2,1)S(1)}) custom-call(s32[1]{0:T(128)} %bitcast.core_ref, bf16[17,16,128]{2,1,0:T(8,128)(2,1)S(1)} %get-tuple-element.40.refs_0_, bf16[17,16,128]{2,1,0:T(8,128)(2,1)S(1)} %collective-permute-done.13.refs_1_, bf16[17,16,128]{2,1,0:T(8,128)(2,1)S(1)} %collective-permute-done.14.refs_2_, ...), custom_call_target="tpu_custom_call" | custom-call | tf_op jit(solution)/shard_map/project/pallas_call | solution.py:233
  93.2 0.1 collective-permute-start.25
  93.3 1.5 collective-permute-done.25
  94.7 0.7 add_convert_fusion.1
  95.5 3.6 %all-to-all-start = ((bf16[16,8,896]{2,1,0:T(8,128)(2,1)}), bf16[16,8,896]{2,1,0:T(8,128)(2,1)S(1)}, u32[]{:S(2)}, u32[]{:S(2)}) async-start(bf16[16,8,896]{2,1,0:T(8,128)(2,1)} %add_convert_fusion.1), calls=%async_computation | async-start | bytes 458752 | tf_op jit(solution)/shard_map/all_to_all | solution.py:449
  99.1 0.1 reduce
  99.3 8.5 %all-to-all-done.arrived_ref = bf16[16,8,896]{2,1,0:T(8,128)(2,1)S(1)} async-done(((bf16[16,8,896]{2,1,0:T(8,128)(2,1)}), bf16[16,8,896]{2,1,0:T(8,128)(2,1)S(1)}, u32[]{:S(2)}, u32[]{:S(2)}) %all-to-all-start) | async-done | bytes 229408 | tf_op jit(solution)/shard_map/all_to_all | solution.py:449
  107.7 1.1 spread.1
  108.9 7.2 %all-to-all-start.1 = ((bf16[64,8,896]{2,1,0:T(8,128)(2,1)}), bf16[64,8,896]{2,1,0:T(8,128)(2,1)S(1)}, u32[]{:S(2)}, u32[]{:S(2)}) async-start(bf16[64,8,896]{2,1,0:T(8,128)(2,1)} %get-tuple-element.56), calls=%async_computation.1 | async-start | bytes 1835008 | tf_op jit(solution)/shard_map/all_to_all | solution.py:457
  116.1 0.7 route.1.coefficient_ref
  116.8 15.9 %all-to-all-done.1.own_ref = bf16[64,8,896]{2,1,0:T(8,128)(2,1)S(1)} async-done(((bf16[64,8,896]{2,1,0:T(8,128)(2,1)}), bf16[64,8,896]{2,1,0:T(8,128)(2,1)S(1)}, u32[]{:S(2)}, u32[]{:S(2)}) %all-to-all-start.1) | async-done | bytes 917536 | tf_op jit(solution)/shard_map/all_to_all | solution.py:457
  132.7 3.2 %hold.1 = (bf16[7168,256]{1,0:T(8,128)(2,1)S(1)}, bf16[7168,256]{1,0:T(8,128)(2,1)S(1)}) custom-call(bf16[7168,256]{1,0:T(8,128)(2,1)} %refs_0_, bf16[7168,256]{1,0:T(8,128)(2,1)} %refs_1_), custom_call_target="tpu_custom_call" | custom-call | tf_op jit(solution)/shard_map/hold/pallas_call | solution.py:313
  136.0 4.8 %experts.1 = (bf16[64,8,896]{2,1,0:T(8,128)(2,1)S(1)}, bf16[64,8,896]{2,1,0:T(8,128)(2,1)S(1)}) custom-call(bf16[64,8,896]{2,1,0:T(8,128)(2,1)S(1)} %all-to-all-done.1.own_ref, bf16[64,8,896]{2,1,0:T(8,128)(2,1)S(1)} %collective-permute-done.26.sib_ref, bf16[7168,256]{1,0:T(8,128)(2,1)S(1)} %get-tuple-element.62.gate_ref, ...), custom_call_target="tpu_custom_call" | custom-call | tf_op jit(solution)/shard_map/experts/pallas_call | solution.py:363
  140.8 0.6 collective-permute-start.27
  141.4 2.1 %collective-permute-done.27 = bf16[64,8,896]{2,1,0:T(8,128)(2,1)S(1)} collective-permute-done((bf16[64,8,896]{2,1,0:T(8,128)(2,1)S(1)}, bf16[64,8,896]{2,1,0:T(8,128)(2,1)S(1)}, u32[]{:S(2)}, u32[]{:S(2)}) %collective-permute-start.27) | collective-permute-done | bytes 917536 | tf_op jit(solution)/shard_map/ppermute | solution.py:400
  143.5 1.2 add_convert_fusion
  144.7 4.7 %all-to-all-start.2 = ((bf16[64,8,896]{2,1,0:T(8,128)(2,1)}), bf16[64,8,896]{2,1,0:T(8,128)(2,1)S(1)}, u32[]{:S(2)}, u32[]{:S(2)}) async-start(bf16[64,8,896]{2,1,0:T(8,128)(2,1)} %add_convert_fusion), calls=%async_computation.2 | async-start | bytes 1835008 | tf_op jit(solution)/shard_map/all_to_all | solution.py:462
  149.4 0.6 copy.15
  150.0 17.5 %all-to-all-done.2.returned_ref = bf16[64,8,896]{2,1,0:T(8,128)(2,1)S(1)} async-done(((bf16[64,8,896]{2,1,0:T(8,128)(2,1)}), bf16[64,8,896]{2,1,0:T(8,128)(2,1)S(1)}, u32[]{:S(2)}, u32[]{:S(2)}) %all-to-all-start.2) | async-done | bytes 917536 | tf_op jit(solution)/shard_map/all_to_all | solution.py:462
  167.5 0.1 gather.1
  167.7 0.6 copy.17
  (39 shorter events, 0.4 us)
Async XLA Ops:
  0.6 36.9 %collective-permute-start.9 = (bf16[8,576,1024]{2,1,0:T(8,128)(2,1)}, bf16[8,576,1024]{2,1,0:T(8,128)(2,1)}, u32[]{:S(2)}, u32[]{:S(2)}) collective-permute-start(bf16[8,576,1024]{2,1,0:T(8,128)(2,1)} %bitcast.22), channel_id=1, source_target_pairs={{0,1},{1,0},{2,3},{3,2},{4,5},{5,4},{6,7},{7,6},{8,9},{9,8},{10,11... | collective-permute-start | bytes 28311560 | tf_op jit(solution)/shard_map/ppermute | solution.py:400
  1.8 8.4 %collective-permute-start.3 = (bf16[4,16,576]{2,1,0:T(8,128)(2,1)S(1)}, bf16[4,16,576]{2,1,0:T(8,128)(2,1)S(1)}, u32[]{:S(2)}, u32[]{:S(2)}) collective-permute-start(bf16[4,16,576]{2,1,0:T(8,128)(2,1)S(1)} %slice.15), channel_id=1, source_target_pairs={{0,2},{2,4},{4,6},{6,0},{1,3},{3,5},{5,7},{7,1},{8,10},{10,12},{12... | collective-permute-start | bytes 221192 | tf_op jit(solution)/shard_map/ppermute | solution.py:400
  3.8 9.1 %collective-permute-start.4 = (bf16[4,16,576]{2,1,0:T(8,128)(2,1)S(1)}, bf16[4,16,576]{2,1,0:T(8,128)(2,1)S(1)}, u32[]{:S(2)}, u32[]{:S(2)}) collective-permute-start(bf16[4,16,576]{2,1,0:T(8,128)(2,1)S(1)} %slice.15), channel_id=1, source_target_pairs={{0,4},{2,6},{4,0},{6,2},{1,5},{3,7},{5,1},{7,3},{8,12},{10,14},{12... | collective-permute-start | bytes 221192 | tf_op jit(solution)/shard_map/ppermute | solution.py:400
  7.4 7.3 %collective-permute-start.5 = (bf16[4,16,576]{2,1,0:T(8,128)(2,1)S(1)}, bf16[4,16,576]{2,1,0:T(8,128)(2,1)S(1)}, u32[]{:S(2)}, u32[]{:S(2)}) collective-permute-start(bf16[4,16,576]{2,1,0:T(8,128)(2,1)S(1)} %slice.15), channel_id=1, source_target_pairs={{0,6},{2,0},{4,2},{6,4},{1,7},{3,1},{5,3},{7,5},{8,14},{10,8},{12,... | collective-permute-start | bytes 221192 | tf_op jit(solution)/shard_map/ppermute | solution.py:400
  8.5 6.5 %collective-permute-start = (bf16[4,16,576]{2,1,0:T(8,128)(2,1)S(1)}, bf16[4,16,576]{2,1,0:T(8,128)(2,1)S(1)}, u32[]{:S(2)}, u32[]{:S(2)}) collective-permute-start(bf16[4,16,576]{2,1,0:T(8,128)(2,1)S(1)} %slice.13), channel_id=1, source_target_pairs={{0,8},{8,16},{16,24},{24,0},{1,9},{9,17},{17,25},{25,1},{2,10},{10... | collective-permute-start | bytes 221192 | tf_op jit(solution)/shard_map/ppermute | solution.py:400
  10.1 6.4 %collective-permute-start.1 = (bf16[4,16,576]{2,1,0:T(8,128)(2,1)S(1)}, bf16[4,16,576]{2,1,0:T(8,128)(2,1)S(1)}, u32[]{:S(2)}, u32[]{:S(2)}) collective-permute-start(bf16[4,16,576]{2,1,0:T(8,128)(2,1)S(1)} %slice.13), channel_id=1, source_target_pairs={{0,16},{8,24},{16,0},{24,8},{1,17},{9,25},{17,1},{25,9},{2,18},{10... | collective-permute-start | bytes 221192 | tf_op jit(solution)/shard_map/ppermute | solution.py:400
  12.9 4.4 %collective-permute-start.2 = (bf16[4,16,576]{2,1,0:T(8,128)(2,1)S(1)}, bf16[4,16,576]{2,1,0:T(8,128)(2,1)S(1)}, u32[]{:S(2)}, u32[]{:S(2)}) collective-permute-start(bf16[4,16,576]{2,1,0:T(8,128)(2,1)S(1)} %slice.13), channel_id=1, source_target_pairs={{0,24},{8,0},{16,8},{24,16},{1,25},{9,1},{17,9},{25,17},{2,26},{10... | collective-permute-start | bytes 221192 | tf_op jit(solution)/shard_map/ppermute | solution.py:400
  17.4 11.0 %collective-permute-start.16 = (bf16[4,4,16,576]{3,2,1,0:T(8,128)(2,1)S(1)}, bf16[4,4,16,576]{3,2,1,0:T(8,128)(2,1)S(1)}, u32[]{:S(2)}, u32[]{:S(2)}) collective-permute-start(bf16[4,4,16,576]{3,2,1,0:T(8,128)(2,1)S(1)} %pad_maximum_fusion.1.q0), channel_id=1, source_target_pairs={{0,8},{8,16},{16,24},{24,0},{1,9},{9,17},{17,25},{25,1},{2,10},{10... | collective-permute-start | bytes 884744 | tf_op jit(solution)/shard_map/ppermute | solution.py:400
  18.8 16.5 %collective-permute-start.17 = (bf16[4,4,16,576]{3,2,1,0:T(8,128)(2,1)S(1)}, bf16[4,4,16,576]{3,2,1,0:T(8,128)(2,1)S(1)}, u32[]{:S(2)}, u32[]{:S(2)}) collective-permute-start(bf16[4,4,16,576]{3,2,1,0:T(8,128)(2,1)S(1)} %pad_maximum_fusion.1.q0), channel_id=1, source_target_pairs={{0,16},{8,24},{16,0},{24,8},{1,17},{9,25},{17,1},{25,9},{2,18},{10... | collective-permute-start | bytes 884744 | tf_op jit(solution)/shard_map/ppermute | solution.py:400
  22.0 15.5 %collective-permute-start.18 = (bf16[4,4,16,576]{3,2,1,0:T(8,128)(2,1)S(1)}, bf16[4,4,16,576]{3,2,1,0:T(8,128)(2,1)S(1)}, u32[]{:S(2)}, u32[]{:S(2)}) collective-permute-start(bf16[4,4,16,576]{3,2,1,0:T(8,128)(2,1)S(1)} %pad_maximum_fusion.1.q0), channel_id=1, source_target_pairs={{0,24},{8,0},{16,8},{24,16},{1,25},{9,1},{17,9},{25,17},{2,26},{10... | collective-permute-start | bytes 884744 | tf_op jit(solution)/shard_map/ppermute | solution.py:400
  22.7 26.7 %collective-permute-start.6 = (bf16[4,4,16,576]{3,2,1,0:T(8,128)(2,1)S(1)}, bf16[4,4,16,576]{3,2,1,0:T(8,128)(2,1)S(1)}, u32[]{:S(2)}, u32[]{:S(2)}) collective-permute-start(bf16[4,4,16,576]{3,2,1,0:T(8,128)(2,1)S(1)} %pad_maximum_fusion.q0), channel_id=1, source_target_pairs={{0,2},{2,4},{4,6},{6,0},{1,3},{3,5},{5,7},{7,1},{8,10},{10,12},{12... | collective-permute-start | bytes 884744 | tf_op jit(solution)/shard_map/ppermute | solution.py:400
  28.4 22.0 %collective-permute-start.7 = (bf16[4,4,16,576]{3,2,1,0:T(8,128)(2,1)S(1)}, bf16[4,4,16,576]{3,2,1,0:T(8,128)(2,1)S(1)}, u32[]{:S(2)}, u32[]{:S(2)}) collective-permute-start(bf16[4,4,16,576]{3,2,1,0:T(8,128)(2,1)S(1)} %pad_maximum_fusion.q0), channel_id=1, source_target_pairs={{0,4},{2,6},{4,0},{6,2},{1,5},{3,7},{5,1},{7,3},{8,12},{10,14},{12... | collective-permute-start | bytes 884744 | tf_op jit(solution)/shard_map/ppermute | solution.py:400
  35.3 15.2 %collective-permute-start.8 = (bf16[4,4,16,576]{3,2,1,0:T(8,128)(2,1)S(1)}, bf16[4,4,16,576]{3,2,1,0:T(8,128)(2,1)S(1)}, u32[]{:S(2)}, u32[]{:S(2)}) collective-permute-start(bf16[4,4,16,576]{3,2,1,0:T(8,128)(2,1)S(1)} %pad_maximum_fusion.q0), channel_id=1, source_target_pairs={{0,6},{2,0},{4,2},{6,4},{1,7},{3,1},{5,3},{7,5},{8,14},{10,8},{12,... | collective-permute-start | bytes 884744 | tf_op jit(solution)/shard_map/ppermute | solution.py:400
  48.3 15.6 %collective-permute-start.19 = (bf16[4,17,16,128]{3,2,1,0:T(8,128)(2,1)S(1)}, bf16[4,17,16,128]{3,2,1,0:T(8,128)(2,1)S(1)}, u32[]{:S(2)}, u32[]{:S(2)}) collective-permute-start(bf16[4,17,16,128]{3,2,1,0:T(8,128)(2,1)S(1)} %get-tuple-element.46), channel_id=1, source_target_pairs={{0,24},{8,0},{16,8},{24,16},{1,25},{9,1},{17,9},{25,17},{2,26},{10... | collective-permute-start | bytes 835592 | tf_op jit(solution)/shard_map/ppermute | solution.py:400
  48.3 16.3 %collective-permute-start.20 = (bf16[4,17,16,128]{3,2,1,0:T(8,128)(2,1)S(1)}, bf16[4,17,16,128]{3,2,1,0:T(8,128)(2,1)S(1)}, u32[]{:S(2)}, u32[]{:S(2)}) collective-permute-start(bf16[4,17,16,128]{3,2,1,0:T(8,128)(2,1)S(1)} %get-tuple-element.47), channel_id=1, source_target_pairs={{0,16},{8,24},{16,0},{24,8},{1,17},{9,25},{17,1},{25,9},{2,18},{10... | collective-permute-start | bytes 835592 | tf_op jit(solution)/shard_map/ppermute | solution.py:400
  49.4 33.8 %copy-start.3 = (bf16[32,4,576]{2,1,0:T(4,128)(2,1)S(1)}, bf16[32,4,576]{2,1,0:T(4,128)(2,1)}, u32[]{:S(2)}) copy-start(bf16[32,4,576]{2,1,0:T(4,128)(2,1)} %param.13) | copy-start | bytes 442372
  49.4 39.0 %copy-start = (bf16[4,512,128]{2,1,0:T(8,128)(2,1)S(1)}, bf16[4,512,128]{2,1,0:T(8,128)(2,1)}, u32[]{:S(2)}) copy-start(bf16[4,512,128]{2,1,0:T(8,128)(2,1)} %refs_10_.1) | copy-start | bytes 1572868
  49.4 39.0 %copy-start.1 = (bf16[32,576]{1,0:T(8,128)(2,1)S(1)}, bf16[32,576]{1,0:T(8,128)(2,1)}, u32[]{:S(2)}) copy-start(bf16[32,576]{1,0:T(8,128)(2,1)} %refs_9_.1) | copy-start | bytes 110596
  49.4 15.2 %collective-permute-start.21 = (bf16[4,17,16,128]{3,2,1,0:T(8,128)(2,1)S(1)}, bf16[4,17,16,128]{3,2,1,0:T(8,128)(2,1)S(1)}, u32[]{:S(2)}, u32[]{:S(2)}) collective-permute-start(bf16[4,17,16,128]{3,2,1,0:T(8,128)(2,1)S(1)} %get-tuple-element.48), channel_id=1, source_target_pairs={{0,8},{8,16},{16,24},{24,0},{1,9},{9,17},{17,25},{25,1},{2,10},{10... | collective-permute-start | bytes 835592 | tf_op jit(solution)/shard_map/ppermute | solution.py:400
  61.2 13.8 %collective-permute-start.10 = (bf16[4,17,16,128]{3,2,1,0:T(8,128)(2,1)S(1)}, bf16[4,17,16,128]{3,2,1,0:T(8,128)(2,1)S(1)}, u32[]{:S(2)}, u32[]{:S(2)}) collective-permute-start(bf16[4,17,16,128]{3,2,1,0:T(8,128)(2,1)S(1)} %get-tuple-element.37), channel_id=1, source_target_pairs={{0,6},{2,0},{4,2},{6,4},{1,7},{3,1},{5,3},{7,5},{8,14},{10,8},{12,... | collective-permute-start | bytes 835592 | tf_op jit(solution)/shard_map/ppermute | solution.py:400
  63.7 12.9 %collective-permute-start.11 = (bf16[4,17,16,128]{3,2,1,0:T(8,128)(2,1)S(1)}, bf16[4,17,16,128]{3,2,1,0:T(8,128)(2,1)S(1)}, u32[]{:S(2)}, u32[]{:S(2)}) collective-permute-start(bf16[4,17,16,128]{3,2,1,0:T(8,128)(2,1)S(1)} %get-tuple-element.38), channel_id=1, source_target_pairs={{0,4},{2,6},{4,0},{6,2},{1,5},{3,7},{5,1},{7,3},{8,12},{10,14},{12... | collective-permute-start | bytes 835592 | tf_op jit(solution)/shard_map/ppermute | solution.py:400
  63.8 14.4 %collective-permute-start.12 = (bf16[4,17,16,128]{3,2,1,0:T(8,128)(2,1)S(1)}, bf16[4,17,16,128]{3,2,1,0:T(8,128)(2,1)S(1)}, u32[]{:S(2)}, u32[]{:S(2)}) collective-permute-start(bf16[4,17,16,128]{3,2,1,0:T(8,128)(2,1)S(1)} %get-tuple-element.39), channel_id=1, source_target_pairs={{0,2},{2,4},{4,6},{6,0},{1,3},{3,5},{5,7},{7,1},{8,10},{10,12},{12... | collective-permute-start | bytes 835592 | tf_op jit(solution)/shard_map/ppermute | solution.py:400
  65.5 17.4 %collective-permute-start.22 = (bf16[17,16,128]{2,1,0:T(8,128)(2,1)S(1)}, bf16[17,16,128]{2,1,0:T(8,128)(2,1)S(1)}, u32[]{:S(2)}, u32[]{:S(2)}) collective-permute-start(bf16[17,16,128]{2,1,0:T(8,128)(2,1)S(1)} %get-tuple-element.50), channel_id=1, source_target_pairs={{0,6},{2,0},{4,2},{6,4},{1,7},{3,1},{5,3},{7,5},{8,14},{10,8},{12,... | collective-permute-start | bytes 208904 | tf_op jit(solution)/shard_map/ppermute | solution.py:400
  68.0 15.3 %collective-permute-start.23 = (bf16[17,16,128]{2,1,0:T(8,128)(2,1)S(1)}, bf16[17,16,128]{2,1,0:T(8,128)(2,1)S(1)}, u32[]{:S(2)}, u32[]{:S(2)}) collective-permute-start(bf16[17,16,128]{2,1,0:T(8,128)(2,1)S(1)} %get-tuple-element.51), channel_id=1, source_target_pairs={{0,4},{2,6},{4,0},{6,2},{1,5},{3,7},{5,1},{7,3},{8,12},{10,14},{12... | collective-permute-start | bytes 208904 | tf_op jit(solution)/shard_map/ppermute | solution.py:400
  75.0 8.3 %collective-permute-start.24 = (bf16[17,16,128]{2,1,0:T(8,128)(2,1)S(1)}, bf16[17,16,128]{2,1,0:T(8,128)(2,1)S(1)}, u32[]{:S(2)}, u32[]{:S(2)}) collective-permute-start(bf16[17,16,128]{2,1,0:T(8,128)(2,1)S(1)} %get-tuple-element.52), channel_id=1, source_target_pairs={{0,2},{2,4},{4,6},{6,0},{1,3},{3,5},{5,7},{7,1},{8,10},{10,12},{12... | collective-permute-start | bytes 208904 | tf_op jit(solution)/shard_map/ppermute | solution.py:400
  79.1 4.7 %collective-permute-start.13 = (bf16[17,16,128]{2,1,0:T(8,128)(2,1)S(1)}, bf16[17,16,128]{2,1,0:T(8,128)(2,1)S(1)}, u32[]{:S(2)}, u32[]{:S(2)}) collective-permute-start(bf16[17,16,128]{2,1,0:T(8,128)(2,1)S(1)} %get-tuple-element.41), channel_id=1, source_target_pairs={{0,24},{8,0},{16,8},{24,16},{1,25},{9,1},{17,9},{25,17},{2,26},{10... | collective-permute-start | bytes 208904 | tf_op jit(solution)/shard_map/ppermute | solution.py:400
  81.5 5.9 %collective-permute-start.14 = (bf16[17,16,128]{2,1,0:T(8,128)(2,1)S(1)}, bf16[17,16,128]{2,1,0:T(8,128)(2,1)S(1)}, u32[]{:S(2)}, u32[]{:S(2)}) collective-permute-start(bf16[17,16,128]{2,1,0:T(8,128)(2,1)S(1)} %get-tuple-element.42), channel_id=1, source_target_pairs={{0,16},{8,24},{16,0},{24,8},{1,17},{9,25},{17,1},{25,9},{2,18},{10... | collective-permute-start | bytes 208904 | tf_op jit(solution)/shard_map/ppermute | solution.py:400
  82.9 5.5 %collective-permute-start.15 = (bf16[17,16,128]{2,1,0:T(8,128)(2,1)S(1)}, bf16[17,16,128]{2,1,0:T(8,128)(2,1)S(1)}, u32[]{:S(2)}, u32[]{:S(2)}) collective-permute-start(bf16[17,16,128]{2,1,0:T(8,128)(2,1)S(1)} %get-tuple-element.43), channel_id=1, source_target_pairs={{0,8},{8,16},{16,24},{24,0},{1,9},{9,17},{17,25},{25,1},{2,10},{10... | collective-permute-start | bytes 208904 | tf_op jit(solution)/shard_map/ppermute | solution.py:400
  88.4 10.7 %copy-start.6 = (bf16[1,7168]{1,0:T(2,128)(2,1)S(1)}, bf16[1,7168]{1,0:T(2,128)(2,1)}, u32[]{:S(2)}) copy-start(bf16[1,7168]{1,0:T(2,128)(2,1)} %param.19) | copy-start | bytes 43012
  88.4 10.9 %copy-start.5 = (f32[7168]{0:T(1024)S(1)}, f32[7168]{0:T(1024)}, u32[]{:S(2)}) copy-start(f32[7168]{0:T(1024)} %param.20) | copy-start | bytes 86020
  88.4 27.7 %copy-start.4 = (bf16[7168,16]{0,1:T(8,128)(2,1)S(1)}, bf16[7168,16]{0,1:T(8,128)(2,1)}, u32[]{:S(2)}) copy-start(bf16[7168,16]{0,1:T(8,128)(2,1)} %param.21) | copy-start | bytes 688132
  93.2 22.9 %copy-start.2 = (s32[1,8]{1,0:T(1,128)S(1)}, s32[1,8]{1,0:T(1,128)}, u32[]{:S(2)}) copy-start(s32[1,8]{1,0:T(1,128)} %routes_ref.1) | copy-start | bytes 100
  93.2 1.6 collective-permute-start.25
  95.5 12.2 %all-to-all-start = ((bf16[16,8,896]{2,1,0:T(8,128)(2,1)}), bf16[16,8,896]{2,1,0:T(8,128)(2,1)S(1)}, u32[]{:S(2)}, u32[]{:S(2)}) async-start(bf16[16,8,896]{2,1,0:T(8,128)(2,1)} %add_convert_fusion.1), calls=%async_computation | async-start | bytes 458752 | tf_op jit(solution)/shard_map/all_to_all | solution.py:449
  108.9 23.9 %all-to-all-start.1 = ((bf16[64,8,896]{2,1,0:T(8,128)(2,1)}), bf16[64,8,896]{2,1,0:T(8,128)(2,1)S(1)}, u32[]{:S(2)}, u32[]{:S(2)}) async-start(bf16[64,8,896]{2,1,0:T(8,128)(2,1)} %get-tuple-element.56), calls=%async_computation.1 | async-start | bytes 1835008 | tf_op jit(solution)/shard_map/all_to_all | solution.py:457
  132.7 3.2 %collective-permute-start.26 = (bf16[64,8,896]{2,1,0:T(8,128)(2,1)S(1)}, bf16[64,8,896]{2,1,0:T(8,128)(2,1)S(1)}, u32[]{:S(2)}, u32[]{:S(2)}) collective-permute-start(bf16[64,8,896]{2,1,0:T(8,128)(2,1)S(1)} %all-to-all-done.1.own_ref), channel_id=1, source_target_pairs={{0,1},{1,0},{2,3},{3,2},{4,5},{5,4},{6,7},{7,6},{8,9},{9,8},{10,11... | collective-permute-start | bytes 2752520 | tf_op jit(solution)/shard_map/ppermute | solution.py:400
  140.8 2.7 %collective-permute-start.27 = (bf16[64,8,896]{2,1,0:T(8,128)(2,1)S(1)}, bf16[64,8,896]{2,1,0:T(8,128)(2,1)S(1)}, u32[]{:S(2)}, u32[]{:S(2)}) collective-permute-start(bf16[64,8,896]{2,1,0:T(8,128)(2,1)S(1)} %get-tuple-element.65), channel_id=1, source_target_pairs={{0,1},{1,0},{2,3},{3,2},{4,5},{5,4},{6,7},{7,6},{8,9},{9,8},{10,11... | collective-permute-start | bytes 2752520 | tf_op jit(solution)/shard_map/ppermute | solution.py:400
  144.7 22.8 %all-to-all-start.2 = ((bf16[64,8,896]{2,1,0:T(8,128)(2,1)}), bf16[64,8,896]{2,1,0:T(8,128)(2,1)S(1)}, u32[]{:S(2)}, u32[]{:S(2)}) async-start(bf16[64,8,896]{2,1,0:T(8,128)(2,1)} %add_convert_fusion), calls=%async_computation.2 | async-start | bytes 1835008 | tf_op jit(solution)/shard_map/all_to_all | solution.py:462

commit v4 on v3

--- a/solution.py
+++ b/solution.py
@@ -149,15 +149,9 @@
 
 def project_kernel(core_ref, *refs, count):
     first, second = refs[0:4], refs[4:8]
-    q_ref, keys_ref, up_ref, w_hbm, kept_ref, given_ref, w_ref, rows_ref, sems = refs[8:]
+    q_ref, keys_ref, up_ref, w_ref, kept_ref, given_ref, rows_ref = refs[8:]
     chunk = kept_ref.shape[2]
 
-    def fetch(k):
-        window = pl.ds(k * chunk, chunk)
-        return pltpu.make_async_copy(w_hbm.at[:, window], w_ref.at[:, window], sems.at[k])
-
-    for k in range(SPAN):
-        fetch(k).start()
     tops, totals, results = [], [], []
     for half in (first, second):
         weights, top, total = merged_stats([ref[4 * count].astype(f32) for ref in half])
@@ -211,7 +205,6 @@
         values.append(jnp.dot(pick, head_value, preferred_element_type=f32).astype(bf16))
     values = jnp.concatenate(values, axis=1)
     for k in range(SPAN):
-        fetch(k).wait()
         block = jnp.dot(values, w_ref[:, k * chunk : (k + 1) * chunk], preferred_element_type=f32)
         for piece in range(chunk // LANES):
             rows_ref[piece, pl.ds(k, grouped, stride=SPAN), :] = block[:, piece * LANES : (piece + 1) * LANES]
@@ -233,16 +226,14 @@
     return pl.pallas_call(
         functools.partial(project_kernel, count=count),
         out_shape=[out, out],
-        in_specs=[pl.BlockSpec(memory_space=pltpu.SMEM)] + [inside] * 11 + [pl.BlockSpec(memory_space=pltpu.HBM)],
+        in_specs=[pl.BlockSpec(memory_space=pltpu.SMEM)] + [inside] * 12,
         out_specs=[inside] * 2,
         scratch_shapes=[
-            pltpu.VMEM(w_out.shape, bf16),
             pltpu.VMEM((width // SPAN // LANES, grouped * SPAN, LANES), f32),
-            pltpu.SemaphoreType.DMA((SPAN,)),
         ],
         compiler_params=pltpu.CompilerParams(vmem_limit_bytes=32 << 20),
         name="project",
-    )(core, *first, *second, own_query, new_keys, value_up, pltpu.with_memory_space_constraint(w_out, pltpu.HBM))
+    )(core, *first, *second, own_query, new_keys, value_up, w_out)
 
 
 def spread_kernel(arrived_ref, residual_ref, gain_ref, attn_ref, stream_ref, normed_ref, rows_ref):
@@ -440,10 +431,14 @@
     scalars = jnp.concatenate([jnp.stack([ctx, ctx ^ 1]).astype(jnp.int32), lengths])
     out_a = attend(scalars, queries_a, cache, sibling_cache, 0, count)
     out_b = attend(scalars, queries_b, cache, sibling_cache, count, count)
-    final_a = return_shifts(merge(return_shifts(out_a, "z"), count), "x")
+    half_a = merge(return_shifts(out_a, "z"), count)
+    half_a = list(half_a)
+    half_a[0], held_out = lax.optimization_barrier((half_a[0], w_out))
+    (held_out,) = hold(held_out)
+    final_a = return_shifts(half_a, "x")
     final_b = return_shifts(merge(return_shifts(out_b, "x"), count), "z")
     kept, given = project(
-        core.astype(jnp.int32).reshape(1), final_a, final_b, own_query, new_keys, value_up_weight, w_out, count
+        core.astype(jnp.int32).reshape(1), final_a, final_b, own_query, new_keys, value_up_weight, held_out, count
     )
     chip_sum = (kept.astype(f32) + shift_by(given, "c", 1).astype(f32)).astype(bf16)
     arrived = lax.all_to_all(chip_sum, ("x", "z"), split_axis=0, concat_axis=0, tiled=True)

time: 169 us -> 170 us (level)
  starting transfers between devices: 53.5 us -> 50.5 us
  waiting for transfers between devices: 70.6 us -> 73.6 us
    ppermute x28, starting transfers between devices: 38 us -> 33.9 us  [shift_by(): lax.ppermute(value, axis, [(i, (i + offset) % size) for i in range(size)])]
    ppermute x28, waiting for transfers between devices: 28.7 us -> 32.1 us  [shift_by(): lax.ppermute(value, axis, [(i, (i + offset) % size) for i in range(size)])]
    pallas_call x1 -> x2, Pallas kernels: 3.21 us -> 6.43 us  [hold(): pl.pallas_call(hold_kernel, out_shape=[pltpu.VMEM(w.shape, w.dtype) for w...]
    pallas_call x1, Pallas kernels: 4.74 us -> 2.8 us  [project(): pl.pallas_call(functools.partial(project_kernel, count=count), out_shape=...]
  transfers between devices with their start and end apart: 31 -> 31, of which waited for: 15 -> 12; matrix products, arithmetic and copies ran while one was open for 2% -> 2% of each run, Pallas kernels for 16% -> 18%
where the time goes in v4:
time: 170 us
  waiting for transfers between devices  73.6 us (43%)
  starting transfers between devices  50.5 us (30%)
  Pallas kernels  39.1 us (23%)
  other arithmetic  2.88 us (2%)
  local copies, waits for them, and re-layouts  2.61 us (2%)
    ppermute x28, starting transfers between devices, shift_by(): lax.ppermute(value, axis, [(i, (i + offset) % size) for i in range(size)])  33.9 us
    ppermute x28, waiting for transfers between devices, shift_by(): lax.ppermute(value, axis, [(i, (i + offset) % size) for i in range(size)])  32.1 us
    pallas_call x2, Pallas kernels, attend(): pl.pallas_call(functools.partial(attend_kernel, first=first, count=count)...  21.4 us
    all_to_all x1, waiting for transfers between devices, local(): lax.all_to_all(chip_out, ('y', 'x', 'z'), split_axis=0, concat_axis=0, ti...  17.5 us
    all_to_all x1, waiting for transfers between devices, local(): lax.all_to_all(rows, ('y', 'x', 'z'), split_axis=0, concat_axis=0, tiled=...  15.8 us
    all_to_all x1, waiting for transfers between devices, local(): lax.all_to_all(chip_sum, ('x', 'z'), split_axis=0, concat_axis=0, tiled=T...  8.31 us
    all_to_all x1, starting transfers between devices, local(): lax.all_to_all(rows, ('y', 'x', 'z'), split_axis=0, concat_axis=0, tiled=...  7.14 us
    pallas_call x2, Pallas kernels, hold(): pl.pallas_call(hold_kernel, out_shape=[pltpu.VMEM(w.shape, w.dtype) for w...  6.43 us
  transfers between devices with their start and end apart: 31, of which 12 were waited for; matrix products, arithmetic and copies ran while one was open for 2% of the time, Pallas kernels for 18%

profile of v4, /device:TPU:0, one launch (start us, length us, event | category | flops | bytes accessed | tf_op | source)
XLA Modules:
  0.0 169.7 jit_solution(9630599445422459718)
XLA Ops:
  0.6 0.1 collective-permute-start.9
  0.7 1.0 fusion
  1.8 2.9 %collective-permute-start.2 = (bf16[4,16,576]{2,1,0:T(8,128)(2,1)S(1)}, bf16[4,16,576]{2,1,0:T(8,128)(2,1)S(1)}, u32[]{:S(2)}, u32[]{:S(2)}) collective-permute-start(bf16[4,16,576]{2,1,0:T(8,128)(2,1)S(1)} %slice.13), channel_id=1, source_target_pairs={{0,24},{8,0},{16,8},{24,16},{1,25},{9,1},{17,9},{25,17},{2,26},{10... | collective-permute-start | bytes 221192 | tf_op jit(solution)/shard_map/ppermute | solution.py:391
  4.7 0.8 collective-permute-start.1
  5.5 0.9 collective-permute-start
  6.4 4.1 %collective-permute-start.5 = (bf16[4,16,576]{2,1,0:T(8,128)(2,1)S(1)}, bf16[4,16,576]{2,1,0:T(8,128)(2,1)S(1)}, u32[]{:S(2)}, u32[]{:S(2)}) collective-permute-start(bf16[4,16,576]{2,1,0:T(8,128)(2,1)S(1)} %slice.15), channel_id=1, source_target_pairs={{0,6},{2,0},{4,2},{6,4},{1,7},{3,1},{5,3},{7,5},{8,14},{10,8},{12,... | collective-permute-start | bytes 221192 | tf_op jit(solution)/shard_map/ppermute | solution.py:391
  10.6 2.1 %collective-permute-start.4 = (bf16[4,16,576]{2,1,0:T(8,128)(2,1)S(1)}, bf16[4,16,576]{2,1,0:T(8,128)(2,1)S(1)}, u32[]{:S(2)}, u32[]{:S(2)}) collective-permute-start(bf16[4,16,576]{2,1,0:T(8,128)(2,1)S(1)} %slice.15), channel_id=1, source_target_pairs={{0,4},{2,6},{4,0},{6,2},{1,5},{3,7},{5,1},{7,3},{8,12},{10,14},{12... | collective-permute-start | bytes 221192 | tf_op jit(solution)/shard_map/ppermute | solution.py:391
  12.7 1.0 collective-permute-start.3
  13.7 0.1 pad_maximum_fusion.q0
  13.8 3.3 %collective-permute-done.4 = bf16[4,16,576]{2,1,0:T(8,128)(2,1)S(1)} collective-permute-done((bf16[4,16,576]{2,1,0:T(8,128)(2,1)S(1)}, bf16[4,16,576]{2,1,0:T(8,128)(2,1)S(1)}, u32[]{:S(2)}, u32[]{:S(2)}) %collective-permute-start.4) | collective-permute-done | bytes 73760 | tf_op jit(solution)/shard_map/ppermute | solution.py:391
  17.1 1.2 collective-permute-done.3
  18.4 0.1 pad_maximum_fusion.1.q0
  18.5 0.1 collective-permute-start.6
  18.5 3.0 %collective-permute-start.7 = (bf16[4,4,16,576]{3,2,1,0:T(8,128)(2,1)S(1)}, bf16[4,4,16,576]{3,2,1,0:T(8,128)(2,1)S(1)}, u32[]{:S(2)}, u32[]{:S(2)}) collective-permute-start(bf16[4,4,16,576]{3,2,1,0:T(8,128)(2,1)S(1)} %pad_maximum_fusion.q0), channel_id=1, source_target_pairs={{0,4},{2,6},{4,0},{6,2},{1,5},{3,7},{5,1},{7,3},{8,12},{10,14},{12... | collective-permute-start | bytes 884744 | tf_op jit(solution)/shard_map/ppermute | solution.py:391
  21.5 1.1 collective-permute-start.8
  22.6 0.6 collective-permute-start.16
  23.2 12.1 %collective-permute-done.6.q1 = bf16[4,4,16,576]{3,2,1,0:T(8,128)(2,1)S(1)} collective-permute-done((bf16[4,4,16,576]{3,2,1,0:T(8,128)(2,1)S(1)}, bf16[4,4,16,576]{3,2,1,0:T(8,128)(2,1)S(1)}, u32[]{:S(2)}, u32[]{:S(2)}) %collective-permute-start.6) | collective-permute-done | bytes 294944 | tf_op jit(solution)/shard_map/ppermute | solution.py:391
  35.3 1.2 collective-permute-start.17
  36.5 1.8 %collective-permute-start.18 = (bf16[4,4,16,576]{3,2,1,0:T(8,128)(2,1)S(1)}, bf16[4,4,16,576]{3,2,1,0:T(8,128)(2,1)S(1)}, u32[]{:S(2)}, u32[]{:S(2)}) collective-permute-start(bf16[4,4,16,576]{3,2,1,0:T(8,128)(2,1)S(1)} %pad_maximum_fusion.1.q0), channel_id=1, source_target_pairs={{0,24},{8,0},{16,8},{24,16},{1,25},{9,1},{17,9},{25,17},{2,26},{10... | collective-permute-start | bytes 884744 | tf_op jit(solution)/shard_map/ppermute | solution.py:391
  38.4 0.7 pad_add_fusion.scalars_ref
  39.1 10.7 %attend.2 = (bf16[4,17,16,128]{3,2,1,0:T(8,128)(2,1)S(1)}, bf16[4,17,16,128]{3,2,1,0:T(8,128)(2,1)S(1)}, bf16[4,17,16,128]{3,2,1,0:T(8,128)(2,1)S(1)}, bf16[4,17,16,128]{3,2,1,0:T(8,128)(2,1)S(1)}) custom-call(s32[10]{0:T(128)S(1)} %pad_add_fusion.scalars_ref, bf16[4,4,16,576]{3,2,1,0:T(8,128)(2,1)S(1)} %pad_maximum_fusion.q0, ...), custom_call_target="tpu_custom_call" | custom-call | tf_op jit(solution)/shard_map/attend/pallas_call | solution.py:96
  49.8 0.1 collective-permute-start.10
  49.9 0.7 collective-permute-start.11
  50.6 1.4 collective-permute-start.12
  52.0 10.7 %attend.3 = (bf16[4,17,16,128]{3,2,1,0:T(8,128)(2,1)S(1)}, bf16[4,17,16,128]{3,2,1,0:T(8,128)(2,1)S(1)}, bf16[4,17,16,128]{3,2,1,0:T(8,128)(2,1)S(1)}, bf16[4,17,16,128]{3,2,1,0:T(8,128)(2,1)S(1)}) custom-call(s32[10]{0:T(128)S(1)} %pad_add_fusion.scalars_ref, bf16[4,4,16,576]{3,2,1,0:T(8,128)(2,1)S(1)} %pad_maximum_fusion.1.q0, ...), custom_call_target="tpu_custom_call" | custom-call | tf_op jit(solution)/shard_map/attend/pallas_call | solution.py:96
  62.7 1.3 collective-permute-start.19
  64.1 1.6 collective-permute-start.20
  65.7 1.3 collective-permute-start.21
  67.1 0.8 merge.2
  67.9 2.0 %collective-permute-start.13 = (bf16[17,16,128]{2,1,0:T(8,128)(2,1)S(1)}, bf16[17,16,128]{2,1,0:T(8,128)(2,1)S(1)}, u32[]{:S(2)}, u32[]{:S(2)}) collective-permute-start(bf16[17,16,128]{2,1,0:T(8,128)(2,1)S(1)} %get-tuple-element.44), channel_id=1, source_target_pairs={{0,24},{8,0},{16,8},{24,16},{1,25},{9,1},{17,9},{25,17},{2,26},{10... | collective-permute-start | bytes 208904 | tf_op jit(solution)/shard_map/ppermute | solution.py:391
  69.9 0.7 collective-permute-start.14
  70.5 7.3 %collective-permute-done.19.a1 = bf16[4,17,16,128]{3,2,1,0:T(8,128)(2,1)S(1)} collective-permute-done((bf16[4,17,16,128]{3,2,1,0:T(8,128)(2,1)S(1)}, bf16[4,17,16,128]{3,2,1,0:T(8,128)(2,1)S(1)}, u32[]{:S(2)}, u32[]{:S(2)}) %collective-permute-start.19) | collective-permute-done | bytes 278560 | tf_op jit(solution)/shard_map/ppermute | solution.py:391
  77.8 2.3 %collective-permute-done.21.a3 = bf16[4,17,16,128]{3,2,1,0:T(8,128)(2,1)S(1)} collective-permute-done((bf16[4,17,16,128]{3,2,1,0:T(8,128)(2,1)S(1)}, bf16[4,17,16,128]{3,2,1,0:T(8,128)(2,1)S(1)}, u32[]{:S(2)}, u32[]{:S(2)}) %collective-permute-start.21) | collective-permute-done | bytes 278560 | tf_op jit(solution)/shard_map/ppermute | solution.py:391
  80.2 0.8 merge.3
  81.0 2.8 %collective-permute-start.22 = (bf16[17,16,128]{2,1,0:T(8,128)(2,1)S(1)}, bf16[17,16,128]{2,1,0:T(8,128)(2,1)S(1)}, u32[]{:S(2)}, u32[]{:S(2)}) collective-permute-start(bf16[17,16,128]{2,1,0:T(8,128)(2,1)S(1)} %get-tuple-element.53), channel_id=1, source_target_pairs={{0,6},{2,0},{4,2},{6,4},{1,7},{3,1},{5,3},{7,5},{8,14},{10,8},{12,... | collective-permute-start | bytes 208904 | tf_op jit(solution)/shard_map/ppermute | solution.py:391
  83.8 1.6 collective-permute-start.23
  85.4 0.1 reshape.30.refs_8_
  85.5 0.0 copy-start
  85.5 0.0 copy-start.1
  85.5 3.2 %hold.2.refs_11_ = bf16[512,7168]{1,0:T(8,128)(2,1)S(1)} custom-call(bf16[512,7168]{1,0:T(8,128)(2,1)} %refs_0_), custom_call_target="tpu_custom_call" | custom-call | tf_op jit(solution)/shard_map/hold/pallas_call | solution.py:304
  88.8 0.8 collective-permute-done.23.refs_6_
  89.6 1.3 collective-permute-done.24.refs_7_
  91.0 0.0 copy-start.4
  91.0 2.8 %project.1 = (bf16[16,8,896]{2,1,0:T(8,128)(2,1)S(1)}, bf16[16,8,896]{2,1,0:T(8,128)(2,1)S(1)}) custom-call(s32[1]{0:T(128)} %bitcast.core_ref, bf16[17,16,128]{2,1,0:T(8,128)(2,1)S(1)} %get-tuple-element.43.refs_0_, bf16[17,16,128]{2,1,0:T(8,128)(2,1)S(1)} %collective-permute-done.13.refs_1_, bf16[17,16,128]{2,1,0:T(8,128)(2,1)S(1)} %collective-permute-done.14.refs_2_, ...), custom_call_target="tpu_custom_call" | custom-call | tf_op jit(solution)/shard_map/project/pallas_call | solution.py:226
  93.8 0.1 collective-permute-start.25
  93.9 1.5 collective-permute-done.25
  95.3 0.7 add_convert_fusion.1
  96.1 4.7 %all-to-all-start = ((bf16[16,8,896]{2,1,0:T(8,128)(2,1)}), bf16[16,8,896]{2,1,0:T(8,128)(2,1)S(1)}, u32[]{:S(2)}, u32[]{:S(2)}) async-start(bf16[16,8,896]{2,1,0:T(8,128)(2,1)} %add_convert_fusion.1), calls=%async_computation | async-start | bytes 458752 | tf_op jit(solution)/shard_map/all_to_all | solution.py:444
  100.9 0.1 reduce
  101.0 8.3 %all-to-all-done.arrived_ref = bf16[16,8,896]{2,1,0:T(8,128)(2,1)S(1)} async-done(((bf16[16,8,896]{2,1,0:T(8,128)(2,1)}), bf16[16,8,896]{2,1,0:T(8,128)(2,1)S(1)}, u32[]{:S(2)}, u32[]{:S(2)}) %all-to-all-start) | async-done | bytes 229408 | tf_op jit(solution)/shard_map/all_to_all | solution.py:444
  109.3 1.1 spread.1
  110.5 7.1 %all-to-all-start.1 = ((bf16[64,8,896]{2,1,0:T(8,128)(2,1)}), bf16[64,8,896]{2,1,0:T(8,128)(2,1)S(1)}, u32[]{:S(2)}, u32[]{:S(2)}) async-start(bf16[64,8,896]{2,1,0:T(8,128)(2,1)} %get-tuple-element.60), calls=%async_computation.1 | async-start | bytes 1835008 | tf_op jit(solution)/shard_map/all_to_all | solution.py:452
  117.7 0.7 route.1.coefficient_ref
  118.4 15.8 %all-to-all-done.1.own_ref = bf16[64,8,896]{2,1,0:T(8,128)(2,1)S(1)} async-done(((bf16[64,8,896]{2,1,0:T(8,128)(2,1)}), bf16[64,8,896]{2,1,0:T(8,128)(2,1)S(1)}, u32[]{:S(2)}, u32[]{:S(2)}) %all-to-all-start.1) | async-done | bytes 917536 | tf_op jit(solution)/shard_map/all_to_all | solution.py:452
  134.1 3.2 %hold.3 = (bf16[7168,256]{1,0:T(8,128)(2,1)S(1)}, bf16[7168,256]{1,0:T(8,128)(2,1)S(1)}) custom-call(bf16[7168,256]{1,0:T(8,128)(2,1)} %refs_0_.1, bf16[7168,256]{1,0:T(8,128)(2,1)} %refs_1_), custom_call_target="tpu_custom_call" | custom-call | tf_op jit(solution)/shard_map/hold/pallas_call | solution.py:304
  137.4 4.8 %experts.1 = (bf16[64,8,896]{2,1,0:T(8,128)(2,1)S(1)}, bf16[64,8,896]{2,1,0:T(8,128)(2,1)S(1)}) custom-call(bf16[64,8,896]{2,1,0:T(8,128)(2,1)S(1)} %all-to-all-done.1.own_ref, bf16[64,8,896]{2,1,0:T(8,128)(2,1)S(1)} %collective-permute-done.26.sib_ref, bf16[7168,256]{1,0:T(8,128)(2,1)S(1)} %get-tuple-element.66.gate_ref, ...), custom_call_target="tpu_custom_call" | custom-call | tf_op jit(solution)/shard_map/experts/pallas_call | solution.py:354
  142.2 0.6 collective-permute-start.27
  142.8 2.1 %collective-permute-done.27 = bf16[64,8,896]{2,1,0:T(8,128)(2,1)S(1)} collective-permute-done((bf16[64,8,896]{2,1,0:T(8,128)(2,1)S(1)}, bf16[64,8,896]{2,1,0:T(8,128)(2,1)S(1)}, u32[]{:S(2)}, u32[]{:S(2)}) %collective-permute-start.27) | collective-permute-done | bytes 917536 | tf_op jit(solution)/shard_map/ppermute | solution.py:391
  144.9 1.2 add_convert_fusion
  146.1 4.7 %all-to-all-start.2 = ((bf16[64,8,896]{2,1,0:T(8,128)(2,1)}), bf16[64,8,896]{2,1,0:T(8,128)(2,1)S(1)}, u32[]{:S(2)}, u32[]{:S(2)}) async-start(bf16[64,8,896]{2,1,0:T(8,128)(2,1)} %add_convert_fusion), calls=%async_computation.2 | async-start | bytes 1835008 | tf_op jit(solution)/shard_map/all_to_all | solution.py:457
  150.8 0.6 copy.15
  151.4 17.5 %all-to-all-done.2.returned_ref = bf16[64,8,896]{2,1,0:T(8,128)(2,1)S(1)} async-done(((bf16[64,8,896]{2,1,0:T(8,128)(2,1)}), bf16[64,8,896]{2,1,0:T(8,128)(2,1)S(1)}, u32[]{:S(2)}, u32[]{:S(2)}) %all-to-all-start.2) | async-done | bytes 917536 | tf_op jit(solution)/shard_map/all_to_all | solution.py:457
  168.9 0.1 gather.1
  169.1 0.6 copy.17
  (40 shorter events, 0.3 us)
Async XLA Ops:
  0.6 38.5 %collective-permute-start.9 = (bf16[8,576,1024]{2,1,0:T(8,128)(2,1)}, bf16[8,576,1024]{2,1,0:T(8,128)(2,1)}, u32[]{:S(2)}, u32[]{:S(2)}) collective-permute-start(bf16[8,576,1024]{2,1,0:T(8,128)(2,1)} %bitcast.22), channel_id=1, source_target_pairs={{0,1},{1,0},{2,3},{3,2},{4,5},{5,4},{6,7},{7,6},{8,9},{9,8},{10,11... | collective-permute-start | bytes 28311560 | tf_op jit(solution)/shard_map/ppermute | solution.py:391
  1.8 8.8 %collective-permute-start.2 = (bf16[4,16,576]{2,1,0:T(8,128)(2,1)S(1)}, bf16[4,16,576]{2,1,0:T(8,128)(2,1)S(1)}, u32[]{:S(2)}, u32[]{:S(2)}) collective-permute-start(bf16[4,16,576]{2,1,0:T(8,128)(2,1)S(1)} %slice.13), channel_id=1, source_target_pairs={{0,24},{8,0},{16,8},{24,16},{1,25},{9,1},{17,9},{25,17},{2,26},{10... | collective-permute-start | bytes 221192 | tf_op jit(solution)/shard_map/ppermute | solution.py:391
  4.7 8.0 %collective-permute-start.1 = (bf16[4,16,576]{2,1,0:T(8,128)(2,1)S(1)}, bf16[4,16,576]{2,1,0:T(8,128)(2,1)S(1)}, u32[]{:S(2)}, u32[]{:S(2)}) collective-permute-start(bf16[4,16,576]{2,1,0:T(8,128)(2,1)S(1)} %slice.13), channel_id=1, source_target_pairs={{0,16},{8,24},{16,0},{24,8},{1,17},{9,25},{17,1},{25,9},{2,18},{10... | collective-permute-start | bytes 221192 | tf_op jit(solution)/shard_map/ppermute | solution.py:391
  5.5 8.2 %collective-permute-start = (bf16[4,16,576]{2,1,0:T(8,128)(2,1)S(1)}, bf16[4,16,576]{2,1,0:T(8,128)(2,1)S(1)}, u32[]{:S(2)}, u32[]{:S(2)}) collective-permute-start(bf16[4,16,576]{2,1,0:T(8,128)(2,1)S(1)} %slice.13), channel_id=1, source_target_pairs={{0,8},{8,16},{16,24},{24,0},{1,9},{9,17},{17,25},{25,1},{2,10},{10... | collective-permute-start | bytes 221192 | tf_op jit(solution)/shard_map/ppermute | solution.py:391
  6.4 7.4 %collective-permute-start.5 = (bf16[4,16,576]{2,1,0:T(8,128)(2,1)S(1)}, bf16[4,16,576]{2,1,0:T(8,128)(2,1)S(1)}, u32[]{:S(2)}, u32[]{:S(2)}) collective-permute-start(bf16[4,16,576]{2,1,0:T(8,128)(2,1)S(1)} %slice.15), channel_id=1, source_target_pairs={{0,6},{2,0},{4,2},{6,4},{1,7},{3,1},{5,3},{7,5},{8,14},{10,8},{12,... | collective-permute-start | bytes 221192 | tf_op jit(solution)/shard_map/ppermute | solution.py:391
  10.6 6.5 %collective-permute-start.4 = (bf16[4,16,576]{2,1,0:T(8,128)(2,1)S(1)}, bf16[4,16,576]{2,1,0:T(8,128)(2,1)S(1)}, u32[]{:S(2)}, u32[]{:S(2)}) collective-permute-start(bf16[4,16,576]{2,1,0:T(8,128)(2,1)S(1)} %slice.15), channel_id=1, source_target_pairs={{0,4},{2,6},{4,0},{6,2},{1,5},{3,7},{5,1},{7,3},{8,12},{10,14},{12... | collective-permute-start | bytes 221192 | tf_op jit(solution)/shard_map/ppermute | solution.py:391
  12.7 5.7 %collective-permute-start.3 = (bf16[4,16,576]{2,1,0:T(8,128)(2,1)S(1)}, bf16[4,16,576]{2,1,0:T(8,128)(2,1)S(1)}, u32[]{:S(2)}, u32[]{:S(2)}) collective-permute-start(bf16[4,16,576]{2,1,0:T(8,128)(2,1)S(1)} %slice.15), channel_id=1, source_target_pairs={{0,2},{2,4},{4,6},{6,0},{1,3},{3,5},{5,7},{7,1},{8,10},{10,12},{12... | collective-permute-start | bytes 221192 | tf_op jit(solution)/shard_map/ppermute | solution.py:391
  18.5 16.9 %collective-permute-start.6 = (bf16[4,4,16,576]{3,2,1,0:T(8,128)(2,1)S(1)}, bf16[4,4,16,576]{3,2,1,0:T(8,128)(2,1)S(1)}, u32[]{:S(2)}, u32[]{:S(2)}) collective-permute-start(bf16[4,4,16,576]{3,2,1,0:T(8,128)(2,1)S(1)} %pad_maximum_fusion.q0), channel_id=1, source_target_pairs={{0,2},{2,4},{4,6},{6,0},{1,3},{3,5},{5,7},{7,1},{8,10},{10,12},{12... | collective-permute-start | bytes 884744 | tf_op jit(solution)/shard_map/ppermute | solution.py:391
  18.5 18.0 %collective-permute-start.7 = (bf16[4,4,16,576]{3,2,1,0:T(8,128)(2,1)S(1)}, bf16[4,4,16,576]{3,2,1,0:T(8,128)(2,1)S(1)}, u32[]{:S(2)}, u32[]{:S(2)}) collective-permute-start(bf16[4,4,16,576]{3,2,1,0:T(8,128)(2,1)S(1)} %pad_maximum_fusion.q0), channel_id=1, source_target_pairs={{0,4},{2,6},{4,0},{6,2},{1,5},{3,7},{5,1},{7,3},{8,12},{10,14},{12... | collective-permute-start | bytes 884744 | tf_op jit(solution)/shard_map/ppermute | solution.py:391
  21.5 17.6 %collective-permute-start.8 = (bf16[4,4,16,576]{3,2,1,0:T(8,128)(2,1)S(1)}, bf16[4,4,16,576]{3,2,1,0:T(8,128)(2,1)S(1)}, u32[]{:S(2)}, u32[]{:S(2)}) collective-permute-start(bf16[4,4,16,576]{3,2,1,0:T(8,128)(2,1)S(1)} %pad_maximum_fusion.q0), channel_id=1, source_target_pairs={{0,6},{2,0},{4,2},{6,4},{1,7},{3,1},{5,3},{7,5},{8,14},{10,8},{12,... | collective-permute-start | bytes 884744 | tf_op jit(solution)/shard_map/ppermute | solution.py:391
  22.6 28.0 %collective-permute-start.16 = (bf16[4,4,16,576]{3,2,1,0:T(8,128)(2,1)S(1)}, bf16[4,4,16,576]{3,2,1,0:T(8,128)(2,1)S(1)}, u32[]{:S(2)}, u32[]{:S(2)}) collective-permute-start(bf16[4,4,16,576]{3,2,1,0:T(8,128)(2,1)S(1)} %pad_maximum_fusion.1.q0), channel_id=1, source_target_pairs={{0,8},{8,16},{16,24},{24,0},{1,9},{9,17},{17,25},{25,1},{2,10},{10... | collective-permute-start | bytes 884744 | tf_op jit(solution)/shard_map/ppermute | solution.py:391
  35.3 16.7 %collective-permute-start.17 = (bf16[4,4,16,576]{3,2,1,0:T(8,128)(2,1)S(1)}, bf16[4,4,16,576]{3,2,1,0:T(8,128)(2,1)S(1)}, u32[]{:S(2)}, u32[]{:S(2)}) collective-permute-start(bf16[4,4,16,576]{3,2,1,0:T(8,128)(2,1)S(1)} %pad_maximum_fusion.1.q0), channel_id=1, source_target_pairs={{0,16},{8,24},{16,0},{24,8},{1,17},{9,25},{17,1},{25,9},{2,18},{10... | collective-permute-start | bytes 884744 | tf_op jit(solution)/shard_map/ppermute | solution.py:391
  36.5 15.5 %collective-permute-start.18 = (bf16[4,4,16,576]{3,2,1,0:T(8,128)(2,1)S(1)}, bf16[4,4,16,576]{3,2,1,0:T(8,128)(2,1)S(1)}, u32[]{:S(2)}, u32[]{:S(2)}) collective-permute-start(bf16[4,4,16,576]{3,2,1,0:T(8,128)(2,1)S(1)} %pad_maximum_fusion.1.q0), channel_id=1, source_target_pairs={{0,24},{8,0},{16,8},{24,16},{1,25},{9,1},{17,9},{25,17},{2,26},{10... | collective-permute-start | bytes 884744 | tf_op jit(solution)/shard_map/ppermute | solution.py:391
  49.8 15.9 %collective-permute-start.10 = (bf16[4,17,16,128]{3,2,1,0:T(8,128)(2,1)S(1)}, bf16[4,17,16,128]{3,2,1,0:T(8,128)(2,1)S(1)}, u32[]{:S(2)}, u32[]{:S(2)}) collective-permute-start(bf16[4,17,16,128]{3,2,1,0:T(8,128)(2,1)S(1)} %get-tuple-element.39), channel_id=1, source_target_pairs={{0,6},{2,0},{4,2},{6,4},{1,7},{3,1},{5,3},{7,5},{8,14},{10,8},{12,... | collective-permute-start | bytes 835592 | tf_op jit(solution)/shard_map/ppermute | solution.py:391
  49.9 17.1 %collective-permute-start.11 = (bf16[4,17,16,128]{3,2,1,0:T(8,128)(2,1)S(1)}, bf16[4,17,16,128]{3,2,1,0:T(8,128)(2,1)S(1)}, u32[]{:S(2)}, u32[]{:S(2)}) collective-permute-start(bf16[4,17,16,128]{3,2,1,0:T(8,128)(2,1)S(1)} %get-tuple-element.40), channel_id=1, source_target_pairs={{0,4},{2,6},{4,0},{6,2},{1,5},{3,7},{5,1},{7,3},{8,12},{10,14},{12... | collective-permute-start | bytes 835592 | tf_op jit(solution)/shard_map/ppermute | solution.py:391
  50.6 34.8 %copy-start.3 = (bf16[32,4,576]{2,1,0:T(4,128)(2,1)S(1)}, bf16[32,4,576]{2,1,0:T(4,128)(2,1)}, u32[]{:S(2)}) copy-start(bf16[32,4,576]{2,1,0:T(4,128)(2,1)} %param.13) | copy-start | bytes 442372
  50.6 16.4 %collective-permute-start.12 = (bf16[4,17,16,128]{3,2,1,0:T(8,128)(2,1)S(1)}, bf16[4,17,16,128]{3,2,1,0:T(8,128)(2,1)S(1)}, u32[]{:S(2)}, u32[]{:S(2)}) collective-permute-start(bf16[4,17,16,128]{3,2,1,0:T(8,128)(2,1)S(1)} %get-tuple-element.41), channel_id=1, source_target_pairs={{0,2},{2,4},{4,6},{6,0},{1,3},{3,5},{5,7},{7,1},{8,10},{10,12},{12... | collective-permute-start | bytes 835592 | tf_op jit(solution)/shard_map/ppermute | solution.py:391
  62.7 15.1 %collective-permute-start.19 = (bf16[4,17,16,128]{3,2,1,0:T(8,128)(2,1)S(1)}, bf16[4,17,16,128]{3,2,1,0:T(8,128)(2,1)S(1)}, u32[]{:S(2)}, u32[]{:S(2)}) collective-permute-start(bf16[4,17,16,128]{3,2,1,0:T(8,128)(2,1)S(1)} %get-tuple-element.49), channel_id=1, source_target_pairs={{0,24},{8,0},{16,8},{24,16},{1,25},{9,1},{17,9},{25,17},{2,26},{10... | collective-permute-start | bytes 835592 | tf_op jit(solution)/shard_map/ppermute | solution.py:391
  64.1 13.8 %collective-permute-start.20 = (bf16[4,17,16,128]{3,2,1,0:T(8,128)(2,1)S(1)}, bf16[4,17,16,128]{3,2,1,0:T(8,128)(2,1)S(1)}, u32[]{:S(2)}, u32[]{:S(2)}) collective-permute-start(bf16[4,17,16,128]{3,2,1,0:T(8,128)(2,1)S(1)} %get-tuple-element.50), channel_id=1, source_target_pairs={{0,16},{8,24},{16,0},{24,8},{1,17},{9,25},{17,1},{25,9},{2,18},{10... | collective-permute-start | bytes 835592 | tf_op jit(solution)/shard_map/ppermute | solution.py:391
  65.7 14.5 %collective-permute-start.21 = (bf16[4,17,16,128]{3,2,1,0:T(8,128)(2,1)S(1)}, bf16[4,17,16,128]{3,2,1,0:T(8,128)(2,1)S(1)}, u32[]{:S(2)}, u32[]{:S(2)}) collective-permute-start(bf16[4,17,16,128]{3,2,1,0:T(8,128)(2,1)S(1)} %get-tuple-element.51), channel_id=1, source_target_pairs={{0,8},{8,16},{16,24},{24,0},{1,9},{9,17},{17,25},{25,1},{2,10},{10... | collective-permute-start | bytes 835592 | tf_op jit(solution)/shard_map/ppermute | solution.py:391
  67.9 17.5 %collective-permute-start.13 = (bf16[17,16,128]{2,1,0:T(8,128)(2,1)S(1)}, bf16[17,16,128]{2,1,0:T(8,128)(2,1)S(1)}, u32[]{:S(2)}, u32[]{:S(2)}) collective-permute-start(bf16[17,16,128]{2,1,0:T(8,128)(2,1)S(1)} %get-tuple-element.44), channel_id=1, source_target_pairs={{0,24},{8,0},{16,8},{24,16},{1,25},{9,1},{17,9},{25,17},{2,26},{10... | collective-permute-start | bytes 208904 | tf_op jit(solution)/shard_map/ppermute | solution.py:391
  69.9 18.9 %collective-permute-start.14 = (bf16[17,16,128]{2,1,0:T(8,128)(2,1)S(1)}, bf16[17,16,128]{2,1,0:T(8,128)(2,1)S(1)}, u32[]{:S(2)}, u32[]{:S(2)}) collective-permute-start(bf16[17,16,128]{2,1,0:T(8,128)(2,1)S(1)} %get-tuple-element.45), channel_id=1, source_target_pairs={{0,16},{8,24},{16,0},{24,8},{1,17},{9,25},{17,1},{25,9},{2,18},{10... | collective-permute-start | bytes 208904 | tf_op jit(solution)/shard_map/ppermute | solution.py:391
  77.8 10.9 %collective-permute-start.15 = (bf16[17,16,128]{2,1,0:T(8,128)(2,1)S(1)}, bf16[17,16,128]{2,1,0:T(8,128)(2,1)S(1)}, u32[]{:S(2)}, u32[]{:S(2)}) collective-permute-start(bf16[17,16,128]{2,1,0:T(8,128)(2,1)S(1)} %get-tuple-element.46), channel_id=1, source_target_pairs={{0,8},{8,16},{16,24},{24,0},{1,9},{9,17},{17,25},{25,1},{2,10},{10... | collective-permute-start | bytes 208904 | tf_op jit(solution)/shard_map/ppermute | solution.py:391
  81.0 7.8 %collective-permute-start.22 = (bf16[17,16,128]{2,1,0:T(8,128)(2,1)S(1)}, bf16[17,16,128]{2,1,0:T(8,128)(2,1)S(1)}, u32[]{:S(2)}, u32[]{:S(2)}) collective-permute-start(bf16[17,16,128]{2,1,0:T(8,128)(2,1)S(1)} %get-tuple-element.53), channel_id=1, source_target_pairs={{0,6},{2,0},{4,2},{6,4},{1,7},{3,1},{5,3},{7,5},{8,14},{10,8},{12,... | collective-permute-start | bytes 208904 | tf_op jit(solution)/shard_map/ppermute | solution.py:391
  83.8 5.8 %collective-permute-start.23 = (bf16[17,16,128]{2,1,0:T(8,128)(2,1)S(1)}, bf16[17,16,128]{2,1,0:T(8,128)(2,1)S(1)}, u32[]{:S(2)}, u32[]{:S(2)}) collective-permute-start(bf16[17,16,128]{2,1,0:T(8,128)(2,1)S(1)} %get-tuple-element.54), channel_id=1, source_target_pairs={{0,4},{2,6},{4,0},{6,2},{1,5},{3,7},{5,1},{7,3},{8,12},{10,14},{12... | collective-permute-start | bytes 208904 | tf_op jit(solution)/shard_map/ppermute | solution.py:391
  85.4 5.5 %collective-permute-start.24 = (bf16[17,16,128]{2,1,0:T(8,128)(2,1)S(1)}, bf16[17,16,128]{2,1,0:T(8,128)(2,1)S(1)}, u32[]{:S(2)}, u32[]{:S(2)}) collective-permute-start(bf16[17,16,128]{2,1,0:T(8,128)(2,1)S(1)} %get-tuple-element.55), channel_id=1, source_target_pairs={{0,2},{2,4},{4,6},{6,0},{1,3},{3,5},{5,7},{7,1},{8,10},{10,12},{12... | collective-permute-start | bytes 208904 | tf_op jit(solution)/shard_map/ppermute | solution.py:391
  85.5 5.4 %copy-start = (bf16[4,512,128]{2,1,0:T(8,128)(2,1)S(1)}, bf16[4,512,128]{2,1,0:T(8,128)(2,1)}, u32[]{:S(2)}) copy-start(bf16[4,512,128]{2,1,0:T(8,128)(2,1)} %refs_10_.1) | copy-start | bytes 1572868
  85.5 5.4 %copy-start.1 = (bf16[32,576]{1,0:T(8,128)(2,1)S(1)}, bf16[32,576]{1,0:T(8,128)(2,1)}, u32[]{:S(2)}) copy-start(bf16[32,576]{1,0:T(8,128)(2,1)} %refs_9_.1) | copy-start | bytes 110596
  90.9 9.9 %copy-start.6 = (bf16[1,7168]{1,0:T(2,128)(2,1)S(1)}, bf16[1,7168]{1,0:T(2,128)(2,1)}, u32[]{:S(2)}) copy-start(bf16[1,7168]{1,0:T(2,128)(2,1)} %param.19) | copy-start | bytes 43012
  90.9 10.0 %copy-start.5 = (f32[7168]{0:T(1024)S(1)}, f32[7168]{0:T(1024)}, u32[]{:S(2)}) copy-start(f32[7168]{0:T(1024)} %param.20) | copy-start | bytes 86020
  91.0 26.7 %copy-start.4 = (bf16[7168,16]{0,1:T(8,128)(2,1)S(1)}, bf16[7168,16]{0,1:T(8,128)(2,1)}, u32[]{:S(2)}) copy-start(bf16[7168,16]{0,1:T(8,128)(2,1)} %param.21) | copy-start | bytes 688132
  93.8 23.9 %copy-start.2 = (s32[1,8]{1,0:T(1,128)S(1)}, s32[1,8]{1,0:T(1,128)}, u32[]{:S(2)}) copy-start(s32[1,8]{1,0:T(1,128)} %routes_ref.1) | copy-start | bytes 100
  93.8 1.6 collective-permute-start.25
  96.1 13.2 %all-to-all-start = ((bf16[16,8,896]{2,1,0:T(8,128)(2,1)}), bf16[16,8,896]{2,1,0:T(8,128)(2,1)S(1)}, u32[]{:S(2)}, u32[]{:S(2)}) async-start(bf16[16,8,896]{2,1,0:T(8,128)(2,1)} %add_convert_fusion.1), calls=%async_computation | async-start | bytes 458752 | tf_op jit(solution)/shard_map/all_to_all | solution.py:444
  110.5 23.7 %all-to-all-start.1 = ((bf16[64,8,896]{2,1,0:T(8,128)(2,1)}), bf16[64,8,896]{2,1,0:T(8,128)(2,1)S(1)}, u32[]{:S(2)}, u32[]{:S(2)}) async-start(bf16[64,8,896]{2,1,0:T(8,128)(2,1)} %get-tuple-element.60), calls=%async_computation.1 | async-start | bytes 1835008 | tf_op jit(solution)/shard_map/all_to_all | solution.py:452
  134.1 3.2 %collective-permute-start.26 = (bf16[64,8,896]{2,1,0:T(8,128)(2,1)S(1)}, bf16[64,8,896]{2,1,0:T(8,128)(2,1)S(1)}, u32[]{:S(2)}, u32[]{:S(2)}) collective-permute-start(bf16[64,8,896]{2,1,0:T(8,128)(2,1)S(1)} %all-to-all-done.1.own_ref), channel_id=1, source_target_pairs={{0,1},{1,0},{2,3},{3,2},{4,5},{5,4},{6,7},{7,6},{8,9},{9,8},{10,11... | collective-permute-start | bytes 2752520 | tf_op jit(solution)/shard_map/ppermute | solution.py:391
  142.2 2.7 %collective-permute-start.27 = (bf16[64,8,896]{2,1,0:T(8,128)(2,1)S(1)}, bf16[64,8,896]{2,1,0:T(8,128)(2,1)S(1)}, u32[]{:S(2)}, u32[]{:S(2)}) collective-permute-start(bf16[64,8,896]{2,1,0:T(8,128)(2,1)S(1)} %get-tuple-element.69), channel_id=1, source_target_pairs={{0,1},{1,0},{2,3},{3,2},{4,5},{5,4},{6,7},{7,6},{8,9},{9,8},{10,11... | collective-permute-start | bytes 2752520 | tf_op jit(solution)/shard_map/ppermute | solution.py:391
  146.1 22.8 %all-to-all-start.2 = ((bf16[64,8,896]{2,1,0:T(8,128)(2,1)}), bf16[64,8,896]{2,1,0:T(8,128)(2,1)S(1)}, u32[]{:S(2)}, u32[]{:S(2)}) async-start(bf16[64,8,896]{2,1,0:T(8,128)(2,1)} %add_convert_fusion), calls=%async_computation.2 | async-start | bytes 1835008 | tf_op jit(solution)/shard_map/all_to_all | solution.py:457
